TPU v7x, 32 devices: a whole 2x2x4 slice. The times are simulated.
32 devices in a mesh: groups: 2 (over y), seq: 4 (over z), chan: 4 (over x, core).
Axes of the slice: x: 2, y: 2, z: 4, core: 2. Of those that a mesh axis runs over, the one named last changes fastest.
Arguments:
- x_rows: bfloat16 [40, 96, 1536], P(('groups', 'seq'), None, 'chan'), parts along dimension 0, may hold values from -6 to 6
- dest_slab: int32 [40], P(('groups', 'seq')), parts along dimension 0, may hold values from 0 to 4, as said below
- kept_len: int32 [40], P(('groups', 'seq')), parts along dimension 0, may hold values from 1 to 96
- convolution_weight: bfloat16 [1536, 5, 1536], P(None, None, 'chan'), may hold values from -0.0625 to 0.0625
- b_conv: float32 [1536], P('chan'), may hold values from -3 to 3
- entry_norm_gain: float32 [1536], P('chan'), may hold values from 0.1 to 1.9
- w_proj: bfloat16 [1024, 1536], P(None, 'chan'), may hold values from -0.15625 to 0.15625
- g_cot: bfloat16 [1024, 1536], P(('seq', 'chan'), 'groups'), parts along dimension 1, may hold values from -6 to 6
Outputs:
- qk_out: bfloat16 [1024, 1536], P(('seq', 'chan'), 'groups'), parts along dimension 1
- dw_conv: float32 [3072, 5, 1536], P(('groups', 'seq'), None, 'chan'), parts along dimension 0
- dw_proj: float32 [2048, 1536], P(('groups', 'seq'), 'chan'), parts along dimension 0
- dx_field: bfloat16 [1536, 3072], P('chan', ('groups', 'seq')), parts along dimension 1
There are 2 independent parts, one for each index of `groups`. A program takes and returns all parts, laid end to end along the dimension named above; an argument that names none is the same for every part. Nothing has to cross between parts.
Inputs may be any that keep to these rules, and one draw needn't show every extreme that they name: `dest_slab`: each slab 0 to 3 is named by exactly 4 blocks; the blocks of one device name each slab at most 2 times, and in every draw some device names some slab exactly 2 times; every device holds exactly 1 block marked 4.
All inputs are finite; a program needn't handle non-finite values.
Results may differ from a plain program's by a relative error of at most 0.005.
Values may be sent and summed in bfloat16 or wider, within the bound.
No kernel may reach another device: no remote copies, remote signals or barrier semaphores. Data moves between devices by JAX's collectives and lax.ppermute only.
A program may use at most 128 MiB of HBM per device.

v0:
```python
import jax
import jax.numpy as jnp
from jax import lax
from jax.sharding import PartitionSpec as P

KERNEL_TAPS = 5
DILATION_STEP = 2
CAP = 2


def padded(cells, sides, width):
    for axis, dim in sides:
        count = lax.axis_size(axis)
        ends = count - 1
        head = lax.slice_in_dim(cells, 0, width, axis=dim)
        tail = lax.slice_in_dim(cells, cells.shape[dim] - width, cells.shape[dim], axis=dim)
        cells = jnp.concatenate(
            [
                lax.ppermute(tail, axis, [(i, (i + 1) % count) for i in range(ends)]),
                cells,
                lax.ppermute(head, axis, [((i + 1) % count, i) for i in range(ends)]),
            ],
            axis=dim,
        )
    return cells


def smooth_gate(values):
    return jax.nn.gelu(values, approximate=True)


def per_device(
    x_rows, dest_slab, kept_len, convolution_weight, b_conv, entry_norm_gain, w_proj, g_cot
):
    seq_count = lax.axis_size("seq")
    chan_count = lax.axis_size("chan")
    src_rows, block_len, shard_ch = x_rows.shape
    every_channel = shard_ch * chan_count
    window_width = 2 * DILATION_STEP
    positions = lax.broadcasted_iota(jnp.int32, (src_rows, block_len), 1)
    keep_mask = (positions < kept_len[:, None]).astype(x_rows.dtype)
    masked = (x_rows * keep_mask[:, :, None]).reshape(src_rows, block_len * shard_ch)
    slab_ids = jnp.arange(seq_count + 1, dtype=jnp.int32)
    onehot = (dest_slab[:, None] == slab_ids[None, :]).astype(jnp.int32)
    before = jnp.cumsum(onehot, axis=0) - onehot
    slot_row = jnp.sum(before * onehot, axis=1)
    target = dest_slab * CAP + slot_row
    send_ids = jnp.arange(seq_count * CAP, dtype=jnp.int32)
    picker = (send_ids[:, None] == target[None, :]).astype(jnp.bfloat16)
    outgoing = jnp.dot(picker, masked, preferred_element_type=jnp.float32).astype(jnp.bfloat16)
    outgoing = outgoing.reshape(seq_count, CAP, block_len * shard_ch)
    sent_counts = jnp.sum(onehot[:, :seq_count], axis=0).astype(jnp.bfloat16).reshape(seq_count, 1)
    arrived, arrived_counts = (
        lax.all_to_all(outgoing, "seq", split_axis=0, concat_axis=0, tiled=True),
        lax.all_to_all(sent_counts, "seq", split_axis=0, concat_axis=0, tiled=True),
    )
    got_counts = arrived_counts[:, 0].astype(jnp.int32)
    offsets = jnp.cumsum(got_counts) - got_counts
    slot_ladder = jnp.arange(CAP, dtype=jnp.int32)
    placed = offsets[:, None] + slot_ladder[None, :]
    placed = jnp.where(slot_ladder[None, :] < got_counts[:, None], placed, -1).reshape(-1)
    block_ids = jnp.arange(seq_count, dtype=jnp.int32)
    arranger = (block_ids[:, None] == placed[None, :]).astype(jnp.bfloat16)
    routed = jnp.dot(
        arranger,
        arrived.reshape(seq_count * CAP, block_len * shard_ch),
        preferred_element_type=jnp.float32,
    )
    routed = routed.astype(jnp.bfloat16).reshape(seq_count * block_len, shard_ch)
    window_length = routed.shape[0]
    pooled_len = window_length // 2
    padded_input = padded(routed, (("seq", 0),), window_width)
    complete_rows = lax.all_gather(padded_input, "chan", axis=1, tiled=True)
    convolved = jnp.zeros((window_length, shard_ch), jnp.float32)
    for kernel_tap_index in range(KERNEL_TAPS):
        convolved = convolved + jnp.dot(
            complete_rows[
                kernel_tap_index * DILATION_STEP : kernel_tap_index * DILATION_STEP + window_length
            ],
            convolution_weight[:, kernel_tap_index, :],
            preferred_element_type=jnp.float32,
        )
    shifted = convolved + b_conv[None, :]
    act, gate_pull = jax.vjp(smooth_gate, shifted)
    paired = act.reshape(pooled_len, 2, shard_ch)
    pooled_output = (paired[:, 0, :] + paired[:, 1, :]) * 0.5
    sum_val, sum_sq = lax.psum(
        (jnp.sum(pooled_output, axis=1), jnp.sum(pooled_output * pooled_output, axis=1)), "chan"
    )
    mean_value = sum_val / every_channel
    inverse_deviation = lax.rsqrt(sum_sq / every_channel - mean_value * mean_value + 1e-05)
    centered_input = (pooled_output - mean_value[:, None]) * inverse_deviation[:, None]
    normalized = (centered_input * entry_norm_gain[None, :]).astype(jnp.bfloat16)
    feat_total = w_proj.shape[0]
    group_feat = feat_total // (seq_count * chan_count)
    proj_view = w_proj.reshape(seq_count, chan_count, group_feat, shard_ch)
    qk_local = lax.psum_scatter(
        jnp.einsum("scfd,pd->csfp", proj_view, normalized, preferred_element_type=jnp.float32),
        "chan",
        scatter_dimension=0,
        tiled=True,
    ).astype(jnp.bfloat16)
    qk_heads = lax.all_to_all(qk_local, "seq", split_axis=1, concat_axis=3, tiled=True)
    qk_out = qk_heads.reshape(group_feat, pooled_len * seq_count)
    cot_local = g_cot.reshape(1, 1, group_feat, g_cot.shape[1])
    cot_wide = lax.all_gather(cot_local, "chan", axis=1, tiled=True)
    cot_full = lax.all_to_all(cot_wide, "seq", split_axis=3, concat_axis=0, tiled=True)
    cot_slab = cot_full.reshape(feat_total, pooled_len)
    dnormed = jnp.einsum("fp,fd->pd", cot_slab, w_proj, preferred_element_type=jnp.float32)
    dw_proj = lax.psum_scatter(
        jnp.dot(cot_slab, normalized, preferred_element_type=jnp.float32),
        "seq",
        scatter_dimension=0,
        tiled=True,
    )
    normalized_gradient = dnormed * entry_norm_gain[None, :]
    leading_sum, trailing_sum = lax.psum(
        (
            jnp.sum(normalized_gradient, axis=1),
            jnp.sum(normalized_gradient * centered_input, axis=1),
        ),
        "chan",
    )
    pooled_gradient = inverse_deviation[:, None] * (
        normalized_gradient
        - (leading_sum / every_channel)[:, None]
        - centered_input * (trailing_sum / every_channel)[:, None]
    )
    dact = jnp.repeat(pooled_gradient * 0.5, 2, axis=0)
    output_gradient = gate_pull(dact)[0].astype(jnp.bfloat16)
    dy_pad = padded(output_gradient, (("seq", 0),), window_width)
    total = jnp.zeros((shard_ch * lax.axis_size("chan"), window_length), jnp.float32)
    for kernel_tap_index in range(KERNEL_TAPS):
        shift_amount = (KERNEL_TAPS - 1 - kernel_tap_index) * DILATION_STEP
        total = total + jnp.einsum(
            "io,po->ip",
            convolution_weight[:, kernel_tap_index, :],
            dy_pad[shift_amount : shift_amount + window_length],
            preferred_element_type=jnp.float32,
        )
    dx_field = lax.psum_scatter(total, "chan", scatter_dimension=0, tiled=True).astype(jnp.bfloat16)
    taps_out = []
    for kernel_tap_index in range(KERNEL_TAPS):
        taps_out.append(
            jnp.einsum(
                "pi,po->io",
                complete_rows[
                    kernel_tap_index * DILATION_STEP : kernel_tap_index * DILATION_STEP
                    + window_length
                ],
                output_gradient,
                preferred_element_type=jnp.float32,
            )
        )
    dw_conv = lax.psum_scatter(jnp.stack(taps_out, axis=1), "seq", scatter_dimension=0, tiled=True)
    return (qk_out, dw_conv, dw_proj, dx_field)


def solution(mesh):
    return jax.shard_map(
        per_device,
        mesh=mesh,
        in_specs=(
            P(("groups", "seq"), None, "chan"),
            P(("groups", "seq")),
            P(("groups", "seq")),
            P(None, None, "chan"),
            P("chan"),
            P("chan"),
            P(None, "chan"),
            P(("seq", "chan"), "groups"),
        ),
        out_specs=(
            P(("seq", "chan"), "groups"),
            P(("groups", "seq"), None, "chan"),
            P(("groups", "seq"), "chan"),
            P("chan", ("groups", "seq")),
        ),
        check_vma=False,
    )
```

profile of v0, /device:TPU:0, one launch (start us, length us, event | category | flops | bytes accessed | tf_op | source)
XLA Modules:
  0.0 386.1 jit_solution(9697722695261216436)
XLA Ops:
  7.2 0.8 fusion.61
  8.0 0.7 copy.46
  8.7 6.3 %all-to-all-start = ((bf16[4,1,1]{2,1,0:T(2,128)(2,1)}), bf16[4,1,1]{2,1,0:T(2,128)(2,1)S(1)}, u32[]{:S(2)}, u32[]{:S(2)}) async-start(bf16[4,1,1]{2,1,0:T(2,128)(2,1)} %copy.46), calls=%async_computation | async-start | bytes 4096 | tf_op jit(solution)/shard_map/all_to_all | solution.py:55
  15.0 0.7 fusion.62
  15.8 0.8 select_reduce_fusion
  16.6 0.7 multiply_add_fusion
  17.3 1.1 multiply_bitcast_fusion
  18.5 0.3 convolution_convert_fusion
  18.9 1.2 reshape.180
  20.0 0.4 all-to-all-done
  20.5 4.7 %all-to-all-start.1 = ((bf16[4,2,36864]{2,1,0:T(2,128)(2,1)}), bf16[4,2,36864]{2,1,0:T(2,128)(2,1)S(1)}, u32[]{:S(2)}, u32[]{:S(2)}) async-start(bf16[4,2,36864]{2,1,0:T(2,128)(2,1)} %reshape.180), calls=%async_computation.1 | async-start | bytes 1179648 | tf_op jit(solution)/shard_map/all_to_all | solution.py:54
  25.7 14.8 %all-to-all-done.1 = bf16[4,2,36864]{2,1,0:T(2,128)(2,1)S(1)} async-done(((bf16[4,2,36864]{2,1,0:T(2,128)(2,1)}), bf16[4,2,36864]{2,1,0:T(2,128)(2,1)S(1)}, u32[]{:S(2)}, u32[]{:S(2)}) %all-to-all-start.1) | async-done | bytes 589856 | tf_op jit(solution)/shard_map/all_to_all | solution.py:54
  40.5 0.2 reshape.181
  40.7 0.3 convolution_convert_fusion.1
  41.0 0.2 reshape.182
  41.2 1.3 collective-permute-start
  42.5 1.3 collective-permute-start.1
  43.8 4.2 %collective-permute-done.1 = bf16[4,384]{1,0:T(4,128)(2,1)S(1)} collective-permute-done((bf16[4,384]{1,0:T(4,128)(2,1)S(1)}, bf16[4,384]{1,0:T(4,128)(2,1)S(1)}, u32[]{:S(2)}, u32[]{:S(2)}) %collective-permute-start.1) | collective-permute-done | bytes 3104 | tf_op jit(solution)/shard_map/ppermute | solution.py:21
  48.0 0.8 pad_maximum_fusion
  48.9 6.5 %all-gather = bf16[256,768]{1,0:T(8,128)(2,1)S(1)} all-gather(bf16[64,768]{1,0:T(8,128)(2,1)S(1)} %copy-done.2), channel_id=2, replica_groups=mesh['groups'=2,'seq'=4,'chan'=4] {'chan'}, dimensions={0}, use_global_device_ids=true | all-gather | bytes 491520 | tf_op jit(solution)/shard_map/all_gather | solution.py:106
  55.4 0.6 copy.50
  55.9 0.6 reshape.198
  56.5 15.9 %all_to_all.41 = bf16[4,2,24576]{2,1,0:T(2,128)(2,1)S(1)} all-to-all(bf16[4,2,24576]{2,1,0:T(2,128)(2,1)S(1)} %reshape.198), channel_id=1, replica_groups=mesh['groups'=2,'seq'=4,'chan'=4] {'seq'}, dimensions={0} | all-to-all | bytes 786432 | tf_op jit(solution)/shard_map/all_to_all | solution.py:107
  72.4 0.5 reshape.199
  72.9 1.1 copy.56
  74.1 2.5 fusion.19
  76.6 2.0 convolution_add_fusion.5
  78.7 2.1 convolution_add_fusion.4
  80.8 2.1 convolution_add_fusion.3
  82.9 3.2 multiply_multiply_fusion.2
  86.1 1.4 reshape.183
  87.5 0.5 fusion.72
  88.2 5.7 %all-reduce.2 = (f32[192]{0:T(256)S(1)}, f32[192]{0:T(256)S(1)}) all-reduce(f32[192]{0:T(256)S(1)} %fusion.57, f32[192]{0:T(256)S(1)} %get-tuple-element.35), channel_id=1, replica_groups=mesh['groups'=2,'seq'=4,'chan'=4] {'chan'}, use_global_device_ids=true, to_apply=%region_7.8 | all-reduce | flops 384 | bytes 3072 | tf_op jit(solution)/shard_map/psum | solution.py:87
  93.9 1.7 convolution_bitcast_fusion.5
  95.6 1.1 fusion.69
  96.8 0.5 convolution_bitcast_fusion.6
  97.3 27.8 %all-reduce.4 = (bf16[4,4,64,192]{3,2,0,1:T(8,128)(2,1)}, f32[192]{0:T(256)S(1)}, f32[192]{0:T(256)S(1)}) all-reduce(f32[4,4,64,192]{3,2,0,1:T(8,128)S(1)} %convolution_bitcast_fusion.6, f32[192]{0:T(256)S(1)} %get-tuple-element.29, f32[192]{0:T(256)S(1)} %get-tuple-element.28), channel_id=3, replica_groups=mesh['groups'=2,'seq'=4,'chan'=4] {'chan'}, use_global_device_ids=true, to_apply=%region_8.9.clone | all-reduce | flops 196992 | bytes 1182720
  125.1 1.1 multiply_multiply_fusion.3
  126.3 0.2 broadcast_in_dim.6
  126.5 0.4 reshape.188
  126.9 1.5 fusion.49
  128.4 2.1 collective-permute-start.3
  130.5 2.1 fusion.14
  132.6 1.3 collective-permute-start.2
  133.9 2.1 fusion.9
  136.0 2.1 collective-permute-done.2
  138.1 2.1 fusion.17
  140.2 2.1 fusion.1
  142.3 3.6 fusion.2
  146.0 2.3 fusion.7
  148.4 2.3 fusion.6
  150.7 2.4 fusion.5
  153.1 2.4 fusion.4
  155.5 2.3 fusion.3
  157.8 0.6 copy-done.5
  158.4 0.6 dynamic-slice
  159.0 1.6 dynamic-slice_convert_fusion
  160.6 8.8 %all_to_all.42 = bf16[1,4,64,192]{3,2,0,1:T(8,128)(2,1)S(1)} all-to-all(bf16[1,4,64,192]{3,2,0,1:T(8,128)(2,1)S(1)} %dynamic-slice_convert_fusion), channel_id=1, replica_groups=mesh['groups'=2,'seq'=4,'chan'=4] {'seq'}, dimensions={1} | all-to-all | bytes 196608 | tf_op jit(solution)/shard_map/all_to_all | solution.py:103
  169.5 0.8 reshape.185
  170.2 1.9 copy.53
  172.1 5.3 %reduce-scatter.9.cloned.1.call-done = f32[384,384]{0,1:T(8,128)} async-done(((f32[1536,384]{0,1:T(8,128)}), f32[384,384]{0,1:T(8,128)}) %reduce-scatter.9.cloned.1.call-update) | async-done | bytes 589840 | tf_op jit(solution)/shard_map/reduce_scatter | solution.py:141
  177.5 1.1 convert_element_type.85
  178.6 0.9 copy.54
  179.5 200.1 %reduce-scatter.5.cloned.1.call-done = f32[384,5,384]{2,0,1:T(8,128)} async-done(((f32[1536,5,384]{2,0,1:T(8,128)}), f32[384,5,384]{2,0,1:T(8,128)}) %reduce-scatter.5.cloned.1.call-update) | async-done | bytes 2949136 | tf_op jit(solution)/shard_map/reduce_scatter | solution.py:155
  (40 shorter events, 1.4 us)
Async XLA Ops:
  7.2 88.4 %copy-start = (bf16[1024,384]{1,0:T(8,128)(2,1)S(1)}, bf16[1024,384]{1,0:T(8,128)(2,1)}, u32[]{:S(2)}) copy-start(bf16[1024,384]{1,0:T(8,128)(2,1)} %param.14) | copy-start | bytes 2359300
  8.7 11.8 %all-to-all-start = ((bf16[4,1,1]{2,1,0:T(2,128)(2,1)}), bf16[4,1,1]{2,1,0:T(2,128)(2,1)S(1)}, u32[]{:S(2)}, u32[]{:S(2)}) async-start(bf16[4,1,1]{2,1,0:T(2,128)(2,1)} %copy.46), calls=%async_computation | async-start | bytes 4096 | tf_op jit(solution)/shard_map/all_to_all | solution.py:55
  20.5 20.0 %all-to-all-start.1 = ((bf16[4,2,36864]{2,1,0:T(2,128)(2,1)}), bf16[4,2,36864]{2,1,0:T(2,128)(2,1)S(1)}, u32[]{:S(2)}, u32[]{:S(2)}) async-start(bf16[4,2,36864]{2,1,0:T(2,128)(2,1)} %reshape.180), calls=%async_computation.1 | async-start | bytes 1179648 | tf_op jit(solution)/shard_map/all_to_all | solution.py:54
  25.1 48.9 %all-gather.3.cloned.1.call-start = ((), (), s32[]{:S(2)}) async-start(), calls=%async_computation.7 | async-start | bytes 1505280 | tf_op jit(solution)/shard_map/all_gather | solution.py:73
  25.7 23.2 %copy-start.2 = (bf16[64,768]{1,0:T(8,128)(2,1)S(1)}, bf16[64,768]{1,0:T(8,128)(2,1)}, u32[]{:S(2)}) copy-start(bf16[64,768]{1,0:T(8,128)(2,1)} %param.15) | copy-start | bytes 294916
  41.2 2.6 collective-permute-start
  42.5 5.5 %collective-permute-start.1 = (bf16[4,384]{1,0:T(4,128)(2,1)S(1)}, bf16[4,384]{1,0:T(4,128)(2,1)S(1)}, u32[]{:S(2)}, u32[]{:S(2)}) collective-permute-start(bf16[4,384]{1,0:T(4,128)(2,1)S(1)} %get-tuple-element.42), channel_id=1, source_target_pairs={{4,0},{8,4},{12,8},{5,1},{9,5},{13,9},{6,2},{10,6},{14,10},{7,3},{... | collective-permute-start | bytes 9224 | tf_op jit(solution)/shard_map/ppermute | solution.py:21
  48.8 121.4 %reduce-scatter.7.cloned.1.call-start = ((), (), s32[]{:S(2)}) async-start(), calls=%async_computation.9 | async-start | bytes 1966080 | tf_op jit(solution)/shard_map/reduce_scatter | solution.py:110
  74.1 2.5 copy-start.1
  80.8 2.1 copy-start.4
  86.1 7.8 %copy-start.3 = (f32[384]{0:T(512)S(1)}, f32[384]{0:T(512)}, u32[]{:S(2)}) copy-start(f32[384]{0:T(512)} %param.13) | copy-start | bytes 4612
  96.7 80.7 %reduce-scatter.9.cloned.1.call-start = ((), (), s32[]{:S(2)}) async-start(), calls=%async_computation.10 | async-start | bytes 2949120 | tf_op jit(solution)/shard_map/reduce_scatter | solution.py:141
  128.4 5.5 %collective-permute-start.3 = (bf16[4,384]{1,0:T(4,128)(2,1)S(1)}, bf16[4,384]{1,0:T(4,128)(2,1)S(1)}, u32[]{:S(2)}, u32[]{:S(2)}) collective-permute-start(bf16[4,384]{1,0:T(4,128)(2,1)S(1)} %get-tuple-element.40), channel_id=1, source_target_pairs={{0,4},{4,8},{8,12},{1,5},{5,9},{9,13},{2,6},{6,10},{10,14},{3,7},{... | collective-permute-start | bytes 9224 | tf_op jit(solution)/shard_map/ppermute | solution.py:19
  132.6 5.5 %collective-permute-start.2 = (bf16[4,384]{1,0:T(4,128)(2,1)S(1)}, bf16[4,384]{1,0:T(4,128)(2,1)S(1)}, u32[]{:S(2)}, u32[]{:S(2)}) collective-permute-start(bf16[4,384]{1,0:T(4,128)(2,1)S(1)} %get-tuple-element.39), channel_id=1, source_target_pairs={{4,0},{8,4},{12,8},{5,1},{9,5},{13,9},{6,2},{10,6},{14,10},{7,3},{... | collective-permute-start | bytes 9224 | tf_op jit(solution)/shard_map/ppermute | solution.py:21
  146.0 233.6 %reduce-scatter.5.cloned.1.call-start = ((), (), s32[]{:S(2)}) async-start(), calls=%async_computation.8 | async-start | bytes 14745600 | tf_op jit(solution)/shard_map/reduce_scatter | solution.py:155
  157.8 0.7 copy-start.5
Sparse Core Ops, SparseCore 0:
  49.0 17.8 all-gather.2
  96.8 34.0 reduce-scatter.6
  146.1 31.3 reduce-scatter.8
  180.4 199.1 reduce-scatter.4
where the time goes:
time: 387 us; the launch traced here: 386 us
  waiting for transfers between devices  227 us (59%)
  blocking collectives  64.6 us (17%)
  matrix products  39.5 us (10%)
  starting transfers between devices  17.1 us (4%)
  local copies, waits for them, and re-layouts  14.3 us (4%)
  between operations  14.1 us (4%)
  other arithmetic  9.36 us (2%)
    reduce_scatter x1, waiting for transfers between devices, per_device(): lax.psum_scatter(jnp.stack(taps_out, axis=1), 'seq', scatter_dimension=0,...  200 us
    unnamed x1, blocking collectives  27.8 us
    all_to_all x1, blocking collectives, per_device(): lax.all_to_all(cot_wide, 'seq', split_axis=3, concat_axis=0, tiled=True)  15.9 us
    all_to_all x1, waiting for transfers between devices, per_device(): lax.all_to_all(outgoing, 'seq', split_axis=0, concat_axis=0, tiled=True)  14.8 us
    dot_general x5, matrix products, per_device(): jnp.einsum('io,po->ip', convolution_weight[:, kernel_tap_index, :], dy_pa...  12 us
    dot_general x5, matrix products, per_device(): jnp.dot(complete_rows[kernel_tap_index * DILATION_STEP:kernel_tap_index *...  11.9 us
    dot_general x5, matrix products, per_device(): jnp.einsum('pi,po->io', complete_rows[kernel_tap_index * DILATION_STEP:ke...  11.8 us
    all_to_all x1, blocking collectives, per_device(): lax.all_to_all(qk_local, 'seq', split_axis=1, concat_axis=3, tiled=True)  8.76 us
  transfers between devices with their start and end apart: 10, of which 6 were waited for; matrix products, arithmetic and copies ran while one was open for 11% of the time, Pallas kernels for 0%

commit v1 on v0

--- a/solution.py
+++ b/solution.py
@@ -42,8 +42,9 @@
     masked = (x_rows * keep_mask[:, :, None]).reshape(src_rows, block_len * shard_ch)
     slab_ids = jnp.arange(seq_count + 1, dtype=jnp.int32)
     onehot = (dest_slab[:, None] == slab_ids[None, :]).astype(jnp.int32)
-    before = jnp.cumsum(onehot, axis=0) - onehot
-    slot_row = jnp.sum(before * onehot, axis=1)
+    row_ids = jnp.arange(src_rows, dtype=jnp.int32)
+    same = (dest_slab[:, None] == dest_slab[None, :]) & (row_ids[None, :] < row_ids[:, None])
+    slot_row = jnp.sum(same.astype(jnp.int32), axis=1)
     target = dest_slab * CAP + slot_row
     send_ids = jnp.arange(seq_count * CAP, dtype=jnp.int32)
     picker = (send_ids[:, None] == target[None, :]).astype(jnp.bfloat16)
@@ -55,7 +56,8 @@
         lax.all_to_all(sent_counts, "seq", split_axis=0, concat_axis=0, tiled=True),
     )
     got_counts = arrived_counts[:, 0].astype(jnp.int32)
-    offsets = jnp.cumsum(got_counts) - got_counts
+    src_ids = jnp.arange(seq_count, dtype=jnp.int32)
+    offsets = jnp.sum(jnp.where(src_ids[None, :] < src_ids[:, None], got_counts[None, :], 0), axis=1)
     slot_ladder = jnp.arange(CAP, dtype=jnp.int32)
     placed = offsets[:, None] + slot_ladder[None, :]
     placed = jnp.where(slot_ladder[None, :] < got_counts[:, None], placed, -1).reshape(-1)
@@ -84,50 +86,48 @@
     act, gate_pull = jax.vjp(smooth_gate, shifted)
     paired = act.reshape(pooled_len, 2, shard_ch)
     pooled_output = (paired[:, 0, :] + paired[:, 1, :]) * 0.5
-    sum_val, sum_sq = lax.psum(
-        (jnp.sum(pooled_output, axis=1), jnp.sum(pooled_output * pooled_output, axis=1)), "chan"
-    )
-    mean_value = sum_val / every_channel
-    inverse_deviation = lax.rsqrt(sum_sq / every_channel - mean_value * mean_value + 1e-05)
+    feat_total = w_proj.shape[0]
+    group_feat = feat_total // (seq_count * chan_count)
+    block_feat = group_feat * chan_count
+    cot_parts = lax.all_to_all(
+        g_cot.reshape(group_feat, seq_count, pooled_len), "seq", split_axis=1, concat_axis=0, tiled=True
+    ).reshape(seq_count, group_feat, pooled_len)
+    cot_slab = lax.all_gather(cot_parts, "chan", axis=1, tiled=True).reshape(feat_total, pooled_len)
+    cot_wide = lax.all_gather(g_cot, "chan", axis=0, tiled=True)
+    dnormed = jnp.einsum("fp,fd->pd", cot_slab, w_proj, preferred_element_type=jnp.float32)
+    dxhat = dnormed * entry_norm_gain[None, :]
+    sums = lax.psum(
+        jnp.stack(
+            [
+                jnp.sum(pooled_output, axis=1),
+                jnp.sum(pooled_output * pooled_output, axis=1),
+                jnp.sum(dxhat, axis=1),
+                jnp.sum(dxhat * pooled_output, axis=1),
+            ]
+        ),
+        "chan",
+    ) / every_channel
+    mean_value = sums[0]
+    inverse_deviation = lax.rsqrt(sums[1] - mean_value * mean_value + 1e-05)
+    leading = sums[2]
+    trailing = inverse_deviation * (sums[3] - mean_value * leading)
     centered_input = (pooled_output - mean_value[:, None]) * inverse_deviation[:, None]
     normalized = (centered_input * entry_norm_gain[None, :]).astype(jnp.bfloat16)
-    feat_total = w_proj.shape[0]
-    group_feat = feat_total // (seq_count * chan_count)
-    proj_view = w_proj.reshape(seq_count, chan_count, group_feat, shard_ch)
-    qk_local = lax.psum_scatter(
-        jnp.einsum("scfd,pd->csfp", proj_view, normalized, preferred_element_type=jnp.float32),
-        "chan",
-        scatter_dimension=0,
-        tiled=True,
-    ).astype(jnp.bfloat16)
-    qk_heads = lax.all_to_all(qk_local, "seq", split_axis=1, concat_axis=3, tiled=True)
-    qk_out = qk_heads.reshape(group_feat, pooled_len * seq_count)
-    cot_local = g_cot.reshape(1, 1, group_feat, g_cot.shape[1])
-    cot_wide = lax.all_gather(cot_local, "chan", axis=1, tiled=True)
-    cot_full = lax.all_to_all(cot_wide, "seq", split_axis=3, concat_axis=0, tiled=True)
-    cot_slab = cot_full.reshape(feat_total, pooled_len)
-    dnormed = jnp.einsum("fp,fd->pd", cot_slab, w_proj, preferred_element_type=jnp.float32)
-    dw_proj = lax.psum_scatter(
-        jnp.dot(cot_slab, normalized, preferred_element_type=jnp.float32),
-        "seq",
-        scatter_dimension=0,
-        tiled=True,
-    )
-    normalized_gradient = dnormed * entry_norm_gain[None, :]
-    leading_sum, trailing_sum = lax.psum(
-        (
-            jnp.sum(normalized_gradient, axis=1),
-            jnp.sum(normalized_gradient * centered_input, axis=1),
-        ),
-        "chan",
-    )
     pooled_gradient = inverse_deviation[:, None] * (
-        normalized_gradient
-        - (leading_sum / every_channel)[:, None]
-        - centered_input * (trailing_sum / every_channel)[:, None]
+        dxhat - leading[:, None] - centered_input * trailing[:, None]
     )
     dact = jnp.repeat(pooled_gradient * 0.5, 2, axis=0)
     output_gradient = gate_pull(dact)[0].astype(jnp.bfloat16)
+    norm_all = lax.all_gather(normalized, "seq", axis=0, tiled=True)
+    dy_all = lax.all_gather(output_gradient, "seq", axis=0, tiled=True)
+    own_ch = every_channel // seq_count
+    x_own = lax.all_to_all(
+        complete_rows.reshape(-1, seq_count, own_ch), "seq", split_axis=1, concat_axis=0, tiled=True
+    ).reshape(seq_count, -1, own_ch)
+    dw_proj = jnp.dot(cot_wide, norm_all, preferred_element_type=jnp.float32)
+    w_block = lax.dynamic_slice_in_dim(w_proj, lax.axis_index("seq") * block_feat, block_feat, axis=0)
+    qk_part = jnp.einsum("fd,pd->fp", w_block, norm_all, preferred_element_type=jnp.float32)
+    qk_out = lax.psum_scatter(qk_part, "chan", scatter_dimension=0, tiled=True).astype(jnp.bfloat16)
     dy_pad = padded(output_gradient, (("seq", 0),), window_width)
     total = jnp.zeros((shard_ch * lax.axis_size("chan"), window_length), jnp.float32)
     for kernel_tap_index in range(KERNEL_TAPS):
@@ -138,21 +138,22 @@
             dy_pad[shift_amount : shift_amount + window_length],
             preferred_element_type=jnp.float32,
         )
-    dx_field = lax.psum_scatter(total, "chan", scatter_dimension=0, tiled=True).astype(jnp.bfloat16)
+    pieces = lax.all_to_all(
+        total.astype(jnp.bfloat16).reshape(chan_count, shard_ch, window_length), "chan", split_axis=0, concat_axis=0, tiled=True
+    )
+    dx_field = jnp.sum(pieces.astype(jnp.float32), axis=0).astype(jnp.bfloat16)
     taps_out = []
     for kernel_tap_index in range(KERNEL_TAPS):
+        begin = kernel_tap_index * DILATION_STEP
         taps_out.append(
             jnp.einsum(
                 "pi,po->io",
-                complete_rows[
-                    kernel_tap_index * DILATION_STEP : kernel_tap_index * DILATION_STEP
-                    + window_length
-                ],
-                output_gradient,
+                x_own[:, begin : begin + window_length].reshape(-1, own_ch),
+                dy_all,
                 preferred_element_type=jnp.float32,
             )
         )
-    dw_conv = lax.psum_scatter(jnp.stack(taps_out, axis=1), "seq", scatter_dimension=0, tiled=True)
+    dw_conv = jnp.stack(taps_out, axis=1)
     return (qk_out, dw_conv, dw_proj, dx_field)
 
 

time: 387 us -> 222 us (0.57)
  waiting for transfers between devices: 227 us -> 79.9 us
  blocking collectives: 64.6 us -> 38.3 us
  starting transfers between devices: 17.1 us -> 29.8 us
  matrix products: 39.5 us -> 31.5 us
    reduce_scatter x3 -> x1, waiting for transfers between devices: 205 us -> 0.01 us  [per_device(): lax.psum_scatter(qk_part, 'chan', scatter_dimension=0, tiled=True)]
    all_to_all x0 -> x3, waiting for transfers between devices: none -> 59.1 us  [the longest x1 35.6 us: per_device(): lax.all_to_all(complete_rows.reshape(-1, seq_count, own_ch), 'seq', split...]
    unnamed x1 -> x0, blocking collectives: 27.8 us -> none
    all_gather x1 -> x3, blocking collectives: 6.46 us -> 32.3 us  [the longest x1 16.7 us: per_device(): norm_all = lax.all_gather(normalized, 'seq', axis=0, tiled=True)]
    all_to_all x2 -> x0, blocking collectives: 24.7 us -> none  [the longest x1 15.9 us: per_device(): lax.all_to_all(cot_wide, 'seq', split_axis=3, concat_axis=0, tiled=True)]
    all_to_all x0 -> x3, starting transfers between devices: none -> 11 us  [the longest x1 3.91 us: per_device(): lax.all_to_all(g_cot.reshape(group_feat, seq_count, pooled_len), 'seq', s...]
    dot_general x7, matrix products: 14 us -> 7.37 us  [the longest x5 5.72 us: per_device(): jnp.einsum('pi,po->io', x_own[:, begin:begin + window_length].reshape(-1,...]
  transfers between devices with their start and end apart: 10 -> 12, of which waited for: 6 -> 6; matrix products, arithmetic and copies ran while one was open for 11% -> 13% of each run, Pallas kernels for 0% -> 0%
where the time goes in v1:
time: 222 us; the launch traced here: 220 us
  waiting for transfers between devices  79.9 us (36%)
  blocking collectives  38.3 us (17%)
  matrix products  31.5 us (14%)
  starting transfers between devices  29.8 us (13%)
  local copies, waits for them, and re-layouts  17.9 us (8%)
  between operations  14.2 us (6%)
  other arithmetic  8.65 us (4%)
    all_to_all x1, waiting for transfers between devices, per_device(): lax.all_to_all(complete_rows.reshape(-1, seq_count, own_ch), 'seq', split...  35.6 us
    all_to_all x1, waiting for transfers between devices, per_device(): lax.all_to_all(total.astype(jnp.bfloat16).reshape(chan_count, shard_ch, w...  17.6 us
    all_gather x1, blocking collectives, per_device(): norm_all = lax.all_gather(normalized, 'seq', axis=0, tiled=True)  16.7 us
    all_to_all x1, waiting for transfers between devices, per_device(): lax.all_to_all(outgoing, 'seq', split_axis=0, concat_axis=0, tiled=True)  14.9 us
    dot_general x5, matrix products, per_device(): jnp.einsum('io,po->ip', convolution_weight[:, kernel_tap_index, :], dy_pa...  12.2 us
    dot_general x5, matrix products, per_device(): jnp.dot(complete_rows[kernel_tap_index * DILATION_STEP:kernel_tap_index *...  10.9 us
    all_gather x1, blocking collectives, per_device(): lax.all_gather(cot_parts, 'chan', axis=1, tiled=True)  9.44 us
    all_to_all x1, starting transfers between devices, per_device(): lax.all_to_all(sent_counts, 'seq', split_axis=0, concat_axis=0, tiled=True)  6.32 us
  transfers between devices with their start and end apart: 12, of which 6 were waited for; matrix products, arithmetic and copies ran while one was open for 13% of the time, Pallas kernels for 0%

profile of v1, /device:TPU:0, one launch (start us, length us, event | category | flops | bytes accessed | tf_op | source)
XLA Modules:
  0.0 220.4 jit_solution(7653049881767182576)
XLA Ops:
  7.2 0.8 iota_compare_fusion.3
  8.0 0.7 copy.50
  8.7 6.3 %all-to-all-start = ((bf16[4,1,1]{2,1,0:T(2,128)(2,1)}), bf16[4,1,1]{2,1,0:T(2,128)(2,1)S(1)}, u32[]{:S(2)}, u32[]{:S(2)}) async-start(bf16[4,1,1]{2,1,0:T(2,128)(2,1)} %copy.50), calls=%async_computation | async-start | bytes 4096 | tf_op jit(solution)/shard_map/all_to_all | solution.py:56
  15.0 0.9 convert_reduce_fusion
  15.9 0.7 fusion.58
  16.7 1.1 multiply_bitcast_fusion
  18.3 1.2 reshape.180
  19.5 1.0 all-to-all-done
  20.5 4.1 %all-to-all-start.1 = ((bf16[4,2,36864]{2,1,0:T(2,128)(2,1)}), bf16[4,2,36864]{2,1,0:T(2,128)(2,1)S(1)}, u32[]{:S(2)}, u32[]{:S(2)}) async-start(bf16[4,2,36864]{2,1,0:T(2,128)(2,1)} %reshape.180), calls=%async_computation.1 | async-start | bytes 1179648 | tf_op jit(solution)/shard_map/all_to_all | solution.py:55
  25.0 14.9 %all-to-all-done.1 = bf16[4,2,36864]{2,1,0:T(2,128)(2,1)S(1)} async-done(((bf16[4,2,36864]{2,1,0:T(2,128)(2,1)}), bf16[4,2,36864]{2,1,0:T(2,128)(2,1)S(1)}, u32[]{:S(2)}, u32[]{:S(2)}) %all-to-all-start.1) | async-done | bytes 589856 | tf_op jit(solution)/shard_map/all_to_all | solution.py:55
  40.2 0.3 convolution_convert_fusion.1
  40.7 1.3 collective-permute-start
  42.0 1.3 collective-permute-start.1
  43.3 4.2 %collective-permute-done.1 = bf16[4,384]{1,0:T(4,128)(2,1)S(1)} collective-permute-done((bf16[4,384]{1,0:T(4,128)(2,1)S(1)}, bf16[4,384]{1,0:T(4,128)(2,1)S(1)}, u32[]{:S(2)}, u32[]{:S(2)}) %collective-permute-start.1) | collective-permute-done | bytes 3104 | tf_op jit(solution)/shard_map/ppermute | solution.py:21
  47.5 0.8 pad_maximum_fusion
  48.5 0.7 copy.53
  49.1 3.9 %all-to-all-start.2 = ((bf16[64,4,192]{2,0,1:T(8,128)(2,1)}), bf16[64,4,192]{2,0,1:T(8,128)(2,1)S(1)}, u32[]{:S(2)}, u32[]{:S(2)}) async-start(bf16[64,4,192]{2,0,1:T(8,128)(2,1)} %copy.53), calls=%async_computation.2 | async-start | bytes 262144 | tf_op jit(solution)/shard_map/all_to_all | solution.py:92
  53.1 5.9 %all-to-all-done.2 = bf16[64,4,192]{2,0,1:T(8,128)(2,1)S(1)} async-done(((bf16[64,4,192]{2,0,1:T(8,128)(2,1)}), bf16[64,4,192]{2,0,1:T(8,128)(2,1)S(1)}, u32[]{:S(2)}, u32[]{:S(2)}) %all-to-all-start.2) | async-done | bytes 98336 | tf_op jit(solution)/shard_map/all_to_all | solution.py:92
  59.1 9.4 %all-gather = bf16[4,256,1,192]{3,0,2,1:T(4,128)(2,1)S(1)} all-gather(bf16[4,64,1,192]{3,0,2,1:T(4,128)(2,1)S(1)} %copy.54), channel_id=2, replica_groups=mesh['groups'=2,'seq'=4,'chan'=4] {'chan'}, dimensions={1}, use_global_device_ids=true | all-gather | bytes 491520 | tf_op jit(solution)/shard_map/all_gather | solution.py:95
  68.5 0.6 copy.55
  69.2 2.5 %fusion.12 = f32[384,384]{1,0:T(8,128)S(1)} fusion(bf16[392,1536]{1,0:T(8,128)(2,1)} %all-gather.4.cloned.1.call-done, bf16[1536,5,384]{2,0,1:T(8,128)(2,1)} %param.11), kind=kOutput, calls=%fused_computation.28 | convolution fusion | flops 452984832 | bytes 2949120 | tf_op jit(solution)/shard_map/dot_general | solution.py:78
  71.7 2.1 convolution_add_fusion.5
  73.8 2.1 convolution_add_fusion.4
  75.9 2.1 convolution_add_fusion.3
  78.0 2.2 multiply_multiply_fusion.2
  80.2 0.3 reshape.183
  80.5 0.5 fusion.69
  81.2 0.5 fusion.52
  81.7 6.0 %psum.7 = f32[4,192]{1,0:T(4,128)S(1)} all-reduce(f32[4,192]{1,0:T(4,128)S(1)} %pad_maximum_fusion.5), channel_id=1, replica_groups=mesh['groups'=2,'seq'=4,'chan'=4] {'chan'}, use_global_device_ids=true, to_apply=%region_7.8 | all-reduce | flops 768 | bytes 6144 | tf_op jit(solution)/shard_map/psum | solution.py:99
  88.2 0.4 reshape.190
  88.6 0.4 fusion.44
  89.0 3.6 %fusion.20 = f32[384,1536]{1,0:T(8,128)} fusion(bf16[384,384]{1,0:T(8,128)(2,1)S(1)} %fusion.44, bf16[1536,5,384]{2,0,1:T(8,128)(2,1)} %param.11), kind=kOutput, calls=%fused_computation.36 | convolution fusion | flops 452984832 | bytes 3833856 | tf_op jit(solution)/shard_map/io,po->ip/dot_general | solution.py:135
  92.6 1.3 collective-permute-start.2
  93.9 4.5 %collective-permute-start.3 = (bf16[4,384]{1,0:T(4,128)(2,1)S(1)}, bf16[4,384]{1,0:T(4,128)(2,1)S(1)}, u32[]{:S(2)}, u32[]{:S(2)}) collective-permute-start(bf16[4,384]{1,0:T(4,128)(2,1)S(1)} %get-tuple-element.43), channel_id=1, source_target_pairs={{0,4},{4,8},{8,12},{1,5},{5,9},{9,13},{2,6},{6,10},{10,14},{3,7},{... | collective-permute-start | bytes 9224 | tf_op jit(solution)/shard_map/ppermute | solution.py:19
  98.4 16.7 %all_gather.17 = bf16[768,384]{1,0:T(8,128)(2,1)S(1)} all-gather(bf16[192,384]{1,0:T(8,128)(2,1)S(1)} %get-tuple-element.41), channel_id=1, replica_groups=mesh['groups'=2,'seq'=4,'chan'=4] {'seq'}, dimensions={0}, use_global_device_ids=true | all-gather | bytes 737280 | tf_op jit(solution)/shard_map/all_gather | solution.py:121
  115.2 1.3 fusion.55
  116.5 2.1 fusion.23
  118.6 2.2 %fusion.15 = f32[384,1536]{1,0:T(8,128)S(1)} fusion(bf16[1536,5,384]{2,0,1:T(8,128)(2,1)} %param.11, bf16[384,384]{1,0:T(8,128)(2,1)S(1)} %fusion.44, bf16[4,384]{1,0:T(4,128)(2,1)S(1)} %collective-permute-done.3), kind=kOutput, calls=%fused_computation.31 | convolution fusion | flops 453574656 | bytes 3836928 | tf_op jit(solution)/shard_map/io,po->ip/dot_general | solution.py:135
  120.8 2.1 fusion.1
  123.0 2.1 fusion.2
  125.1 1.1 copy.78
  126.2 3.5 %all-to-all-start.4 = ((bf16[4,384,384]{1,2,0:T(8,128)(2,1)}), bf16[4,384,384]{1,2,0:T(8,128)(2,1)S(1)}, u32[]{:S(2)}, u32[]{:S(2)}) async-start(bf16[4,384,384]{1,2,0:T(8,128)(2,1)} %bitcast.123), calls=%async_computation.5 | async-start | bytes 2359296 | tf_op jit(solution)/shard_map/all_to_all | solution.py:141
  129.8 2.4 %copy.77 = bf16[49,4,8,384]{3,2,0,1:T(8,128)(2,1)} copy(bf16[49,4,8,384]{3,2,1,0:T(8,128)(2,1)} %bitcast.128) | data formatting | bytes 2408448 | tf_op jit(solution)/shard_map/reshape | solution.py:125
  132.2 17.6 %all-to-all-done.4 = bf16[4,384,384]{1,2,0:T(8,128)(2,1)S(1)} async-done(((bf16[4,384,384]{1,2,0:T(8,128)(2,1)}), bf16[4,384,384]{1,2,0:T(8,128)(2,1)S(1)}, u32[]{:S(2)}, u32[]{:S(2)}) %all-to-all-start.4) | async-done | bytes 1179680 | tf_op jit(solution)/shard_map/all_to_all | solution.py:141
  149.8 1.0 copy-done.3
  150.8 3.5 %all-to-all-start.3 = ((bf16[392,4,384]{2,0,1:T(8,128)(2,1)}), bf16[392,4,384]{2,0,1:T(8,128)(2,1)S(1)}, u32[]{:S(2)}, u32[]{:S(2)}) async-start(bf16[392,4,384]{2,0,1:T(8,128)(2,1)} %bitcast.122), calls=%async_computation.4 | async-start | bytes 2408448 | tf_op jit(solution)/shard_map/all_to_all | solution.py:124
  154.4 0.7 all-gather.6.cloned.1.call-update
  155.1 6.1 %all_gather.19 = bf16[256,768]{1,0:T(8,128)(2,1)S(1)} all-gather(bf16[64,768]{1,0:T(8,128)(2,1)S(1)} %copy-done.9), channel_id=1, replica_groups=mesh['groups'=2,'seq'=4,'chan'=4] {'chan'}, dimensions={0}, use_global_device_ids=true | all-gather | bytes 491520 | tf_op jit(solution)/shard_map/all_gather | solution.py:96
  161.3 0.4 convolution_bitcast_fusion.5
  161.7 0.9 copy.59
  162.6 1.6 reduce_sum.82
  164.1 0.9 copy.60
  165.0 1.6 convert_element_type.68
  166.6 35.6 %all-to-all-done.3 = bf16[392,4,384]{2,0,1:T(8,128)(2,1)S(1)} async-done(((bf16[392,4,384]{2,0,1:T(8,128)(2,1)}), bf16[392,4,384]{2,0,1:T(8,128)(2,1)S(1)}, u32[]{:S(2)}, u32[]{:S(2)}) %all-to-all-start.3) | async-done | bytes 1204256 | tf_op jit(solution)/shard_map/all_to_all | solution.py:124
  202.2 2.9 %fusion.68 = (bf16[4,384,384]{2,1,0:T(8,128)(2,1)}, bf16[4,384,384]{2,1,0:T(8,128)(2,1)}, bf16[4,384,384]{2,1,0:T(8,128)(2,1)}, bf16[4,384,384]{2,1,0:T(8,128)(2,1)}, bf16[4,384,384]{2,1,0:T(8,128)(2,1)}) fusion(bf16[4,392,384]{2,1,0:T(8,128)(2,1)S(1)} %bitcast.121), kind=kLoop, calls=%fused_computation.117 | loop fusion | bytes 11796480 | tf_op jit(solution)/shard_map/slice | solution.py:151
  205.1 2.6 %fusion.8 = f32[384,5,384]{2,0,1:T(8,128)S(1)} fusion(bf16[1536,384]{1,0:T(8,128)(2,1)} %bitcast.133, bf16[1536,384]{1,0:T(8,128)(2,1)} %all-gather.6.cloned.1.call-done), kind=kOutput, calls=%fused_computation.21 | convolution fusion | flops 452984832 | bytes 2949120 | tf_op jit(solution)/shard_map/pi,po->io/dot_general | solution.py:149
  207.7 0.8 fusion.7
  208.5 0.5 copy-done.7
  209.0 0.8 fusion.6
  209.8 0.5 copy-done.6
  210.2 0.8 fusion.5
  211.0 0.5 copy-done.5
  211.5 0.8 fusion.4
  212.3 1.6 copy-done.14
  (59 shorter events, 2.5 us)
Async XLA Ops:
  7.2 73.9 %copy-start = (bf16[1024,384]{1,0:T(8,128)(2,1)S(1)}, bf16[1024,384]{1,0:T(8,128)(2,1)}, u32[]{:S(2)}) copy-start(bf16[1024,384]{1,0:T(8,128)(2,1)} %param.14) | copy-start | bytes 2359300
  7.2 10.8 %copy-start.13 = (s32[5]{0:T(128)S(1)}, s32[5]{0:T(128)}, u32[]{:S(2)}) copy-start(s32[5]{0:T(128)} %param.9) | copy-start | bytes 64
  8.7 11.8 %all-to-all-start = ((bf16[4,1,1]{2,1,0:T(2,128)(2,1)}), bf16[4,1,1]{2,1,0:T(2,128)(2,1)S(1)}, u32[]{:S(2)}, u32[]{:S(2)}) async-start(bf16[4,1,1]{2,1,0:T(2,128)(2,1)} %copy.50), calls=%async_computation | async-start | bytes 4096 | tf_op jit(solution)/shard_map/all_to_all | solution.py:56
  20.5 19.4 %all-to-all-start.1 = ((bf16[4,2,36864]{2,1,0:T(2,128)(2,1)}), bf16[4,2,36864]{2,1,0:T(2,128)(2,1)S(1)}, u32[]{:S(2)}, u32[]{:S(2)}) async-start(bf16[4,2,36864]{2,1,0:T(2,128)(2,1)} %reshape.180), calls=%async_computation.1 | async-start | bytes 1179648 | tf_op jit(solution)/shard_map/all_to_all | solution.py:55
  24.6 44.6 %all-gather.4.cloned.1.call-start = ((), (), s32[]{:S(2)}) async-start(), calls=%async_computation.6 | async-start | bytes 1505280 | tf_op jit(solution)/shard_map/all_gather | solution.py:75
  40.1 8.1 %copy-start.9 = (bf16[64,768]{1,0:T(8,128)(2,1)S(1)}, bf16[64,768]{1,0:T(8,128)(2,1)}, u32[]{:S(2)}) copy-start(bf16[64,768]{1,0:T(8,128)(2,1)} %param.15) | copy-start | bytes 294916
  40.7 2.6 %collective-permute-start = (bf16[4,384]{1,0:T(4,128)(2,1)S(1)}, bf16[4,384]{1,0:T(4,128)(2,1)S(1)}, u32[]{:S(2)}, u32[]{:S(2)}) collective-permute-start(bf16[4,384]{1,0:T(4,128)(2,1)S(1)} %get-tuple-element.44), channel_id=1, source_target_pairs={{0,4},{4,8},{8,12},{1,5},{5,9},{9,13},{2,6},{6,10},{10,14},{3,7},{... | collective-permute-start | bytes 9224 | tf_op jit(solution)/shard_map/ppermute | solution.py:19
  42.0 5.5 %collective-permute-start.1 = (bf16[4,384]{1,0:T(4,128)(2,1)S(1)}, bf16[4,384]{1,0:T(4,128)(2,1)S(1)}, u32[]{:S(2)}, u32[]{:S(2)}) collective-permute-start(bf16[4,384]{1,0:T(4,128)(2,1)S(1)} %get-tuple-element.45), channel_id=1, source_target_pairs={{4,0},{8,4},{12,8},{5,1},{9,5},{13,9},{6,2},{10,6},{14,10},{7,3},{... | collective-permute-start | bytes 9224 | tf_op jit(solution)/shard_map/ppermute | solution.py:21
  49.1 9.8 %all-to-all-start.2 = ((bf16[64,4,192]{2,0,1:T(8,128)(2,1)}), bf16[64,4,192]{2,0,1:T(8,128)(2,1)S(1)}, u32[]{:S(2)}, u32[]{:S(2)}) async-start(bf16[64,4,192]{2,0,1:T(8,128)(2,1)} %copy.53), calls=%async_computation.2 | async-start | bytes 262144 | tf_op jit(solution)/shard_map/all_to_all | solution.py:92
  53.0 112.0 %reduce-scatter.2.cloned.1.call-start = ((), (), s32[]{:S(2)}) async-start(), calls=%async_computation.7 | async-start | bytes 983040 | tf_op jit(solution)/shard_map/reduce_scatter | solution.py:130
  69.2 2.5 %copy-start.4 = (bf16[392,1536]{1,0:T(8,128)(2,1)S(1)}, bf16[392,1536]{1,0:T(8,128)(2,1)}, u32[]{:S(2)}) copy-start(bf16[392,1536]{1,0:T(8,128)(2,1)} %all-gather.4.cloned.1.call-done) | copy-start | bytes 3612676
  75.8 2.1 copy-start.12
  80.5 0.7 copy-start.10
  89.0 34.0 %copy-start.1 = (bf16[384,384]{1,0:T(8,128)(2,1)}, bf16[384,384]{1,0:T(8,128)(2,1)S(1)}, u32[]{:S(2)}) copy-start(bf16[384,384]{1,0:T(8,128)(2,1)S(1)} %fusion.44) | copy-start | bytes 884740
  92.6 23.9 %collective-permute-start.2 = (bf16[4,384]{1,0:T(4,128)(2,1)S(1)}, bf16[4,384]{1,0:T(4,128)(2,1)S(1)}, u32[]{:S(2)}, u32[]{:S(2)}) collective-permute-start(bf16[4,384]{1,0:T(4,128)(2,1)S(1)} %get-tuple-element.42), channel_id=1, source_target_pairs={{4,0},{8,4},{12,8},{5,1},{9,5},{13,9},{6,2},{10,6},{14,10},{7,3},{... | collective-permute-start | bytes 9224 | tf_op jit(solution)/shard_map/ppermute | solution.py:21
  93.9 24.7 %collective-permute-start.3 = (bf16[4,384]{1,0:T(4,128)(2,1)S(1)}, bf16[4,384]{1,0:T(4,128)(2,1)S(1)}, u32[]{:S(2)}, u32[]{:S(2)}) collective-permute-start(bf16[4,384]{1,0:T(4,128)(2,1)S(1)} %get-tuple-element.43), channel_id=1, source_target_pairs={{0,4},{4,8},{8,12},{1,5},{5,9},{9,13},{2,6},{6,10},{10,14},{3,7},{... | collective-permute-start | bytes 9224 | tf_op jit(solution)/shard_map/ppermute | solution.py:19
  118.5 2.3 %copy-start.2 = (f32[384,1536]{1,0:T(8,128)S(1)}, f32[384,1536]{1,0:T(8,128)}, u32[]{:S(2)}) copy-start(f32[384,1536]{1,0:T(8,128)} %fusion.20) | copy-start | bytes 7077892
  126.2 23.6 %all-to-all-start.4 = ((bf16[4,384,384]{1,2,0:T(8,128)(2,1)}), bf16[4,384,384]{1,2,0:T(8,128)(2,1)S(1)}, u32[]{:S(2)}, u32[]{:S(2)}) async-start(bf16[4,384,384]{1,2,0:T(8,128)(2,1)} %bitcast.123), calls=%async_computation.5 | async-start | bytes 2359296 | tf_op jit(solution)/shard_map/all_to_all | solution.py:141
  149.8 1.0 copy-start.3
  150.8 51.4 %all-to-all-start.3 = ((bf16[392,4,384]{2,0,1:T(8,128)(2,1)}), bf16[392,4,384]{2,0,1:T(8,128)(2,1)S(1)}, u32[]{:S(2)}, u32[]{:S(2)}) async-start(bf16[392,4,384]{2,0,1:T(8,128)(2,1)} %bitcast.122), calls=%async_computation.4 | async-start | bytes 2408448 | tf_op jit(solution)/shard_map/all_to_all | solution.py:124
  154.4 50.7 %all-gather.6.cloned.1.call-start = ((), (), s32[]{:S(2)}) async-start(), calls=%async_computation.8 | async-start | bytes 1474560 | tf_op jit(solution)/shard_map/all_gather | solution.py:122
  205.1 2.6 %copy-start.8 = (bf16[4,384,384]{2,1,0:T(8,128)(2,1)S(1)}, bf16[4,384,384]{2,1,0:T(8,128)(2,1)}, u32[]{:S(2)}) copy-start(bf16[4,384,384]{2,1,0:T(8,128)(2,1)} %get-tuple-element.36) | copy-start | bytes 3538948
  205.1 2.6 %copy-start.11 = (bf16[1536,384]{1,0:T(8,128)(2,1)S(1)}, bf16[1536,384]{1,0:T(8,128)(2,1)}, u32[]{:S(2)}) copy-start(bf16[1536,384]{1,0:T(8,128)(2,1)} %all-gather.6.cloned.1.call-done) | copy-start | bytes 3538948
  207.7 1.3 copy-start.7
  209.0 1.3 copy-start.6
  210.2 1.3 copy-start.5
  212.3 1.6 copy-start.14
Sparse Core Ops, SparseCore 0:
  48.4 20.1 all-gather.3
  116.6 26.7 reduce-scatter.1
  156.9 45.9 all-gather.5

commit v2 on v0

v2 whole, which is shorter than its diff:
```python
import functools

import jax
import jax.numpy as jnp
from jax import lax
from jax.experimental import pallas as pl
from jax.experimental.pallas import tpu as pltpu
from jax.sharding import PartitionSpec as P

KERNEL_TAPS = 5
DILATION_STEP = 2
CAP = 2
EDGE = 2 * DILATION_STEP
BF = jnp.bfloat16
F32 = jnp.float32
ROOT = 0.7978845608028654
CUBE = 0.044715

VMEM = pl.BlockSpec(memory_space=pltpu.VMEM)
SMEM = pl.BlockSpec(memory_space=pltpu.SMEM)
ANY = pl.BlockSpec(memory_space=pl.ANY)


def struct(shape, dtype):
    return jax.ShapeDtypeStruct(shape, dtype)


def launch(body, outs, ins, specs=None, scratch=(), flops=0, moved=0, name=None):
    return pl.pallas_call(
        body,
        out_shape=outs,
        in_specs=specs or [VMEM] * len(ins),
        out_specs=jax.tree.map(lambda _: VMEM, outs),
        scratch_shapes=list(scratch),
        compiler_params=pltpu.CompilerParams(vmem_limit_bytes=40 * 1024 * 1024),
        cost_estimate=pl.CostEstimate(flops=flops, bytes_accessed=moved, transcendentals=0),
        name=name,
    )(*ins)


def dot(a, b, dims=((1,), (0,))):
    return lax.dot_general(a, b, (dims, ((), ())), preferred_element_type=F32)


def wrap(value, count):
    return lax.rem(value + count, count)


def pack_kernel(slabs, rows, block_len, dest_ref, kept_ref, x_ref, *outs):
    me = lax.axis_index("seq")
    payload = outs[0].shape[0]
    dest = [jnp.where(dest_ref[r] >= slabs, -100, dest_ref[r]) for r in range(rows)]
    rank, total = [], []
    for r in range(rows):
        before, count = jnp.int32(0), jnp.int32(0)
        for q in range(rows):
            same = (dest[q] == dest[r]).astype(jnp.int32)
            count = count + same
            if q < r:
                before = before + same
        rank.append(before)
        total.append(count)
    columns = rows * block_len
    col = lax.broadcasted_iota(jnp.int32, (1, columns), 1)
    dest_v = jnp.full((1, columns), -100, jnp.int32)
    rank_v = jnp.zeros((1, columns), jnp.int32)
    last_v = jnp.zeros((1, columns), jnp.int32)
    place = jnp.zeros((1, columns), jnp.int32)
    for r in range(rows):
        offset = col - r * block_len
        here = (offset >= 0) & (offset < kept_ref[r]) & (offset < block_len)
        dest_v = jnp.where(here, dest[r], dest_v)
        rank_v = jnp.where(here, rank[r], rank_v)
        last_v = jnp.where(here, (rank[r] == total[r] - 1).astype(jnp.int32), last_v)
        place = jnp.where(here, offset, place)
    row = lax.broadcasted_iota(jnp.int32, (payload, columns), 0)
    line = lax.broadcasted_iota(jnp.int32, (payload, 1), 0)
    base = CAP * block_len
    x = x_ref[...]
    for k, out in enumerate(outs):
        to = wrap(me + k, slabs)
        key = jnp.where(dest_v == to, rank_v * block_len + place, -1)
        key = jnp.where((dest_v == to + 1) & (rank_v == 0) & (place < EDGE), base + place, key)
        tail = place - (block_len - EDGE)
        key = jnp.where((dest_v == to - 1) & (last_v == 1) & (tail >= 0), base + EDGE + tail, key)
        picker = jnp.where(row == key, 1.0, 0.0).astype(BF)
        rows_out = dot(picker, x)
        for spot, slab in enumerate((to, to - 1, to + 1)):
            count = jnp.int32(0)
            for r in range(rows):
                count = count + (dest[r] == slab).astype(jnp.int32)
            rows_out = jnp.where(line == base + 2 * EDGE + spot, count.astype(F32), rows_out)
        out[...] = rows_out.astype(BF)


def unpack_kernel(slabs, block_len, *refs):
    ins, out = refs[:slabs], refs[slabs]
    me = lax.axis_index("seq")
    payload = ins[0].shape[0]
    base = CAP * block_len
    length = slabs * block_len
    heads = [r[payload - 16 : payload, :].astype(F32) for r in ins]
    own = [h[2 * EDGE : 2 * EDGE + 1, :payload] for h in heads]
    prev = [h[2 * EDGE + 1 : 2 * EDGE + 2, :payload] for h in heads]
    following = [h[2 * EDGE + 2 : 2 * EDGE + 3, :payload] for h in heads]
    source = [wrap(me - k, slabs) for k in range(slabs)]
    col = lax.broadcasted_iota(jnp.int32, (1, payload), 1)
    slot = jnp.where(col >= block_len, 1, 0)
    place = (col - slot * block_len).astype(F32)
    slot = slot.astype(F32)
    colf = col.astype(F32)
    row = lax.broadcasted_iota(jnp.int32, out.shape[:1] + (payload,), 0).astype(F32)
    total = jnp.zeros(out.shape, F32)
    for k in range(slabs):
        offsets = []
        for counts in (own, prev, following):
            ahead = jnp.zeros((1, payload), F32)
            for q in range(slabs):
                if q != k:
                    ahead = ahead + jnp.where(source[q] < source[k], counts[q], 0.0)
            offsets.append(ahead)
        main = jnp.where(slot < own[k], (offsets[0] + slot) * block_len + place, -1.0)
        right = jnp.where((following[k] > 0.5) & (offsets[2] < 0.5), length + EDGE + colf - base, -1.0)
        left = jnp.where((prev[k] > 0.5) & (offsets[1] + prev[k] > slabs - 0.5), length + colf - base - EDGE, -1.0)
        key = jnp.where(col < base, main, jnp.where(col < base + EDGE, right, jnp.where(col < base + 2 * EDGE, left, -1.0)))
        total = total + dot(jnp.where(row == key, 1.0, 0.0).astype(BF), ins[k][...])
    out[...] = total.astype(BF)


def cot_kernel(slabs, chans, *refs):
    ins, (w_ref, gain_ref, out, full) = refs[:chans], refs[chans:]
    me, ch = lax.axis_index("seq"), lax.axis_index("chan")
    feat = ins[0].shape[1]
    for j in range(chans):
        owner = lax.bitwise_xor(ch, j)
        for k in range(slabs):
            begin = pl.multiple_of((wrap(me - k, slabs) * chans + owner) * feat, 8)
            full[pl.ds(begin, feat), :] = ins[j][k].astype(F32)
    out[...] = dot(full[...].astype(BF), w_ref[...], ((0,), (0,))) * gain_ref[...]


def conv_kernel(chans, slabs, *refs):
    xs, (w_ref, bias_ref, dxhat_ref, pooled_ref, slope_ref, stats_ref), rest = refs[:chans], refs[chans : chans + 6], refs[chans + 6 :]
    pieces, (weights, full, conv, shifted_sum, lanes, sems) = rest[:-6], rest[-6:]
    me, ch = lax.axis_index("seq"), lax.axis_index("chan")
    rows, width = xs[0].shape
    length = shifted_sum.shape[0]
    copies = []
    for t in range(KERNEL_TAPS):
        copies.append(pltpu.make_async_copy(w_ref.at[t], weights.at[t], sems.at[t]))
        copies[-1].start()
    for j in range(chans):
        begin = pl.multiple_of(lax.bitwise_xor(ch, j) * width, 128)
        full[:, pl.ds(begin, width)] = xs[j][...]
    part = length // chans
    begin = pl.multiple_of(ch * part, 8)
    own = width * chans // slabs
    if len(pieces) > 1:
        for k, piece in enumerate(pieces):
            first = pl.multiple_of(wrap(me + k, slabs) * own, 128)
            piece[...] = full[pl.ds(begin, part), pl.ds(first, own)]
    else:
        pieces[0][...] = full[pl.ds(begin, part), :]
    x = full[...]
    for t in range(KERNEL_TAPS):
        copies[t].wait()
        product = dot(x, weights[t])
        conv[0:EDGE] = product[length : length + EDGE]
        conv[EDGE : EDGE + length] = product[:length]
        conv[EDGE + length : 2 * EDGE + length] = product[length + EDGE : length + 2 * EDGE]
        moved = conv[t * DILATION_STEP : t * DILATION_STEP + length]
        if t == 0:
            shifted_sum[...] = moved + bias_ref[...]
        else:
            shifted_sum[...] += moved
    v = shifted_sum[...]
    th = jnp.tanh(ROOT * (v + CUBE * (v * v * v)))
    half = 0.5 * (1.0 + th)
    slope_ref[...] = half + (0.5 * ROOT) * v * (1.0 - th * th) * (1.0 + (3.0 * CUBE) * (v * v))
    act = v * half
    count = length // 2
    columns = []
    for c in range(width // 128):
        lanes[c] = act[:, c * 128 : (c + 1) * 128]
        columns.append((lanes[c, pl.ds(0, count, stride=2), :] + lanes[c, pl.ds(1, count, stride=2), :]) * 0.5)
    pooled = jnp.concatenate(columns, axis=1)
    pooled_ref[...] = pooled
    dxhat = dxhat_ref[...]
    sums = [
        jnp.sum(pooled, axis=1, keepdims=True),
        jnp.sum(pooled * pooled, axis=1, keepdims=True),
        jnp.sum(dxhat, axis=1, keepdims=True),
        jnp.sum(dxhat * pooled, axis=1, keepdims=True),
    ]
    lane = lax.broadcasted_iota(jnp.int32, (count, 128), 1)
    table = jnp.zeros((count, 128), F32)
    for n, s in enumerate(sums):
        table = jnp.where(lane == n, s, table)
    padded = stats_ref.shape[1]
    if padded > count:
        table = jnp.concatenate([table, jnp.zeros((padded - count, 128), F32)], axis=0)
    stats_ref[...] = table.T[:8]


def grad_kernel(chans, *refs):
    stats, (pooled_ref, slope_ref, dxhat_ref, gain_ref, normed_ref, dy_ref, head_ref, tail_ref, twice) = refs[:chans], refs[chans:]
    count, width = pooled_ref.shape
    total = stats[0][...]
    for s in stats[1:]:
        total = total + s[...]
    total = total * (1.0 / (width * chans))
    table = jnp.concatenate([total, jnp.zeros((120, total.shape[1]), F32)], axis=0).T[:count]
    mean = table[:, 0:1]
    rstd = lax.rsqrt(table[:, 1:2] - mean * mean + 1e-05)
    leading = table[:, 2:3]
    trailing = rstd * (table[:, 3:4] - mean * leading)
    xhat = (pooled_ref[...] - mean) * rstd
    normed_ref[...] = (xhat * gain_ref[...]).astype(BF)
    half = (0.5 * rstd) * (dxhat_ref[...] - leading - xhat * trailing)
    columns = []
    for c in range(width // 128):
        twice[c, pl.ds(0, count, stride=2), :] = half[:, c * 128 : (c + 1) * 128]
        twice[c, pl.ds(1, count, stride=2), :] = half[:, c * 128 : (c + 1) * 128]
        columns.append(twice[c])
    dy = (jnp.concatenate(columns, axis=1) * slope_ref[...]).astype(BF)
    dy_ref[...] = dy
    head_ref[...] = dy[:16]
    tail_ref[...] = dy[dy.shape[0] - 16 :]


def dx_kernel(chans, *refs):
    (dy_ref, left_ref, right_ref, w_ref), outs, (weights, wide, moved, sems) = refs[:4], refs[4 : 4 + chans], refs[4 + chans :]
    ch = lax.axis_index("chan")
    length, width = dy_ref.shape
    order = list(range(chans - 1, -1, -1))
    copies = []
    for j in order:
        begin = pl.multiple_of(lax.bitwise_xor(ch, j) * width, 16)
        copies.append(pltpu.make_async_copy(w_ref.at[:, pl.ds(begin, width), :], weights.at[j], sems.at[j]))
        copies[-1].start()
    wide[0:EDGE] = left_ref[...].astype(F32)[16 - EDGE :]
    wide[EDGE : EDGE + length] = dy_ref[...].astype(F32)
    wide[EDGE + length : 2 * EDGE + length] = right_ref[...].astype(F32)[:EDGE]
    for t in range(KERNEL_TAPS):
        begin = 2 * EDGE - t * DILATION_STEP
        moved[t] = wide[begin : begin + length].astype(BF)
    for n, j in enumerate(order):
        copies[n].wait()
        total = dot(weights[j, 0], moved[0], ((1,), (1,)))
        for t in range(1, KERNEL_TAPS):
            total = total + dot(weights[j, t], moved[t], ((1,), (1,)))
        outs[j][...] = total.astype(outs[j].dtype)


def transpose_kernel(slabs, chans, x_ref, out, full):
    me = lax.axis_index("seq")
    part = x_ref.shape[2]
    for j in range(chans):
        for k in range(slabs):
            begin = pl.multiple_of((wrap(me - k, slabs) * chans + j) * part, 8)
            full[pl.ds(begin, part), :] = x_ref[j, k]
    out[...] = full[...].T


def dw_kernel(slabs, *refs):
    xt_ref, dys, (out, full, moved) = refs[0], refs[1 : 1 + slabs], refs[1 + slabs :]
    me = lax.axis_index("seq")
    length, width = dys[0].shape
    every = length * slabs
    full[0:8] = jnp.zeros((8, width), F32)
    full[8 + every : 16 + every] = jnp.zeros((8, width), F32)
    for k in range(slabs):
        begin = pl.multiple_of(wrap(me - k, slabs) * length + 8, 8)
        full[pl.ds(begin, length), :] = dys[k][...].astype(F32)
    xt = xt_ref[...]
    for t in range(KERNEL_TAPS):
        begin = 8 + EDGE - t * DILATION_STEP
        moved[...] = full[begin : begin + every].astype(BF)
        out[t] = dot(xt, moved[...])


def proj_kernel(slabs, chans, *refs):
    cots, normed, (w_ref, dw_ref), outs, (wide, full, part) = (
        refs[:chans],
        refs[chans : chans + slabs],
        refs[chans + slabs : chans + slabs + 2],
        refs[chans + slabs + 2 : 2 * chans + slabs + 2],
        refs[2 * chans + slabs + 2 :],
    )
    me, ch = lax.axis_index("seq"), lax.axis_index("chan")
    feat = cots[0].shape[0]
    count = normed[0].shape[0]
    for j in range(chans):
        wide[pl.ds(pl.multiple_of(lax.bitwise_xor(ch, j) * feat, 8), feat), :] = cots[j][...]
    for k in range(slabs):
        full[pl.ds(pl.multiple_of(wrap(me - k, slabs) * count, 8), count), :] = normed[k][...]
    every = full[...]
    dw_ref[...] = dot(wide[...], every)
    rows = feat * chans
    part[...] = dot(w_ref[pl.ds(pl.multiple_of(me * rows, 8), rows), :], every, ((1,), (1,)))
    for j in range(chans):
        outs[j][...] = part[pl.ds(pl.multiple_of(lax.bitwise_xor(ch, j) * feat, 8), feat), :].astype(outs[j].dtype)


def swaps(value, count):
    return [value] + [lax.ppermute(value, "chan", [(i, i ^ j) for i in range(count)]) for j in range(1, count)]


def turn(value, k, count):
    return lax.ppermute(value, "seq", [(i, (i + k) % count) for i in range(count)]) if k else value


def gather_seq(value, count):
    if count <= 8:
        return [turn(value, k, count) for k in range(count)]
    every = lax.all_gather(value, "seq", axis=0, tiled=False)
    every = jnp.roll(every[::-1], lax.axis_index("seq") + 1, axis=0)
    return [every[k] for k in range(count)]


def trade_seq(values, count):
    if count <= 8:
        return [turn(v, k, count) for k, v in enumerate(values)]
    me = lax.axis_index("seq")
    sent = jnp.roll(jnp.stack(values), me, axis=0)
    got = lax.all_to_all(sent, "seq", split_axis=0, concat_axis=0, tiled=True)
    got = jnp.roll(got[::-1], me + 1, axis=0)
    return [got[k] for k in range(count)]


def per_device(x_rows, dest_slab, kept_len, convolution_weight, b_conv, entry_norm_gain, w_proj, g_cot):
    slabs = lax.axis_size("seq")
    chans = lax.axis_size("chan")
    rows, block_len, width = x_rows.shape
    channels = width * chans
    length = slabs * block_len
    count = length // 2
    payload = CAP * block_len + 16
    feat, positions = g_cot.shape
    padded_rows = length + 16
    taps = jnp.transpose(convolution_weight, (1, 0, 2))
    gain = entry_norm_gain.reshape(1, width)
    own = channels // slabs
    part = length // chans

    packed = launch(
        functools.partial(pack_kernel, slabs, rows, block_len),
        [struct((payload, width), BF)] * slabs,
        [dest_slab, kept_len, x_rows.reshape(rows * block_len, width)],
        specs=[SMEM, SMEM, VMEM],
        flops=2 * payload * slabs * rows * block_len * width,
        moved=2 * payload * slabs * width,
        name="pack",
    )
    arrived = trade_seq(packed, slabs)

    me = lax.axis_index("seq")
    cot_parts = [
        lax.dynamic_slice_in_dim(g_cot, wrap(me + k, slabs) * count, count, axis=1) for k in range(slabs)
    ]
    cot_mine = jnp.stack(trade_seq(cot_parts, slabs))
    cot_all = swaps(cot_mine, chans)
    cot_wide = swaps(g_cot, chans)
    dxhat = launch(
        functools.partial(cot_kernel, slabs, chans),
        struct((count, width), F32),
        [*cot_all, w_proj, gain],
        scratch=[pltpu.VMEM((feat * chans * slabs, count), F32)],
        flops=2 * feat * chans * slabs * count * width,
        moved=2 * feat * chans * slabs * (count + width),
        name="cotangent",
    )

    routed = launch(
        functools.partial(unpack_kernel, slabs, block_len),
        struct((padded_rows, width), BF),
        arrived,
        flops=2 * payload * slabs * padded_rows * width,
        moved=2 * payload * slabs * width,
        name="unpack",
    )
    x_all = swaps(routed, chans)
    small = slabs == chans
    piece_shapes = [struct((part, own), BF)] * slabs if small else [struct((part, channels), BF)]
    conv_outs = launch(
        functools.partial(conv_kernel, chans, slabs),
        [struct((count, width), F32), struct((length, width), F32), struct((8, -(-count // 128) * 128), F32), *piece_shapes],
        [*x_all, taps, b_conv.reshape(1, width), dxhat],
        specs=[VMEM] * chans + [ANY, VMEM, VMEM],
        scratch=[
            pltpu.VMEM((KERNEL_TAPS, channels, width), BF),
            pltpu.VMEM((padded_rows, channels), BF),
            pltpu.VMEM((length + 2 * EDGE, width), F32),
            pltpu.VMEM((length, width), F32),
            pltpu.VMEM((width // 128, length, 128), F32),
            pltpu.SemaphoreType.DMA((KERNEL_TAPS,)),
        ],
        flops=2 * padded_rows * channels * width * KERNEL_TAPS,
        moved=2 * channels * width * KERNEL_TAPS,
        name="conv",
    )
    pooled, slope, stats, pieces = conv_outs[0], conv_outs[1], conv_outs[2], conv_outs[3:]
    if small:
        mine = jnp.stack(trade_seq(pieces, slabs))
    else:
        mine = lax.all_to_all(pieces[0].reshape(part, slabs, own), "seq", split_axis=1, concat_axis=0, tiled=True)
        mine = jnp.roll(mine.reshape(slabs, part, own)[::-1], me + 1, axis=0)
    x_own = lax.all_gather(mine, "chan", axis=0, tiled=False)
    x_turned = launch(
        functools.partial(transpose_kernel, slabs, chans),
        struct((own, length * slabs), BF),
        [x_own],
        scratch=[pltpu.VMEM((length * slabs, own), BF)],
        moved=4 * own * length * slabs,
        name="turn_x",
    )

    normed, dy, head, tail = launch(
        functools.partial(grad_kernel, chans),
        [struct((count, width), BF), struct((length, width), BF), struct((16, width), BF), struct((16, width), BF)],
        [*swaps(stats, chans), pooled, slope, dxhat, gain],
        scratch=[pltpu.VMEM((width // 128, length, 128), F32)],
        flops=20 * length * width,
        moved=12 * length * width,
        name="gradient",
    )
    ends = slabs - 1
    from_left = lax.ppermute(tail, "seq", [(i, i + 1) for i in range(ends)])
    from_right = lax.ppermute(head, "seq", [(i + 1, i) for i in range(ends)])
    normed_all = gather_seq(normed, slabs)
    dy_all = gather_seq(dy, slabs)

    dx_parts = launch(
        functools.partial(dx_kernel, chans),
        [struct((width, length), F32)] + [struct((width, length), BF)] * (chans - 1),
        [dy, from_left, from_right, taps],
        specs=[VMEM, VMEM, VMEM, ANY],
        scratch=[
            pltpu.VMEM((chans, KERNEL_TAPS, width, width), BF),
            pltpu.VMEM((length + 2 * EDGE, width), F32),
            pltpu.VMEM((KERNEL_TAPS, length, width), BF),
            pltpu.SemaphoreType.DMA((chans,)),
        ],
        flops=2 * length * channels * width * KERNEL_TAPS,
        moved=2 * channels * width * KERNEL_TAPS,
        name="dx",
    )
    dx_sum = dx_parts[0]
    for j in range(1, chans):
        dx_sum = dx_sum + lax.ppermute(dx_parts[j], "chan", [(i, i ^ j) for i in range(chans)]).astype(F32)
    dx_field = dx_sum.astype(BF)

    proj = launch(
        functools.partial(proj_kernel, slabs, chans),
        [struct((feat * chans, width), F32), struct((feat, positions), F32)] + [struct((feat, positions), BF)] * (chans - 1),
        [*cot_wide, *normed_all, w_proj],
        scratch=[
            pltpu.VMEM((feat * chans, positions), BF),
            pltpu.VMEM((positions, width), BF),
            pltpu.VMEM((feat * chans, positions), F32),
        ],
        flops=4 * feat * chans * positions * width,
        moved=4 * feat * chans * width,
        name="projection",
    )
    dw_proj, qk_parts = proj[0], proj[1:]
    qk_sum = qk_parts[0]
    for j in range(1, chans):
        qk_sum = qk_sum + lax.ppermute(qk_parts[j], "chan", [(i, i ^ j) for i in range(chans)]).astype(F32)
    qk_out = qk_sum.astype(BF)

    dw_taps = launch(
        functools.partial(dw_kernel, slabs),
        struct((KERNEL_TAPS, own, width), F32),
        [x_turned, *dy_all],
        scratch=[pltpu.VMEM((length * slabs + 16, width), F32), pltpu.VMEM((length * slabs, width), BF)],
        flops=2 * length * slabs * own * width * KERNEL_TAPS,
        moved=4 * own * width * KERNEL_TAPS,
        name="dw",
    )
    return (qk_out, jnp.transpose(dw_taps, (1, 0, 2)), dw_proj, dx_field)


def solution(mesh):
    return jax.shard_map(
        per_device,
        mesh=mesh,
        in_specs=(
            P(("groups", "seq"), None, "chan"),
            P(("groups", "seq")),
            P(("groups", "seq")),
            P(None, None, "chan"),
            P("chan"),
            P("chan"),
            P(None, "chan"),
            P(("seq", "chan"), "groups"),
        ),
        out_specs=(
            P(("seq", "chan"), "groups"),
            P(("groups", "seq"), None, "chan"),
            P(("groups", "seq"), "chan"),
            P("chan", ("groups", "seq")),
        ),
        check_vma=False,
    )
```

time: 387 us -> 148 us (0.38)
  the two profiles are of different devices: /device:TPU:0 before, /device:TPU:9 now
where the time goes in v2:
time: 148 us; the launch traced here: 147 us
  waiting for transfers between devices  63.1 us (43%)
  starting transfers between devices  34.5 us (23%)
  Pallas kernels  21.7 us (15%)
  between operations  14.2 us (10%)
  local copies, waits for them, and re-layouts  11.3 us (8%)
  other arithmetic  2.34 us (2%)
    ppermute x15, waiting for transfers between devices, turn(): lax.ppermute(value, 'seq', [(i, (i + k) % count) for i in range(count)])  28 us
    pallas_call x9, Pallas kernels, launch(): pl.pallas_call(body, out_shape=outs, in_specs=specs or [VMEM] * len(ins),...  21.7 us
    ppermute x12, waiting for transfers between devices, swaps(): lax.ppermute(value, 'chan', [(i, i ^ j) for i in range(count)])  21.4 us
    ppermute x15, starting transfers between devices, turn(): lax.ppermute(value, 'seq', [(i, (i + k) % count) for i in range(count)])  14.6 us
    ppermute x3, waiting for transfers between devices, per_device(): lax.ppermute(dx_parts[j], 'chan', [(i, i ^ j) for i in range(chans)])  10.3 us
    ppermute x12, starting transfers between devices, swaps(): lax.ppermute(value, 'chan', [(i, i ^ j) for i in range(count)])  9.7 us
    unnamed x16, local copies, waits for them, and re-layouts  9 us
    ppermute x1, starting transfers between devices, per_device(): from_right = lax.ppermute(head, 'seq', [(i + 1, i) for i in range(ends)])  3.36 us
  transfers between devices with their start and end apart: 36, of which 16 were waited for; matrix products, arithmetic and copies ran while one was open for 3% of the time, Pallas kernels for 6%

profile of v2, /device:TPU:9, one launch (start us, length us, event | category | flops | bytes accessed | tf_op | source)
XLA Modules:
  0.0 147.1 jit_solution(15338306998362361372)
XLA Ops:
  7.2 1.0 copy-done.5
  8.3 0.7 copy-done.6
  8.9 0.7 copy-done.7
  9.6 1.2 pack.1
  10.8 1.3 collective-permute-start.3
  12.1 1.1 collective-permute-start.4
  13.2 1.4 collective-permute-start.5
  14.6 1.0 dynamic-slice_bitcast_fusion
  15.7 3.1 %collective-permute-start.10 = (bf16[64,192]{1,0:T(8,128)(2,1)S(1)}, bf16[64,192]{1,0:T(8,128)(2,1)S(1)}, u32[]{:S(2)}, u32[]{:S(2)}) collective-permute-start(bf16[64,192]{1,0:T(8,128)(2,1)S(1)} %get-tuple-element.53), channel_id=1, source_target_pairs={{0,8},{4,12},{8,0},{12,4},{1,9},{5,13},{9,1},{13,5},{2,10},{6,14},... | collective-permute-start | bytes 73736 | tf_op jit(solution)/shard_map/ppermute | solution.py:310
  18.8 7.8 %collective-permute-done.4.refs_2_ = bf16[208,384]{1,0:T(8,128)(2,1)S(1)} collective-permute-done((bf16[208,384]{1,0:T(8,128)(2,1)S(1)}, bf16[208,384]{1,0:T(8,128)(2,1)S(1)}, u32[]{:S(2)}, u32[]{:S(2)}) %collective-permute-start.4) | collective-permute-done | bytes 159776 | tf_op jit(solution)/shard_map/ppermute | solution.py:310
  26.6 2.9 %collective-permute-done.5.refs_3_ = bf16[208,384]{1,0:T(8,128)(2,1)S(1)} collective-permute-done((bf16[208,384]{1,0:T(8,128)(2,1)S(1)}, bf16[208,384]{1,0:T(8,128)(2,1)S(1)}, u32[]{:S(2)}, u32[]{:S(2)}) %collective-permute-start.5) | collective-permute-done | bytes 159776 | tf_op jit(solution)/shard_map/ppermute | solution.py:310
  29.4 0.6 unpack.1.refs_0_
  30.0 0.7 collective-permute-start.6
  30.7 1.2 collective-permute-start.7
  31.9 0.5 collective-permute-start.8
  32.7 1.2 collective-permute-start.13
  33.9 1.2 collective-permute-start.14
  35.1 0.7 reshape.19.refs_5_.refs_7_
  35.8 0.7 reshape.18.refs_5_
  36.5 12.4 %collective-permute-done.13.refs_2_ = bf16[4,64,192]{2,1,0:T(8,128)(2,1)S(1)} collective-permute-done((bf16[4,64,192]{2,1,0:T(8,128)(2,1)S(1)}, bf16[4,64,192]{2,1,0:T(8,128)(2,1)S(1)}, u32[]{:S(2)}, u32[]{:S(2)}) %collective-permute-start.13) | collective-permute-done | bytes 98336 | tf_op jit(solution)/shard_map/ppermute | solution.py:306
  48.9 3.0 %collective-permute-done.14.refs_3_ = bf16[4,64,192]{2,1,0:T(8,128)(2,1)S(1)} collective-permute-done((bf16[4,64,192]{2,1,0:T(8,128)(2,1)S(1)}, bf16[4,64,192]{2,1,0:T(8,128)(2,1)S(1)}, u32[]{:S(2)}, u32[]{:S(2)}) %collective-permute-start.14) | collective-permute-done | bytes 98336 | tf_op jit(solution)/shard_map/ppermute | solution.py:306
  51.9 0.5 cotangent.1.refs_6_
  52.4 2.7 %copy-done.3 = bf16[1536,5,384]{2,0,1:T(8,128)(2,1)S(1)} copy-done((bf16[1536,5,384]{2,0,1:T(8,128)(2,1)S(1)}, bf16[1536,5,384]{2,0,1:T(8,128)(2,1)}, u32[]{:S(2)}) %copy-start.3) | copy-done | bytes 5898264
  55.1 6.0 %conv.1 = (f32[192,384]{1,0:T(8,128)S(1)}, f32[384,384]{1,0:T(8,128)S(1)}, f32[8,256]{1,0:T(8,128)S(1)}, bf16[96,384]{1,0:T(8,128)(2,1)S(1)}, bf16[96,384]{1,0:T...) custom-call(bf16[400,384]{1,0:T(8,128)(2,1)S(1)} %unpack.1.refs_0_, ...), custom_call_target="tpu_custom_call" | custom-call | flops 2359296000 | bytes 5898240 | tf_op jit(solution)/shard_map/conv/pallas_call | solution.py:29
  61.2 2.0 %collective-permute-start.25 = (bf16[96,384]{1,0:T(8,128)(2,1)S(1)}, bf16[96,384]{1,0:T(8,128)(2,1)S(1)}, u32[]{:S(2)}, u32[]{:S(2)}) collective-permute-start(bf16[96,384]{1,0:T(8,128)(2,1)S(1)} %get-tuple-element.42), channel_id=1, source_target_pairs={{0,8},{4,12},{8,0},{12,4},{1,9},{5,13},{9,1},{13,5},{2,10},{6,14},... | collective-permute-start | bytes 221192 | tf_op jit(solution)/shard_map/ppermute | solution.py:310
  63.2 1.4 collective-permute-start.26
  64.8 2.4 %collective-permute-done.25 = bf16[96,384]{1,0:T(8,128)(2,1)S(1)} collective-permute-done((bf16[96,384]{1,0:T(8,128)(2,1)S(1)}, bf16[96,384]{1,0:T(8,128)(2,1)S(1)}, u32[]{:S(2)}, u32[]{:S(2)}) %collective-permute-start.25) | collective-permute-done | bytes 73760 | tf_op jit(solution)/shard_map/ppermute | solution.py:310
  67.2 3.4 %collective-permute-done.26 = bf16[96,384]{1,0:T(8,128)(2,1)S(1)} collective-permute-done((bf16[96,384]{1,0:T(8,128)(2,1)S(1)}, bf16[96,384]{1,0:T(8,128)(2,1)S(1)}, u32[]{:S(2)}, u32[]{:S(2)}) %collective-permute-start.26) | collective-permute-done | bytes 73760 | tf_op jit(solution)/shard_map/ppermute | solution.py:310
  70.6 0.8 pad_maximum_fusion
  71.4 0.6 collective-permute-start.15
  72.0 1.2 collective-permute-start.16
  73.2 0.5 collective-permute-start.17
  73.7 0.8 collective-permute-done.16.refs_2_
  74.5 1.8 %collective-permute-done.17.refs_3_ = f32[8,256]{1,0:T(8,128)S(1)} collective-permute-done((f32[8,256]{1,0:T(8,128)S(1)}, f32[8,256]{1,0:T(8,128)S(1)}, u32[]{:S(2)}, u32[]{:S(2)}) %collective-permute-start.17) | collective-permute-done | bytes 8224 | tf_op jit(solution)/shard_map/ppermute | solution.py:306
  76.3 0.6 gradient.1
  76.8 1.9 %collective-permute-start.30 = (bf16[16,384]{1,0:T(8,128)(2,1)S(1)}, bf16[16,384]{1,0:T(8,128)(2,1)S(1)}, u32[]{:S(2)}, u32[]{:S(2)}) collective-permute-start(bf16[16,384]{1,0:T(8,128)(2,1)S(1)} %get-tuple-element.46), channel_id=1, source_target_pairs={{0,4},{4,8},{8,12},{1,5},{5,9},{9,13},{2,6},{6,10},{10,14},{3,7},{... | collective-permute-start | bytes 36872 | tf_op jit(solution)/shard_map/ppermute | solution.py:428
  78.8 3.4 %collective-permute-start.31 = (bf16[16,384]{1,0:T(8,128)(2,1)S(1)}, bf16[16,384]{1,0:T(8,128)(2,1)S(1)}, u32[]{:S(2)}, u32[]{:S(2)}) collective-permute-start(bf16[16,384]{1,0:T(8,128)(2,1)S(1)} %get-tuple-element.47), channel_id=1, source_target_pairs={{4,0},{8,4},{12,8},{5,1},{9,5},{13,9},{6,2},{10,6},{14,10},{7,3},{... | collective-permute-start | bytes 36872 | tf_op jit(solution)/shard_map/ppermute | solution.py:429
  82.1 1.0 collective-permute-start
  83.1 0.4 collective-permute-start.1
  83.5 1.2 collective-permute-start.19
  84.7 1.1 collective-permute-start.20
  85.8 2.7 %copy-done.4 = bf16[1536,5,384]{2,0,1:T(8,128)(2,1)S(1)} copy-done((bf16[1536,5,384]{2,0,1:T(8,128)(2,1)S(1)}, bf16[1536,5,384]{2,0,1:T(8,128)(2,1)}, u32[]{:S(2)}) %copy-start.4) | copy-done | bytes 5898264
  88.5 5.9 %dx.1 = (f32[384,384]{1,0:T(8,128)S(1)}, bf16[384,384]{1,0:T(8,128)(2,1)S(1)}, bf16[384,384]{1,0:T(8,128)(2,1)S(1)}, bf16[384,384]{1,0:T(8,128)(2,1)S(1)}) custom-call(bf16[384,384]{1,0:T(8,128)(2,1)S(1)} %get-tuple-element.44.refs_1_.refs_0_, bf16[16,384]{1,0:T(8,128)(2,1)S(1)} %collective-permute-done.30.refs_1_, ...), custom_call_target="tpu_custom_call" | custom-call | flops 2264924160 | bytes 5898240 | tf_op jit(solution)/shard_map/dx/pallas_call | solution.py:29
  94.4 1.2 collective-permute-start.32
  95.7 1.1 collective-permute-start.2
  96.7 3.4 %collective-permute-done.2.refs_3_ = bf16[64,768]{1,0:T(8,128)(2,1)S(1)} collective-permute-done((bf16[64,768]{1,0:T(8,128)(2,1)S(1)}, bf16[64,768]{1,0:T(8,128)(2,1)S(1)}, u32[]{:S(2)}, u32[]{:S(2)}) %collective-permute-start.2) | collective-permute-done | bytes 98336 | tf_op jit(solution)/shard_map/ppermute | solution.py:306
  100.2 1.2 projection.1
  101.5 1.1 collective-permute-start.22
  102.6 0.9 collective-permute-start.23
  103.5 1.1 collective-permute-start.33
  104.6 0.4 collective-permute-start.34
  105.0 0.5 collective-permute-done.22
  105.5 0.3 collective-permute-start.27
  105.8 2.8 %collective-permute-done.23 = bf16[64,768]{1,0:T(8,128)(2,1)S(1)} collective-permute-done((bf16[64,768]{1,0:T(8,128)(2,1)S(1)}, bf16[64,768]{1,0:T(8,128)(2,1)S(1)}, u32[]{:S(2)}, u32[]{:S(2)}) %collective-permute-start.23) | collective-permute-done | bytes 98336 | tf_op jit(solution)/shard_map/ppermute | solution.py:469
  108.6 1.5 %collective-permute-start.28 = (bf16[384,384]{1,0:T(8,128)(2,1)S(1)}, bf16[384,384]{1,0:T(8,128)(2,1)S(1)}, u32[]{:S(2)}, u32[]{:S(2)}) collective-permute-start(bf16[384,384]{1,0:T(8,128)(2,1)S(1)} %get-tuple-element.44.refs_1_.refs_0_), channel_id=1, source_target_pairs={{0,8},{4,12},{8,0},{12,4},{1,9},{5,13},{9,1},{13,5},{2,10},{6,14},... | collective-permute-start | bytes 884744 | tf_op jit(solution)/shard_map/ppermute | solution.py:310
  110.1 0.7 add_convert_fusion.1
  110.8 3.4 %collective-permute-done.33 = bf16[384,384]{1,0:T(8,128)(2,1)S(1)} collective-permute-done((bf16[384,384]{1,0:T(8,128)(2,1)S(1)}, bf16[384,384]{1,0:T(8,128)(2,1)S(1)}, u32[]{:S(2)}, u32[]{:S(2)}) %collective-permute-start.33) | collective-permute-done | bytes 294944 | tf_op jit(solution)/shard_map/ppermute | solution.py:450
  114.3 6.8 %collective-permute-done.34 = bf16[384,384]{1,0:T(8,128)(2,1)S(1)} collective-permute-done((bf16[384,384]{1,0:T(8,128)(2,1)S(1)}, bf16[384,384]{1,0:T(8,128)(2,1)S(1)}, u32[]{:S(2)}, u32[]{:S(2)}) %collective-permute-start.34) | collective-permute-done | bytes 294944 | tf_op jit(solution)/shard_map/ppermute | solution.py:450
  121.1 0.9 add_convert_fusion
  122.0 1.3 copy-done.1
  123.2 0.5 turn_x.1.refs_0_
  123.7 6.0 %collective-permute-done.28.refs_3_ = bf16[384,384]{1,0:T(8,128)(2,1)S(1)} collective-permute-done((bf16[384,384]{1,0:T(8,128)(2,1)S(1)}, bf16[384,384]{1,0:T(8,128)(2,1)S(1)}, u32[]{:S(2)}, u32[]{:S(2)}) %collective-permute-start.28) | collective-permute-done | bytes 294944 | tf_op jit(solution)/shard_map/ppermute | solution.py:310
  129.7 5.4 %collective-permute-done.29.refs_4_ = bf16[384,384]{1,0:T(8,128)(2,1)S(1)} collective-permute-done((bf16[384,384]{1,0:T(8,128)(2,1)S(1)}, bf16[384,384]{1,0:T(8,128)(2,1)S(1)}, u32[]{:S(2)}, u32[]{:S(2)}) %collective-permute-start.29) | collective-permute-done | bytes 294944 | tf_op jit(solution)/shard_map/ppermute | solution.py:310
  135.1 5.2 %dw.1 = f32[5,384,384]{2,1,0:T(8,128)} custom-call(bf16[384,1536]{1,0:T(8,128)(2,1)S(1)} %turn_x.1.refs_0_, bf16[384,384]{1,0:T(8,128)(2,1)S(1)} %get-tuple-element.44.refs_1_.refs_0_, bf16[384,384]{1,0:T(8,128)(2,1)S(1)} %collective-permute-done.27.refs_2_, bf16[384,384]{1,0:T(8,128)(2,1)S(1)} %collective-permute-done.28.refs_3_, ...), custom_call_target="tpu_custom_call" | custom-call | flops 2264924160 | bytes 2949120 | tf_op jit(solution)/shard_map/dw/pallas_call | solution.py:29
  (41 shorter events, 1.0 us)
Async XLA Ops:
  7.2 44.7 %copy-start = (bf16[1024,384]{1,0:T(8,128)(2,1)S(1)}, bf16[1024,384]{1,0:T(8,128)(2,1)}, u32[]{:S(2)}) copy-start(bf16[1024,384]{1,0:T(8,128)(2,1)} %refs_8_.1) | copy-start | bytes 2359300
  7.2 114.8 %all-gather.3.cloned.1.call-start = ((), (), s32[]{:S(2)}) async-start(), calls=%async_computation | async-start | bytes 1474560 | tf_op jit(solution)/shard_map/all_gather | solution.py:408
  7.2 1.1 copy-start.5
  8.3 0.7 copy-start.6
  8.9 0.7 copy-start.7
  10.8 8.0 %collective-permute-start.3 = (bf16[208,384]{1,0:T(8,128)(2,1)S(1)}, bf16[208,384]{1,0:T(8,128)(2,1)S(1)}, u32[]{:S(2)}, u32[]{:S(2)}) collective-permute-start(bf16[208,384]{1,0:T(8,128)(2,1)S(1)} %get-tuple-element.29), channel_id=1, source_target_pairs={{0,4},{4,8},{8,12},{12,0},{1,5},{5,9},{9,13},{13,1},{2,6},{6,10},{... | collective-permute-start | bytes 479240 | tf_op jit(solution)/shard_map/ppermute | solution.py:310
  12.1 14.4 %collective-permute-start.4 = (bf16[208,384]{1,0:T(8,128)(2,1)S(1)}, bf16[208,384]{1,0:T(8,128)(2,1)S(1)}, u32[]{:S(2)}, u32[]{:S(2)}) collective-permute-start(bf16[208,384]{1,0:T(8,128)(2,1)S(1)} %get-tuple-element.30), channel_id=1, source_target_pairs={{0,8},{4,12},{8,0},{12,4},{1,9},{5,13},{9,1},{13,5},{2,10},{6,14},... | collective-permute-start | bytes 479240 | tf_op jit(solution)/shard_map/ppermute | solution.py:310
  13.2 16.2 %collective-permute-start.5 = (bf16[208,384]{1,0:T(8,128)(2,1)S(1)}, bf16[208,384]{1,0:T(8,128)(2,1)S(1)}, u32[]{:S(2)}, u32[]{:S(2)}) collective-permute-start(bf16[208,384]{1,0:T(8,128)(2,1)S(1)} %get-tuple-element.31), channel_id=1, source_target_pairs={{0,12},{4,0},{8,4},{12,8},{1,13},{5,1},{9,5},{13,9},{2,14},{6,2},{... | collective-permute-start | bytes 479240 | tf_op jit(solution)/shard_map/ppermute | solution.py:310
  15.6 16.3 %collective-permute-start.9 = (bf16[64,192]{1,0:T(8,128)(2,1)S(1)}, bf16[64,192]{1,0:T(8,128)(2,1)S(1)}, u32[]{:S(2)}, u32[]{:S(2)}) collective-permute-start(bf16[64,192]{1,0:T(8,128)(2,1)S(1)} %get-tuple-element.54), channel_id=1, source_target_pairs={{0,4},{4,8},{8,12},{12,0},{1,5},{5,9},{9,13},{13,1},{2,6},{6,10},{... | collective-permute-start | bytes 73736 | tf_op jit(solution)/shard_map/ppermute | solution.py:310
  15.7 16.7 %collective-permute-start.10 = (bf16[64,192]{1,0:T(8,128)(2,1)S(1)}, bf16[64,192]{1,0:T(8,128)(2,1)S(1)}, u32[]{:S(2)}, u32[]{:S(2)}) collective-permute-start(bf16[64,192]{1,0:T(8,128)(2,1)S(1)} %get-tuple-element.53), channel_id=1, source_target_pairs={{0,8},{4,12},{8,0},{12,4},{1,9},{5,13},{9,1},{13,5},{2,10},{6,14},... | collective-permute-start | bytes 73736 | tf_op jit(solution)/shard_map/ppermute | solution.py:310
  18.8 13.6 %collective-permute-start.11 = (bf16[64,192]{1,0:T(8,128)(2,1)S(1)}, bf16[64,192]{1,0:T(8,128)(2,1)S(1)}, u32[]{:S(2)}, u32[]{:S(2)}) collective-permute-start(bf16[64,192]{1,0:T(8,128)(2,1)S(1)} %get-tuple-element.55), channel_id=1, source_target_pairs={{0,12},{4,0},{8,4},{12,8},{1,13},{5,1},{9,5},{13,9},{2,14},{6,2},{... | collective-permute-start | bytes 73736 | tf_op jit(solution)/shard_map/ppermute | solution.py:310
  30.0 22.4 %collective-permute-start.6 = (bf16[400,384]{1,0:T(8,128)(2,1)S(1)}, bf16[400,384]{1,0:T(8,128)(2,1)S(1)}, u32[]{:S(2)}, u32[]{:S(2)}) collective-permute-start(bf16[400,384]{1,0:T(8,128)(2,1)S(1)} %unpack.1.refs_0_), channel_id=1, source_target_pairs={{0,1},{1,0},{2,3},{3,2},{4,5},{5,4},{6,7},{7,6},{8,9},{9,8},{10,11... | collective-permute-start | bytes 921608 | tf_op jit(solution)/shard_map/ppermute | solution.py:306
  30.7 21.7 %collective-permute-start.7 = (bf16[400,384]{1,0:T(8,128)(2,1)S(1)}, bf16[400,384]{1,0:T(8,128)(2,1)S(1)}, u32[]{:S(2)}, u32[]{:S(2)}) collective-permute-start(bf16[400,384]{1,0:T(8,128)(2,1)S(1)} %unpack.1.refs_0_), channel_id=1, source_target_pairs={{0,2},{1,3},{2,0},{3,1},{4,6},{5,7},{6,4},{7,5},{8,10},{9,11},{10,... | collective-permute-start | bytes 921608 | tf_op jit(solution)/shard_map/ppermute | solution.py:306
  31.9 20.5 %collective-permute-start.8 = (bf16[400,384]{1,0:T(8,128)(2,1)S(1)}, bf16[400,384]{1,0:T(8,128)(2,1)S(1)}, u32[]{:S(2)}, u32[]{:S(2)}) collective-permute-start(bf16[400,384]{1,0:T(8,128)(2,1)S(1)} %unpack.1.refs_0_), channel_id=1, source_target_pairs={{0,3},{1,2},{2,1},{3,0},{4,7},{5,6},{6,5},{7,4},{8,11},{9,10},{10,... | collective-permute-start | bytes 921608 | tf_op jit(solution)/shard_map/ppermute | solution.py:306
  32.4 1.4 collective-permute-start.12
  32.7 16.3 %collective-permute-start.13 = (bf16[4,64,192]{2,1,0:T(8,128)(2,1)S(1)}, bf16[4,64,192]{2,1,0:T(8,128)(2,1)S(1)}, u32[]{:S(2)}, u32[]{:S(2)}) collective-permute-start(bf16[4,64,192]{2,1,0:T(8,128)(2,1)S(1)} %pad_maximum_fusion.1.refs_0_), channel_id=1, source_target_pairs={{0,2},{1,3},{2,0},{3,1},{4,6},{5,7},{6,4},{7,5},{8,10},{9,11},{10,... | collective-permute-start | bytes 294920 | tf_op jit(solution)/shard_map/ppermute | solution.py:306
  33.9 18.0 %collective-permute-start.14 = (bf16[4,64,192]{2,1,0:T(8,128)(2,1)S(1)}, bf16[4,64,192]{2,1,0:T(8,128)(2,1)S(1)}, u32[]{:S(2)}, u32[]{:S(2)}) collective-permute-start(bf16[4,64,192]{2,1,0:T(8,128)(2,1)S(1)} %pad_maximum_fusion.1.refs_0_), channel_id=1, source_target_pairs={{0,3},{1,2},{2,1},{3,0},{4,7},{5,6},{6,5},{7,4},{8,11},{9,10},{10,... | collective-permute-start | bytes 294920 | tf_op jit(solution)/shard_map/ppermute | solution.py:306
  52.4 2.7 %copy-start.3 = (bf16[1536,5,384]{2,0,1:T(8,128)(2,1)S(1)}, bf16[1536,5,384]{2,0,1:T(8,128)(2,1)}, u32[]{:S(2)}) copy-start(bf16[1536,5,384]{2,0,1:T(8,128)(2,1)} %param.11) | copy-start | bytes 17694724
  55.1 27.0 %copy-start.2 = (bf16[64,768]{1,0:T(8,128)(2,1)S(1)}, bf16[64,768]{1,0:T(8,128)(2,1)}, u32[]{:S(2)}) copy-start(bf16[64,768]{1,0:T(8,128)(2,1)} %refs_0_.1) | copy-start | bytes 294916
  61.1 3.7 %collective-permute-start.24 = (bf16[96,384]{1,0:T(8,128)(2,1)S(1)}, bf16[96,384]{1,0:T(8,128)(2,1)S(1)}, u32[]{:S(2)}, u32[]{:S(2)}) collective-permute-start(bf16[96,384]{1,0:T(8,128)(2,1)S(1)} %get-tuple-element.41), channel_id=1, source_target_pairs={{0,4},{4,8},{8,12},{12,0},{1,5},{5,9},{9,13},{13,1},{2,6},{6,10},{... | collective-permute-start | bytes 221192 | tf_op jit(solution)/shard_map/ppermute | solution.py:310
  61.2 6.0 %collective-permute-start.25 = (bf16[96,384]{1,0:T(8,128)(2,1)S(1)}, bf16[96,384]{1,0:T(8,128)(2,1)S(1)}, u32[]{:S(2)}, u32[]{:S(2)}) collective-permute-start(bf16[96,384]{1,0:T(8,128)(2,1)S(1)} %get-tuple-element.42), channel_id=1, source_target_pairs={{0,8},{4,12},{8,0},{12,4},{1,9},{5,13},{9,1},{13,5},{2,10},{6,14},... | collective-permute-start | bytes 221192 | tf_op jit(solution)/shard_map/ppermute | solution.py:310
  63.2 7.4 %collective-permute-start.26 = (bf16[96,384]{1,0:T(8,128)(2,1)S(1)}, bf16[96,384]{1,0:T(8,128)(2,1)S(1)}, u32[]{:S(2)}, u32[]{:S(2)}) collective-permute-start(bf16[96,384]{1,0:T(8,128)(2,1)S(1)} %get-tuple-element.43), channel_id=1, source_target_pairs={{0,12},{4,0},{8,4},{12,8},{1,13},{5,1},{9,5},{13,9},{2,14},{6,2},{... | collective-permute-start | bytes 221192 | tf_op jit(solution)/shard_map/ppermute | solution.py:310
  71.4 2.3 %collective-permute-start.15 = (f32[8,256]{1,0:T(8,128)S(1)}, f32[8,256]{1,0:T(8,128)S(1)}, u32[]{:S(2)}, u32[]{:S(2)}) collective-permute-start(f32[8,256]{1,0:T(8,128)S(1)} %get-tuple-element.32.refs_0_), channel_id=1, source_target_pairs={{0,1},{1,0},{2,3},{3,2},{4,5},{5,4},{6,7},{7,6},{8,9},{9,8},{10,11... | collective-permute-start | bytes 24584 | tf_op jit(solution)/shard_map/ppermute | solution.py:306
  72.0 2.5 %collective-permute-start.16 = (f32[8,256]{1,0:T(8,128)S(1)}, f32[8,256]{1,0:T(8,128)S(1)}, u32[]{:S(2)}, u32[]{:S(2)}) collective-permute-start(f32[8,256]{1,0:T(8,128)S(1)} %get-tuple-element.32.refs_0_), channel_id=1, source_target_pairs={{0,2},{1,3},{2,0},{3,1},{4,6},{5,7},{6,4},{7,5},{8,10},{9,11},{10,... | collective-permute-start | bytes 24584 | tf_op jit(solution)/shard_map/ppermute | solution.py:306
  73.2 3.1 %collective-permute-start.17 = (f32[8,256]{1,0:T(8,128)S(1)}, f32[8,256]{1,0:T(8,128)S(1)}, u32[]{:S(2)}, u32[]{:S(2)}) collective-permute-start(f32[8,256]{1,0:T(8,128)S(1)} %get-tuple-element.32.refs_0_), channel_id=1, source_target_pairs={{0,3},{1,2},{2,1},{3,0},{4,7},{5,6},{6,5},{7,4},{8,11},{9,10},{10,... | collective-permute-start | bytes 24584 | tf_op jit(solution)/shard_map/ppermute | solution.py:306
  76.8 6.7 %collective-permute-start.30 = (bf16[16,384]{1,0:T(8,128)(2,1)S(1)}, bf16[16,384]{1,0:T(8,128)(2,1)S(1)}, u32[]{:S(2)}, u32[]{:S(2)}) collective-permute-start(bf16[16,384]{1,0:T(8,128)(2,1)S(1)} %get-tuple-element.46), channel_id=1, source_target_pairs={{0,4},{4,8},{8,12},{1,5},{5,9},{9,13},{2,6},{6,10},{10,14},{3,7},{... | collective-permute-start | bytes 36872 | tf_op jit(solution)/shard_map/ppermute | solution.py:428
  78.8 5.9 %collective-permute-start.31 = (bf16[16,384]{1,0:T(8,128)(2,1)S(1)}, bf16[16,384]{1,0:T(8,128)(2,1)S(1)}, u32[]{:S(2)}, u32[]{:S(2)}) collective-permute-start(bf16[16,384]{1,0:T(8,128)(2,1)S(1)} %get-tuple-element.47), channel_id=1, source_target_pairs={{4,0},{8,4},{12,8},{5,1},{9,5},{13,9},{6,2},{10,6},{14,10},{7,3},{... | collective-permute-start | bytes 36872 | tf_op jit(solution)/shard_map/ppermute | solution.py:429
  82.1 12.3 %collective-permute-start = (bf16[64,768]{1,0:T(8,128)(2,1)S(1)}, bf16[64,768]{1,0:T(8,128)(2,1)S(1)}, u32[]{:S(2)}, u32[]{:S(2)}) collective-permute-start(bf16[64,768]{1,0:T(8,128)(2,1)S(1)} %copy-done.2), channel_id=1, source_target_pairs={{0,1},{1,0},{2,3},{3,2},{4,5},{5,4},{6,7},{7,6},{8,9},{9,8},{10,11... | collective-permute-start | bytes 294920 | tf_op jit(solution)/shard_map/ppermute | solution.py:306
  83.1 12.6 %collective-permute-start.1 = (bf16[64,768]{1,0:T(8,128)(2,1)S(1)}, bf16[64,768]{1,0:T(8,128)(2,1)S(1)}, u32[]{:S(2)}, u32[]{:S(2)}) collective-permute-start(bf16[64,768]{1,0:T(8,128)(2,1)S(1)} %copy-done.2), channel_id=1, source_target_pairs={{0,2},{1,3},{2,0},{3,1},{4,6},{5,7},{6,4},{7,5},{8,10},{9,11},{10,... | collective-permute-start | bytes 294920 | tf_op jit(solution)/shard_map/ppermute | solution.py:306
  83.5 16.7 %collective-permute-start.18 = (bf16[192,384]{1,0:T(8,128)(2,1)S(1)}, bf16[192,384]{1,0:T(8,128)(2,1)S(1)}, u32[]{:S(2)}, u32[]{:S(2)}) collective-permute-start(bf16[192,384]{1,0:T(8,128)(2,1)S(1)} %get-tuple-element.35.refs_4_), channel_id=1, source_target_pairs={{0,4},{4,8},{8,12},{12,0},{1,5},{5,9},{9,13},{13,1},{2,6},{6,10},{... | collective-permute-start | bytes 442376 | tf_op jit(solution)/shard_map/ppermute | solution.py:310
  83.5 16.7 %collective-permute-start.19 = (bf16[192,384]{1,0:T(8,128)(2,1)S(1)}, bf16[192,384]{1,0:T(8,128)(2,1)S(1)}, u32[]{:S(2)}, u32[]{:S(2)}) collective-permute-start(bf16[192,384]{1,0:T(8,128)(2,1)S(1)} %get-tuple-element.35.refs_4_), channel_id=1, source_target_pairs={{0,8},{4,12},{8,0},{12,4},{1,9},{5,13},{9,1},{13,5},{2,10},{6,14},... | collective-permute-start | bytes 442376 | tf_op jit(solution)/shard_map/ppermute | solution.py:310
  84.7 15.5 %collective-permute-start.20 = (bf16[192,384]{1,0:T(8,128)(2,1)S(1)}, bf16[192,384]{1,0:T(8,128)(2,1)S(1)}, u32[]{:S(2)}, u32[]{:S(2)}) collective-permute-start(bf16[192,384]{1,0:T(8,128)(2,1)S(1)} %get-tuple-element.35.refs_4_), channel_id=1, source_target_pairs={{0,12},{4,0},{8,4},{12,8},{1,13},{5,1},{9,5},{13,9},{2,14},{6,2},{... | collective-permute-start | bytes 442376 | tf_op jit(solution)/shard_map/ppermute | solution.py:310
  85.8 2.7 %copy-start.4 = (bf16[1536,5,384]{2,0,1:T(8,128)(2,1)S(1)}, bf16[1536,5,384]{2,0,1:T(8,128)(2,1)}, u32[]{:S(2)}) copy-start(bf16[1536,5,384]{2,0,1:T(8,128)(2,1)} %param.11) | copy-start | bytes 17694724
  94.4 15.7 %collective-permute-start.32 = (bf16[384,384]{1,0:T(8,128)(2,1)S(1)}, bf16[384,384]{1,0:T(8,128)(2,1)S(1)}, u32[]{:S(2)}, u32[]{:S(2)}) collective-permute-start(bf16[384,384]{1,0:T(8,128)(2,1)S(1)} %get-tuple-element.49), channel_id=1, source_target_pairs={{0,1},{1,0},{2,3},{3,2},{4,5},{5,4},{6,7},{7,6},{8,9},{9,8},{10,11... | collective-permute-start | bytes 884744 | tf_op jit(solution)/shard_map/ppermute | solution.py:450
  95.7 4.5 %collective-permute-start.2 = (bf16[64,768]{1,0:T(8,128)(2,1)S(1)}, bf16[64,768]{1,0:T(8,128)(2,1)S(1)}, u32[]{:S(2)}, u32[]{:S(2)}) collective-permute-start(bf16[64,768]{1,0:T(8,128)(2,1)S(1)} %copy-done.2), channel_id=1, source_target_pairs={{0,3},{1,2},{2,1},{3,0},{4,7},{5,6},{6,5},{7,4},{8,11},{9,10},{10,... | collective-permute-start | bytes 294920 | tf_op jit(solution)/shard_map/ppermute | solution.py:306
  101.4 3.2 %collective-permute-start.21 = (bf16[64,768]{1,0:T(8,128)(2,1)S(1)}, bf16[64,768]{1,0:T(8,128)(2,1)S(1)}, u32[]{:S(2)}, u32[]{:S(2)}) collective-permute-start(bf16[64,768]{1,0:T(8,128)(2,1)S(1)} %get-tuple-element.37), channel_id=1, source_target_pairs={{0,1},{1,0},{2,3},{3,2},{4,5},{5,4},{6,7},{7,6},{8,9},{9,8},{10,11... | collective-permute-start | bytes 294920 | tf_op jit(solution)/shard_map/ppermute | solution.py:469
  101.5 4.0 %collective-permute-start.22 = (bf16[64,768]{1,0:T(8,128)(2,1)S(1)}, bf16[64,768]{1,0:T(8,128)(2,1)S(1)}, u32[]{:S(2)}, u32[]{:S(2)}) collective-permute-start(bf16[64,768]{1,0:T(8,128)(2,1)S(1)} %get-tuple-element.38), channel_id=1, source_target_pairs={{0,2},{1,3},{2,0},{3,1},{4,6},{5,7},{6,4},{7,5},{8,10},{9,11},{10,... | collective-permute-start | bytes 294920 | tf_op jit(solution)/shard_map/ppermute | solution.py:469
  102.6 6.0 %collective-permute-start.23 = (bf16[64,768]{1,0:T(8,128)(2,1)S(1)}, bf16[64,768]{1,0:T(8,128)(2,1)S(1)}, u32[]{:S(2)}, u32[]{:S(2)}) collective-permute-start(bf16[64,768]{1,0:T(8,128)(2,1)S(1)} %get-tuple-element.39), channel_id=1, source_target_pairs={{0,3},{1,2},{2,1},{3,0},{4,7},{5,6},{6,5},{7,4},{8,11},{9,10},{10,... | collective-permute-start | bytes 294920 | tf_op jit(solution)/shard_map/ppermute | solution.py:469
  103.5 10.7 %collective-permute-start.33 = (bf16[384,384]{1,0:T(8,128)(2,1)S(1)}, bf16[384,384]{1,0:T(8,128)(2,1)S(1)}, u32[]{:S(2)}, u32[]{:S(2)}) collective-permute-start(bf16[384,384]{1,0:T(8,128)(2,1)S(1)} %get-tuple-element.50), channel_id=1, source_target_pairs={{0,2},{1,3},{2,0},{3,1},{4,6},{5,7},{6,4},{7,5},{8,10},{9,11},{10,... | collective-permute-start | bytes 884744 | tf_op jit(solution)/shard_map/ppermute | solution.py:450
  104.6 16.4 %collective-permute-start.34 = (bf16[384,384]{1,0:T(8,128)(2,1)S(1)}, bf16[384,384]{1,0:T(8,128)(2,1)S(1)}, u32[]{:S(2)}, u32[]{:S(2)}) collective-permute-start(bf16[384,384]{1,0:T(8,128)(2,1)S(1)} %get-tuple-element.51), channel_id=1, source_target_pairs={{0,3},{1,2},{2,1},{3,0},{4,7},{5,6},{6,5},{7,4},{8,11},{9,10},{10,... | collective-permute-start | bytes 884744 | tf_op jit(solution)/shard_map/ppermute | solution.py:450
  105.5 18.2 %collective-permute-start.27 = (bf16[384,384]{1,0:T(8,128)(2,1)S(1)}, bf16[384,384]{1,0:T(8,128)(2,1)S(1)}, u32[]{:S(2)}, u32[]{:S(2)}) collective-permute-start(bf16[384,384]{1,0:T(8,128)(2,1)S(1)} %get-tuple-element.44.refs_1_.refs_0_), channel_id=1, source_target_pairs={{0,4},{4,8},{8,12},{12,0},{1,5},{5,9},{9,13},{13,1},{2,6},{6,10},{... | collective-permute-start | bytes 884744 | tf_op jit(solution)/shard_map/ppermute | solution.py:310
  108.6 21.0 %collective-permute-start.28 = (bf16[384,384]{1,0:T(8,128)(2,1)S(1)}, bf16[384,384]{1,0:T(8,128)(2,1)S(1)}, u32[]{:S(2)}, u32[]{:S(2)}) collective-permute-start(bf16[384,384]{1,0:T(8,128)(2,1)S(1)} %get-tuple-element.44.refs_1_.refs_0_), channel_id=1, source_target_pairs={{0,8},{4,12},{8,0},{12,4},{1,9},{5,13},{9,1},{13,5},{2,10},{6,14},... | collective-permute-start | bytes 884744 | tf_op jit(solution)/shard_map/ppermute | solution.py:310
  110.1 24.9 %collective-permute-start.29 = (bf16[384,384]{1,0:T(8,128)(2,1)S(1)}, bf16[384,384]{1,0:T(8,128)(2,1)S(1)}, u32[]{:S(2)}, u32[]{:S(2)}) collective-permute-start(bf16[384,384]{1,0:T(8,128)(2,1)S(1)} %get-tuple-element.44.refs_1_.refs_0_), channel_id=1, source_target_pairs={{0,12},{4,0},{8,4},{12,8},{1,13},{5,1},{9,5},{13,9},{2,14},{6,2},{... | collective-permute-start | bytes 884744 | tf_op jit(solution)/shard_map/ppermute | solution.py:310
  122.0 1.3 copy-start.1
Sparse Core Ops, SparseCore 0:
  71.5 19.2 all-gather.2

commit v3 on v1

--- a/solution.py
+++ b/solution.py
@@ -1,11 +1,365 @@
+import functools
+
 import jax
 import jax.numpy as jnp
 from jax import lax
+from jax.experimental import pallas as pl
+from jax.experimental.pallas import tpu as pltpu
 from jax.sharding import PartitionSpec as P
 
 KERNEL_TAPS = 5
 DILATION_STEP = 2
 CAP = 2
+EDGE = 2 * DILATION_STEP
+BF = jnp.bfloat16
+F32 = jnp.float32
+ROOT = 0.7978845608028654
+CUBE = 0.044715
+
+VMEM = pl.BlockSpec(memory_space=pltpu.VMEM)
+SMEM = pl.BlockSpec(memory_space=pltpu.SMEM)
+HBM = pl.BlockSpec(memory_space=pltpu.HBM)
+
+
+def struct(shape, dtype):
+    return jax.ShapeDtypeStruct(shape, dtype)
+
+
+def launch(body, outs, ins, specs=None, scratch=(), flops=0, moved=0, room=8, name=None):
+    return pl.pallas_call(
+        body,
+        out_shape=outs,
+        in_specs=specs or [VMEM] * len(ins),
+        out_specs=jax.tree.map(lambda _: VMEM, outs),
+        scratch_shapes=list(scratch),
+        compiler_params=pltpu.CompilerParams(vmem_limit_bytes=room * 1024 * 1024),
+        cost_estimate=pl.CostEstimate(flops=flops, bytes_accessed=moved, transcendentals=0),
+        name=name,
+    )(*ins)
+
+
+def dot(a, b, dims=((1,), (0,))):
+    return lax.dot_general(a, b, (dims, ((), ())), preferred_element_type=F32)
+
+
+def wrap(value, count):
+    return lax.rem(value + count, count)
+
+
+def pack_kernel(slabs, rows, block_len, dest_hbm, kept_hbm, x_hbm, cot_ref, *refs):
+    outs, (dest_ref, kept_ref, x_ref, parts, sems) = refs[:slabs], refs[slabs:]
+    copies = [
+        pltpu.make_async_copy(a, b, sems.at[n])
+        for n, (a, b) in enumerate(((dest_hbm, dest_ref), (kept_hbm, kept_ref), (x_hbm, x_ref)))
+    ]
+    for copy in copies:
+        copy.start()
+    copies[0].wait()
+    copies[1].wait()
+    me = lax.axis_index("seq")
+    payload = CAP * block_len + 16
+    feat, count = parts.shape[1:]
+    for d in range(slabs):
+        parts[d] = cot_ref[:, d * count : (d + 1) * count]
+    dest = [jnp.where(dest_ref[r] >= slabs, -100, dest_ref[r]) for r in range(rows)]
+    rank, total = [], []
+    for r in range(rows):
+        before, count = jnp.int32(0), jnp.int32(0)
+        for q in range(rows):
+            same = (dest[q] == dest[r]).astype(jnp.int32)
+            count = count + same
+            if q < r:
+                before = before + same
+        rank.append(before)
+        total.append(count)
+    columns = rows * block_len
+    col = lax.broadcasted_iota(jnp.int32, (1, columns), 1)
+    dest_v = jnp.full((1, columns), -100, jnp.int32)
+    rank_v = jnp.zeros((1, columns), jnp.int32)
+    last_v = jnp.zeros((1, columns), jnp.int32)
+    place = jnp.zeros((1, columns), jnp.int32)
+    for r in range(rows):
+        offset = col - r * block_len
+        here = (offset >= 0) & (offset < kept_ref[r]) & (offset < block_len)
+        dest_v = jnp.where(here, dest[r], dest_v)
+        rank_v = jnp.where(here, rank[r], rank_v)
+        last_v = jnp.where(here, (rank[r] == total[r] - 1).astype(jnp.int32), last_v)
+        place = jnp.where(here, offset, place)
+    row = lax.broadcasted_iota(jnp.int32, (payload, columns), 0)
+    line = lax.broadcasted_iota(jnp.int32, (payload, 1), 0)
+    base = CAP * block_len
+    copies[2].wait()
+    x = x_ref[...]
+    for k, out in enumerate(outs):
+        to = wrap(me + k, slabs)
+        key = jnp.where(dest_v == to, rank_v * block_len + place, -1)
+        key = jnp.where((dest_v == to + 1) & (rank_v == 0) & (place < EDGE), base + place, key)
+        tail = place - (block_len - EDGE)
+        key = jnp.where((dest_v == to - 1) & (last_v == 1) & (tail >= 0), base + EDGE + tail, key)
+        picker = jnp.where(row == key, 1.0, 0.0).astype(BF)
+        rows_out = dot(picker, x)
+        for spot, slab in enumerate((to, to - 1, to + 1)):
+            number = jnp.int32(0)
+            for r in range(rows):
+                number = number + (dest[r] == slab).astype(jnp.int32)
+            rows_out = jnp.where(line == base + 2 * EDGE + spot, number.astype(F32), rows_out)
+        out[:payload] = rows_out.astype(BF)
+        piece = parts[to].astype(F32)
+        out[payload:] = jnp.concatenate([piece[: feat // 2], piece[feat // 2 :]], axis=1).astype(BF)
+
+
+def unpack_kernel(slabs, block_len, *refs):
+    ins, out, cot = refs[:slabs], refs[slabs], refs[slabs + 1]
+    me = lax.axis_index("seq")
+    payload = CAP * block_len + 16
+    base = CAP * block_len
+    length = slabs * block_len
+    heads = [r[payload - 16 : payload, :].astype(F32) for r in ins]
+    own = [h[2 * EDGE : 2 * EDGE + 1, :payload] for h in heads]
+    prev = [h[2 * EDGE + 1 : 2 * EDGE + 2, :payload] for h in heads]
+    following = [h[2 * EDGE + 2 : 2 * EDGE + 3, :payload] for h in heads]
+    source = [wrap(me - k, slabs) for k in range(slabs)]
+    col = lax.broadcasted_iota(jnp.int32, (1, payload), 1)
+    slot = jnp.where(col >= block_len, 1, 0)
+    place = (col - slot * block_len).astype(F32)
+    slot = slot.astype(F32)
+    colf = col.astype(F32)
+    row = lax.broadcasted_iota(jnp.int32, out.shape[:1] + (payload,), 0).astype(F32)
+    total = jnp.zeros(out.shape, F32)
+    for k in range(slabs):
+        offsets = []
+        for counts in (own, prev, following):
+            ahead = jnp.zeros((1, payload), F32)
+            for q in range(slabs):
+                if q != k:
+                    ahead = ahead + jnp.where(source[q] < source[k], counts[q], 0.0)
+            offsets.append(ahead)
+        main = jnp.where(slot < own[k], (offsets[0] + slot) * block_len + place, -1.0)
+        right = jnp.where((following[k] > 0.5) & (offsets[2] < 0.5), length + EDGE + colf - base, -1.0)
+        left = jnp.where((prev[k] > 0.5) & (offsets[1] + prev[k] > slabs - 0.5), length + colf - base - EDGE, -1.0)
+        key = jnp.where(col < base, main, jnp.where(col < base + EDGE, right, jnp.where(col < base + 2 * EDGE, left, -1.0)))
+        total = total + dot(jnp.where(row == key, 1.0, 0.0).astype(BF), ins[k][:payload])
+        half, count = cot.shape[1] // 2, cot.shape[2]
+        piece = ins[k][payload:].astype(F32)
+        cot[k, :half] = piece[:, :count].astype(BF)
+        cot[k, half:] = piece[:, count:].astype(BF)
+    out[...] = total.astype(BF)
+
+
+def cot_kernel(slabs, chans, *refs):
+    ins, (w_ref, gain_ref, out, full) = refs[:chans], refs[chans:]
+    me, ch = lax.axis_index("seq"), lax.axis_index("chan")
+    feat = ins[0].shape[1]
+    for j in range(chans):
+        owner = lax.bitwise_xor(ch, j)
+        for k in range(slabs):
+            begin = pl.multiple_of((wrap(me - k, slabs) * chans + owner) * feat, 16)
+            full[pl.ds(begin, feat), :] = ins[j][k]
+    out[...] = dot(full[...], w_ref[...], ((0,), (0,))) * gain_ref[...][None, :]
+
+
+def stage_kernel(w_ref, out, sem):
+    copy = pltpu.make_async_copy(w_ref, out, sem)
+    copy.start()
+    copy.wait()
+
+
+def quarter_kernel(slabs, chans, *refs):
+    xs, pieces = refs[:chans], refs[chans:]
+    me, ch = lax.axis_index("seq"), lax.axis_index("chan")
+    width = xs[0].shape[1]
+    part = pieces[0].shape[0]
+    begin = pl.multiple_of(ch * part, 8)
+    for k, piece in enumerate(pieces):
+        for j in range(chans):
+
+            @pl.when(lax.bitwise_xor(ch, j) == wrap(me + k, slabs))
+            def _(piece=piece, j=j):
+                piece[...] = xs[j][pl.ds(begin, part), :]
+
+
+def conv_kernel(chans, *refs):
+    xs, (w_ref, bias_ref, pooled_ref, slope_ref), rest = refs[:chans], refs[chans : chans + 4], refs[chans + 4 :]
+    full, conv, shifted_sum, lanes = rest
+    ch = lax.axis_index("chan")
+    rows, width = xs[0].shape
+    length = shifted_sum.shape[0]
+    for j in range(chans):
+        begin = pl.multiple_of(lax.bitwise_xor(ch, j) * width, 128)
+        full[:, pl.ds(begin, width)] = xs[j][...]
+    x = full[...]
+    for t in range(KERNEL_TAPS):
+        product = dot(x, w_ref[t])
+        conv[0:EDGE] = product[length : length + EDGE]
+        conv[EDGE : EDGE + length] = product[:length]
+        conv[EDGE + length : 2 * EDGE + length] = product[length + EDGE : length + 2 * EDGE]
+        moved = conv[t * DILATION_STEP : t * DILATION_STEP + length]
+        if t == 0:
+            shifted_sum[...] = moved + bias_ref[...][None, :]
+        else:
+            shifted_sum[...] += moved
+    v = shifted_sum[...]
+    th = jnp.tanh(ROOT * (v + CUBE * (v * v * v)))
+    half = 0.5 * (1.0 + th)
+    slope_ref[...] = half + (0.5 * ROOT) * v * (1.0 - th * th) * (1.0 + (3.0 * CUBE) * (v * v))
+    act = v * half
+    count = length // 2
+    columns = []
+    for c in range(width // 128):
+        lanes[c] = act[:, c * 128 : (c + 1) * 128]
+        columns.append((lanes[c, pl.ds(0, count, stride=2), :] + lanes[c, pl.ds(1, count, stride=2), :]) * 0.5)
+    pooled = jnp.concatenate(columns, axis=1)
+    pooled_ref[...] = pooled
+
+
+def sums_kernel(pooled_ref, dxhat_ref, stats_ref):
+    pooled = pooled_ref[...]
+    count = pooled.shape[0]
+    dxhat = dxhat_ref[...]
+    sums = [
+        jnp.sum(pooled, axis=1, keepdims=True),
+        jnp.sum(pooled * pooled, axis=1, keepdims=True),
+        jnp.sum(dxhat, axis=1, keepdims=True),
+        jnp.sum(dxhat * pooled, axis=1, keepdims=True),
+    ]
+    lane = lax.broadcasted_iota(jnp.int32, (count, 128), 1)
+    table = jnp.zeros((count, 128), F32)
+    for n, s in enumerate(sums):
+        table = jnp.where(lane == n, s, table)
+    padded = stats_ref.shape[1]
+    if padded > count:
+        table = jnp.concatenate([table, jnp.zeros((padded - count, 128), F32)], axis=0)
+    stats_ref[...] = table.T[:8]
+
+
+def grad_kernel(chans, *refs):
+    stats, (pooled_ref, slope_ref, dxhat_ref, gain_ref, low_ref, high_ref, twice) = refs[:chans], refs[chans:]
+    count, width = pooled_ref.shape
+    total = stats[0][...]
+    for s in stats[1:]:
+        total = total + s[...]
+    total = total * (1.0 / (width * chans))
+    table = jnp.concatenate([total, jnp.zeros((120, total.shape[1]), F32)], axis=0).T[:count]
+    mean = table[:, 0:1]
+    rstd = lax.rsqrt(table[:, 1:2] - mean * mean + 1e-05)
+    leading = table[:, 2:3]
+    trailing = rstd * (table[:, 3:4] - mean * leading)
+    xhat = (pooled_ref[...] - mean) * rstd
+    low_ref[:count] = (xhat * gain_ref[...][None, :]).astype(BF)
+    half = (0.5 * rstd) * (dxhat_ref[...] - leading - xhat * trailing)
+    columns = []
+    for c in range(width // 128):
+        twice[c, pl.ds(0, count, stride=2), :] = half[:, c * 128 : (c + 1) * 128]
+        twice[c, pl.ds(1, count, stride=2), :] = half[:, c * 128 : (c + 1) * 128]
+        columns.append(twice[c])
+    dy = (jnp.concatenate(columns, axis=1) * slope_ref[...]).astype(BF)
+    extra = low_ref.shape[0] - count
+    low_ref[count:] = dy[:extra]
+    high_ref[...] = dy[extra:]
+
+
+def dx_kernel(picks, *refs):
+    n = len(picks)
+    (low_ref, high_ref, left_ref, right_ref, w_ref), outs, (wide, moved) = refs[:5], refs[5 : 5 + n], refs[5 + n :]
+    ch = lax.axis_index("chan")
+    width = low_ref.shape[1]
+    length = moved.shape[1]
+    upper = high_ref.shape[0]
+    begin = low_ref.shape[0] - (length - upper)
+    me = lax.axis_index("seq")
+    left = left_ref[upper - 16 : upper].astype(F32)[16 - EDGE :]
+    right = right_ref[begin : begin + 16].astype(F32)[:EDGE]
+    wide[0:EDGE] = jnp.where(me == 0, 0.0, left)
+    wide[EDGE : EDGE + length - upper] = low_ref[begin:].astype(F32)
+    wide[EDGE + length - upper : EDGE + length] = high_ref[...].astype(F32)
+    wide[EDGE + length : 2 * EDGE + length] = jnp.where(me == lax.axis_size("seq") - 1, 0.0, right)
+    for t in range(KERNEL_TAPS):
+        begin = 2 * EDGE - t * DILATION_STEP
+        moved[t] = wide[begin : begin + length].astype(BF)
+    for slot, j in enumerate(picks):
+        block = pl.ds(pl.multiple_of(lax.bitwise_xor(ch, j) * width, 16), width)
+        total = dot(w_ref[0, block, :], moved[0], ((1,), (1,)))
+        for t in range(1, KERNEL_TAPS):
+            total = total + dot(w_ref[t, block, :], moved[t], ((1,), (1,)))
+        outs[slot][...] = total.astype(outs[slot].dtype)
+
+
+def transpose_kernel(slabs, chans, x_ref, out, full):
+    me = lax.axis_index("seq")
+    part = x_ref.shape[2]
+    for j in range(chans):
+        for k in range(slabs):
+            begin = pl.multiple_of((wrap(me - k, slabs) * chans + j) * part, 8)
+            full[pl.ds(begin, part), :] = x_ref[j, k]
+    out[...] = full[...].T
+
+
+def dw_kernel(slabs, *refs):
+    xt_ref, dys, (out, full, moved) = refs[0], refs[1:-3], refs[-3:]
+    me = lax.axis_index("seq")
+    width = dys[0].shape[1]
+    every = xt_ref.shape[1]
+    length = every // slabs
+    full[0:8] = jnp.zeros((8, width), F32)
+    full[8 + every : 16 + every] = jnp.zeros((8, width), F32)
+    half = len(dys) // 2
+    upper = dys[half].shape[0]
+    extra = length - upper
+    lows = [r[dys[0].shape[0] - extra :] for r in dys[:half]]
+    highs = [r[...] for r in dys[half:]]
+    for k in range(slabs):
+        begin = pl.multiple_of(wrap(me - k, slabs) * length + 8, 8)
+        full[pl.ds(begin, extra), :] = lows[k].astype(F32)
+        full[pl.ds(begin + extra, upper), :] = highs[k].astype(F32)
+    xt = xt_ref[...]
+    for t in range(KERNEL_TAPS):
+        begin = 8 + EDGE - t * DILATION_STEP
+        moved[...] = full[begin : begin + every].astype(BF)
+        out[t] = dot(xt, moved[...])
+
+
+def proj_kernel(slabs, chans, *refs):
+    cots, normed, rest = refs[:chans], refs[chans : -(chans + 5)], refs[-(chans + 5) :]
+    (w_ref, dw_ref), outs, (wide, full, part) = rest[:2], rest[2 : 2 + chans], rest[2 + chans :]
+    me, ch = lax.axis_index("seq"), lax.axis_index("chan")
+    feat = cots[0].shape[0]
+    count = full.shape[0] // slabs
+    for j in range(chans):
+        wide[pl.ds(pl.multiple_of(lax.bitwise_xor(ch, j) * feat, 8), feat), :] = cots[j][...]
+    for k, rows in enumerate([r[:count] for r in normed]):
+        full[pl.ds(pl.multiple_of(wrap(me - k, slabs) * count, 8), count), :] = rows
+    every = full[...]
+    dw_ref[...] = dot(wide[...], every)
+    rows = feat * chans
+    part[...] = dot(w_ref[pl.ds(pl.multiple_of(me * rows, 8), rows), :], every, ((1,), (1,)))
+    for j in range(chans):
+        outs[j][...] = part[pl.ds(pl.multiple_of(lax.bitwise_xor(ch, j) * feat, 8), feat), :].astype(outs[j].dtype)
+
+
+def after(values, *earlier):
+    return lax.optimization_barrier((values, earlier))[0]
+
+
+def swaps(value, count):
+    return [value] + [lax.ppermute(value, "chan", [(i, i ^ j) for i in range(count)]) for j in range(1, count)]
+
+
+def turn(value, k, count):
+    return lax.ppermute(value, "seq", [(i, (i + k) % count) for i in range(count)]) if k else value
+
+
+def relay(value, count):
+    near = [(i, i ^ 1) for i in range(count)]
+    far = lax.ppermute(value, "chan", [(i, i ^ 2) for i in range(count)])
+    return [value, lax.ppermute(value, "chan", near), far, lax.ppermute(far, "chan", near)]
+
+
+def gather_seq(value, count):
+    return [turn(value, k, count) for k in range(count)]
+
+
+def trade_seq(values, count):
+    return [turn(v, k, count) for k, v in enumerate(values)]
 
 
 def padded(cells, sides, width):
@@ -29,7 +383,7 @@
     return jax.nn.gelu(values, approximate=True)
 
 
-def per_device(
+def plain_path(
     x_rows, dest_slab, kept_len, convolution_weight, b_conv, entry_norm_gain, w_proj, g_cot
 ):
     seq_count = lax.axis_size("seq")
@@ -157,6 +511,177 @@
     return (qk_out, dw_conv, dw_proj, dx_field)
 
 
+def per_device(x_rows, dest_slab, kept_len, convolution_weight, b_conv, entry_norm_gain, w_proj, g_cot):
+    slabs = lax.axis_size("seq")
+    chans = lax.axis_size("chan")
+    if slabs != 4 or chans != 4:
+        return plain_path(x_rows, dest_slab, kept_len, convolution_weight, b_conv, entry_norm_gain, w_proj, g_cot)
+    rows, block_len, width = x_rows.shape
+    channels = width * chans
+    length = slabs * block_len
+    count = length // 2
+    payload = CAP * block_len + 16
+    feat, positions = g_cot.shape
+    padded_rows = length + 16
+    taps = jnp.transpose(convolution_weight, (1, 0, 2))
+    gain = entry_norm_gain
+    me = lax.axis_index("seq")
+    own = channels // slabs
+    part = length // chans
+    extra = length // 4
+
+    packed = launch(
+        functools.partial(pack_kernel, slabs, rows, block_len),
+        [struct((payload + feat // 2, width), BF)] * slabs,
+        [dest_slab, kept_len, x_rows.reshape(rows * block_len, width), g_cot],
+        specs=[HBM, HBM, HBM, VMEM],
+        scratch=[
+            pltpu.SMEM((rows,), jnp.int32),
+            pltpu.SMEM((rows,), jnp.int32),
+            pltpu.VMEM((rows * block_len, width), BF),
+            pltpu.VMEM((slabs, feat, count), BF),
+            pltpu.SemaphoreType.DMA((3,)),
+        ],
+        flops=2 * payload * slabs * rows * block_len * width,
+        moved=2 * payload * slabs * width,
+        name="pack",
+    )
+    arrived = trade_seq(packed, slabs)
+
+    def staged(*earlier):
+        return launch(
+            stage_kernel,
+            struct(taps.shape, BF),
+            [after(taps, *earlier) if earlier else taps],
+            specs=[HBM],
+            scratch=[pltpu.SemaphoreType.DMA(())],
+            moved=4 * channels * width * KERNEL_TAPS,
+            name="stage",
+        )
+
+    taps_early = staged()
+    arrived, taps_early = lax.optimization_barrier((arrived, taps_early))
+
+    routed, cot_mine = launch(
+        functools.partial(unpack_kernel, slabs, block_len),
+        [struct((padded_rows, width), BF), struct((slabs, feat, count), BF)],
+        arrived,
+        flops=2 * payload * slabs * padded_rows * width,
+        moved=2 * payload * slabs * width,
+        name="unpack",
+    )
+    x_all = relay(routed, chans)
+    dxhat = launch(
+        functools.partial(cot_kernel, slabs, chans),
+        struct((count, width), F32),
+        [*swaps(cot_mine, chans), w_proj, gain],
+        scratch=[pltpu.VMEM((feat * chans * slabs, count), BF)],
+        name="cotangent",
+    )
+    cot_wide = swaps(g_cot, chans)
+    pieces = launch(
+        functools.partial(quarter_kernel, slabs, chans), [struct((part, own), BF)] * slabs, x_all, name="quarter"
+    )
+    traded = trade_seq(pieces, slabs)
+    pooled, slope = launch(
+        functools.partial(conv_kernel, chans),
+        [struct((count, width), F32), struct((length, width), F32)],
+        [*x_all, taps_early, b_conv],
+        flops=2 * padded_rows * channels * width * KERNEL_TAPS,
+        moved=2 * channels * width * KERNEL_TAPS,
+        room=16,
+        scratch=[
+            pltpu.VMEM((padded_rows, channels), BF),
+            pltpu.VMEM((length + 2 * EDGE, width), F32),
+            pltpu.VMEM((length, width), F32),
+            pltpu.VMEM((width // 128, length, 128), F32),
+        ],
+        name="conv",
+    )
+
+    stats = launch(
+        sums_kernel, struct((8, -(-count // 128) * 128), F32), [pooled, dxhat], name="sums"
+    )
+    low, high = launch(
+        functools.partial(grad_kernel, chans),
+        [struct((count + extra, width), BF), struct((length - extra, width), BF)],
+        [*swaps(stats, chans), pooled, slope, dxhat, gain],
+        scratch=[pltpu.VMEM((width // 128, length, 128), F32)],
+        flops=20 * length * width,
+        moved=12 * length * width,
+        name="gradient",
+    )
+    x_own = lax.all_gather(jnp.stack(after(traded, low)), "chan", axis=0, tiled=False)
+    x_turned = launch(
+        functools.partial(transpose_kernel, slabs, chans),
+        struct((own, length * slabs), BF),
+        [x_own],
+        scratch=[pltpu.VMEM((length * slabs, own), BF)],
+        name="turn_x",
+    )
+    low_all = gather_seq(low, slabs)
+    high_all = gather_seq(high, slabs)
+
+    taps_late = staged(low)
+    low_far = after(low, low_all[1], low_all[3], high_all[1], high_all[3], taps_late, cot_wide)
+    low_near = after(low_far, low_all[2])
+
+    def dx_part(low, picks, dtypes, name):
+        return launch(
+            functools.partial(dx_kernel, picks),
+            [struct((width, length), d) for d in dtypes],
+            [low, high, high_all[1], low_all[3], taps_late],
+            scratch=[pltpu.VMEM((length + 2 * EDGE, width), F32), pltpu.VMEM((KERNEL_TAPS, length, width), BF)],
+            flops=2 * len(picks) * length * width * width * KERNEL_TAPS,
+            moved=2 * len(picks) * width * width * KERNEL_TAPS,
+            room=14,
+            name=name,
+        )
+
+    near = [(i, i ^ 1) for i in range(chans)]
+    over = [(i, i ^ 2) for i in range(chans)]
+    through, across = dx_part(low_far, (3, 2), (BF, F32), "dx_far")
+    across = (across + lax.ppermute(through, "chan", near).astype(F32)).astype(BF)
+    across = lax.ppermute(across, "chan", over)
+    beside, mine_dx = dx_part(low_near, (1, 0), (BF, F32), "dx_near")
+    beside = lax.ppermute(beside, "chan", near)
+    dx_field = (mine_dx + beside.astype(F32) + across.astype(F32)).astype(BF)
+
+    w_late, x_turned = lax.optimization_barrier((w_proj, x_turned))
+    proj = launch(
+        functools.partial(proj_kernel, slabs, chans),
+        [struct((feat * chans, width), F32), struct((feat, positions), F32)] + [struct((feat, positions), BF)] * (chans - 1),
+        [*cot_wide, *low_all, w_late],
+        scratch=[
+            pltpu.VMEM((feat * chans, positions), BF),
+            pltpu.VMEM((positions, width), BF),
+            pltpu.VMEM((feat * chans, positions), F32),
+        ],
+        room=12,
+        flops=4 * feat * chans * positions * width,
+        moved=4 * feat * chans * width,
+        name="projection",
+    )
+    dw_proj, qk_parts = proj[0], proj[1:]
+    qk_got = [lax.ppermute(qk_parts[j], "chan", [(i, i ^ j) for i in range(chans)]) for j in range(1, chans)]
+    dw_taps = launch(
+        functools.partial(dw_kernel, slabs),
+        struct((KERNEL_TAPS, own, width), F32),
+        [x_turned, *low_all, *high_all],
+        room=16,
+        scratch=[pltpu.VMEM((length * slabs + 16, width), F32), pltpu.VMEM((length * slabs, width), BF)],
+        flops=2 * length * slabs * own * width * KERNEL_TAPS,
+        moved=4 * own * width * KERNEL_TAPS,
+        name="dw",
+    )
+    qk_got, dw_taps = lax.optimization_barrier((qk_got, dw_taps))
+    qk_sum = qk_parts[0]
+    for got in qk_got:
+        qk_sum = qk_sum + got.astype(F32)
+    qk_out = qk_sum.astype(BF)
+    return (qk_out, jnp.transpose(dw_taps, (1, 0, 2)), dw_proj, dx_field)
+
+
 def solution(mesh):
     return jax.shard_map(
         per_device,

time: 222 us -> 128 us (0.58)
  blocking collectives: 38.3 us -> 0 us
  matrix products: 31.5 us -> 0 us
  waiting for transfers between devices: 79.9 us -> 50.2 us
  Pallas kernels: 0 us -> 19.4 us
  local copies, waits for them, and re-layouts: 17.9 us -> 9.84 us
  other arithmetic: 8.65 us -> 2.32 us
  starting transfers between devices: 29.8 us -> 32.1 us
    all_to_all x5 -> x0, waiting for transfers between devices: 75 us -> none  [the longest x1 35.6 us: per_device(): lax.all_to_all(complete_rows.reshape(-1, seq_count, own_ch), 'seq', split...]
    ppermute x4 -> x30, waiting for transfers between devices: 4.19 us -> 50.2 us  [the longest x12 18.2 us: turn(): lax.ppermute(value, 'seq', [(i, (i + k) % count) for i in range(count)])]
    all_gather x3 -> x0, blocking collectives: 32.3 us -> none  [the longest x1 16.7 us: per_device(): norm_all = lax.all_gather(normalized, 'seq', axis=0, tiled=True)]
    dot_general x20 -> x0, matrix products: 31.5 us -> none  [the longest x5 12.2 us: per_device(): jnp.einsum('io,po->ip', convolution_weight[:, kernel_tap_index, :], dy_pa...]
    ppermute x4 -> x30, starting transfers between devices: 8.41 us -> 32 us  [the longest x12 21.7 us: turn(): lax.ppermute(value, 'seq', [(i, (i + k) % count) for i in range(count)])]
    all_to_all x5 -> x0, starting transfers between devices: 21.4 us -> none  [the longest x1 6.32 us: per_device(): lax.all_to_all(sent_counts, 'seq', split_axis=0, concat_axis=0, tiled=True)]
    pallas_call x0 -> x14, Pallas kernels: none -> 19.4 us  [launch(): pl.pallas_call(body, out_shape=outs, in_specs=specs or [VMEM] * len(ins),...]
    reshape x9 -> x0, local copies, waits for them, and re-layouts: 6.76 us -> none  [the longest x1 2.42 us: per_device(): complete_rows.reshape(-1, seq_count, own_ch)]
  transfers between devices with their start and end apart: 12 -> 31, of which waited for: 6 -> 14; matrix products, arithmetic and copies ran while one was open for 13% -> 1% of each run, Pallas kernels for 0% -> 14%
where the time goes in v3:
time: 128 us
  waiting for transfers between devices  50.2 us (39%)
  starting transfers between devices  32.1 us (25%)
  Pallas kernels  19.4 us (15%)
  between operations  14.3 us (11%)
  local copies, waits for them, and re-layouts  9.84 us (8%)
  other arithmetic  2.32 us (2%)
    ppermute x12, starting transfers between devices, turn(): lax.ppermute(value, 'seq', [(i, (i + k) % count) for i in range(count)])  21.7 us
    pallas_call x14, Pallas kernels, launch(): pl.pallas_call(body, out_shape=outs, in_specs=specs or [VMEM] * len(ins),...  19.4 us
    ppermute x12, waiting for transfers between devices, turn(): lax.ppermute(value, 'seq', [(i, (i + k) % count) for i in range(count)])  18.2 us
    ppermute x9, waiting for transfers between devices, swaps(): lax.ppermute(value, 'chan', [(i, i ^ j) for i in range(count)])  15.9 us
    unnamed x22, local copies, waits for them, and re-layouts  9.84 us
    ppermute x1, waiting for transfers between devices, per_device(): across = lax.ppermute(across, 'chan', over)  7.97 us
    ppermute x1, waiting for transfers between devices, relay(): far = lax.ppermute(value, 'chan', [(i, i ^ 2) for i in range(count)])  7.6 us
    ppermute x9, starting transfers between devices, swaps(): lax.ppermute(value, 'chan', [(i, i ^ j) for i in range(count)])  5.92 us
  transfers between devices with their start and end apart: 31, of which 14 were waited for; matrix products, arithmetic and copies ran while one was open for 1% of the time, Pallas kernels for 14%

profile of v3, /device:TPU:0, one launch (start us, length us, event | category | flops | bytes accessed | tf_op | source)
XLA Modules:
  0.0 128.1 jit_solution(3868364715120280453)
XLA Ops:
  7.2 0.0 all-gather.3.cloned.1.call-start
  7.2 0.9 copy-done.4
  8.1 1.0 copy-done.7
  9.1 0.7 copy-done.9
  9.8 0.7 copy-done.10
  10.4 1.3 pack.1
  11.7 3.1 %collective-permute-start.3 = (bf16[240,384]{1,0:T(8,128)(2,1)S(1)}, bf16[240,384]{1,0:T(8,128)(2,1)S(1)}, u32[]{:S(2)}, u32[]{:S(2)}) collective-permute-start(bf16[240,384]{1,0:T(8,128)(2,1)S(1)} %get-tuple-element.46), channel_id=1, source_target_pairs={{0,4},{4,8},{8,12},{12,0},{1,5},{5,9},{9,13},{13,1},{2,6},{6,10},{... | collective-permute-start | bytes 552968 | tf_op jit(solution)/shard_map/ppermute | solution.py:348
  14.8 2.6 %collective-permute-start.4 = (bf16[240,384]{1,0:T(8,128)(2,1)S(1)}, bf16[240,384]{1,0:T(8,128)(2,1)S(1)}, u32[]{:S(2)}, u32[]{:S(2)}) collective-permute-start(bf16[240,384]{1,0:T(8,128)(2,1)S(1)} %get-tuple-element.47), channel_id=1, source_target_pairs={{0,8},{4,12},{8,0},{12,4},{1,9},{5,13},{9,1},{13,5},{2,10},{6,14},... | collective-permute-start | bytes 552968 | tf_op jit(solution)/shard_map/ppermute | solution.py:348
  17.3 1.3 %collective-permute-start.5 = (bf16[240,384]{1,0:T(8,128)(2,1)S(1)}, bf16[240,384]{1,0:T(8,128)(2,1)S(1)}, u32[]{:S(2)}, u32[]{:S(2)}) collective-permute-start(bf16[240,384]{1,0:T(8,128)(2,1)S(1)} %get-tuple-element.48), channel_id=1, source_target_pairs={{0,12},{4,0},{8,4},{12,8},{1,13},{5,1},{9,5},{13,9},{2,14},{6,2},{... | collective-permute-start | bytes 552968 | tf_op jit(solution)/shard_map/ppermute | solution.py:348
  18.7 2.7 %copy-done = bf16[1536,5,384]{2,0,1:T(8,128)(2,1)S(1)} copy-done((bf16[1536,5,384]{2,0,1:T(8,128)(2,1)S(1)}, bf16[1536,5,384]{2,0,1:T(8,128)(2,1)}, u32[]{:S(2)}) %copy-start) | copy-done | bytes 5898264
  21.4 0.6 stage.2.refs_4_
  21.9 0.4 collective-permute-done.3.refs_1_
  22.3 7.1 %collective-permute-done.4.refs_2_ = bf16[240,384]{1,0:T(8,128)(2,1)S(1)} collective-permute-done((bf16[240,384]{1,0:T(8,128)(2,1)S(1)}, bf16[240,384]{1,0:T(8,128)(2,1)S(1)}, u32[]{:S(2)}, u32[]{:S(2)}) %collective-permute-start.4) | collective-permute-done | bytes 184352 | tf_op jit(solution)/shard_map/ppermute | solution.py:348
  29.4 0.6 unpack.1
  30.0 1.5 %collective-permute-start.7 = (bf16[400,384]{1,0:T(8,128)(2,1)S(1)}, bf16[400,384]{1,0:T(8,128)(2,1)S(1)}, u32[]{:S(2)}, u32[]{:S(2)}) collective-permute-start(bf16[400,384]{1,0:T(8,128)(2,1)S(1)} %get-tuple-element.53.refs_0_), channel_id=1, source_target_pairs={{0,2},{1,3},{2,0},{3,1},{4,6},{5,7},{6,4},{7,5},{8,10},{9,11},{10,... | collective-permute-start | bytes 921608 | tf_op jit(solution)/shard_map/ppermute | solution.py:353
  31.6 7.6 %collective-permute-done.7.refs_2_ = bf16[400,384]{1,0:T(8,128)(2,1)S(1)} collective-permute-done((bf16[400,384]{1,0:T(8,128)(2,1)S(1)}, bf16[400,384]{1,0:T(8,128)(2,1)S(1)}, u32[]{:S(2)}, u32[]{:S(2)}) %collective-permute-start.7) | collective-permute-done | bytes 307232 | tf_op jit(solution)/shard_map/ppermute | solution.py:353
  39.2 1.5 %collective-permute-start.10 = (bf16[4,64,192]{2,1,0:T(8,128)(2,1)S(1)}, bf16[4,64,192]{2,1,0:T(8,128)(2,1)S(1)}, u32[]{:S(2)}, u32[]{:S(2)}) collective-permute-start(bf16[4,64,192]{2,1,0:T(8,128)(2,1)S(1)} %get-tuple-element.56.refs_0_), channel_id=1, source_target_pairs={{0,2},{1,3},{2,0},{3,1},{4,6},{5,7},{6,4},{7,5},{8,10},{9,11},{10,... | collective-permute-start | bytes 294920 | tf_op jit(solution)/shard_map/ppermute | solution.py:344
  40.7 0.4 collective-permute-start.11
  41.0 0.3 collective-permute-start.9
  41.3 4.2 %collective-permute-done.10.refs_2_ = bf16[4,64,192]{2,1,0:T(8,128)(2,1)S(1)} collective-permute-done((bf16[4,64,192]{2,1,0:T(8,128)(2,1)S(1)}, bf16[4,64,192]{2,1,0:T(8,128)(2,1)S(1)}, u32[]{:S(2)}, u32[]{:S(2)}) %collective-permute-start.10) | collective-permute-done | bytes 98336 | tf_op jit(solution)/shard_map/ppermute | solution.py:344
  45.5 2.0 %collective-permute-done.11.refs_3_ = bf16[4,64,192]{2,1,0:T(8,128)(2,1)S(1)} collective-permute-done((bf16[4,64,192]{2,1,0:T(8,128)(2,1)S(1)}, bf16[4,64,192]{2,1,0:T(8,128)(2,1)S(1)}, u32[]{:S(2)}, u32[]{:S(2)}) %collective-permute-start.11) | collective-permute-done | bytes 98336 | tf_op jit(solution)/shard_map/ppermute | solution.py:344
  47.5 0.5 cotangent.1.dxhat_ref.refs_6_
  48.0 0.1 quarter.1
  48.2 4.6 %collective-permute-start.18 = (bf16[96,384]{1,0:T(8,128)(2,1)S(1)}, bf16[96,384]{1,0:T(8,128)(2,1)S(1)}, u32[]{:S(2)}, u32[]{:S(2)}) collective-permute-start(bf16[96,384]{1,0:T(8,128)(2,1)S(1)} %get-tuple-element.60), channel_id=1, source_target_pairs={{0,4},{4,8},{8,12},{12,0},{1,5},{5,9},{9,13},{13,1},{2,6},{6,10},{... | collective-permute-start | bytes 221192 | tf_op jit(solution)/shard_map/ppermute | solution.py:348
  52.7 0.6 collective-permute-start.19
  53.3 1.9 %collective-permute-start.20 = (bf16[96,384]{1,0:T(8,128)(2,1)S(1)}, bf16[96,384]{1,0:T(8,128)(2,1)S(1)}, u32[]{:S(2)}, u32[]{:S(2)}) collective-permute-start(bf16[96,384]{1,0:T(8,128)(2,1)S(1)} %get-tuple-element.62), channel_id=1, source_target_pairs={{0,12},{4,0},{8,4},{12,8},{1,13},{5,1},{9,5},{13,9},{2,14},{6,2},{... | collective-permute-start | bytes 221192 | tf_op jit(solution)/shard_map/ppermute | solution.py:348
  55.2 3.9 %conv.1 = (f32[192,384]{1,0:T(8,128)S(1)}, f32[384,384]{1,0:T(8,128)S(1)}) custom-call(bf16[400,384]{1,0:T(8,128)(2,1)S(1)} %get-tuple-element.53.refs_0_, bf16[400,384]{1,0:T(8,128)(2,1)S(1)} %collective-permute-done.6.refs_1_, bf16[400,384]{1,0:T(8,128)(2,1)S(1)} %collective-permute-done.7.refs_2_, bf16[400,384]{1,0:T(8,128)(2,1)S(1)} %collective-permute-done.8.refs_3_, ...), custom_call_target="tpu_custom_call" | custom-call | flops 2359296000 | bytes 5898240 | tf_op jit(solution)/shard_map/conv/pallas_call | solution.py:29
  59.1 0.2 sums.1.refs_0_
  59.3 0.0 collective-permute-start.12
  59.3 1.6 %collective-permute-start.13 = (f32[8,256]{1,0:T(8,128)S(1)}, f32[8,256]{1,0:T(8,128)S(1)}, u32[]{:S(2)}, u32[]{:S(2)}) collective-permute-start(f32[8,256]{1,0:T(8,128)S(1)} %sums.1.refs_0_), channel_id=1, source_target_pairs={{0,2},{1,3},{2,0},{3,1},{4,6},{5,7},{6,4},{7,5},{8,10},{9,11},{10,... | collective-permute-start | bytes 24584 | tf_op jit(solution)/shard_map/ppermute | solution.py:344
  60.9 0.9 collective-permute-start.14
  61.8 1.3 %collective-permute-done.13.refs_2_ = f32[8,256]{1,0:T(8,128)S(1)} collective-permute-done((f32[8,256]{1,0:T(8,128)S(1)}, f32[8,256]{1,0:T(8,128)S(1)}, u32[]{:S(2)}, u32[]{:S(2)}) %collective-permute-start.13) | collective-permute-done | bytes 8224 | tf_op jit(solution)/shard_map/ppermute | solution.py:344
  63.1 0.9 collective-permute-done.14.refs_3_
  64.0 0.6 gradient.1
  64.6 0.8 pad_maximum_fusion
  65.4 0.0 all-gather.3.cloned.1.call-update
  65.4 0.2 collective-permute-start
  65.6 0.2 collective-permute-start.15
  65.8 3.7 %collective-permute-start.17 = (bf16[288,384]{1,0:T(8,128)(2,1)S(1)}, bf16[288,384]{1,0:T(8,128)(2,1)S(1)}, u32[]{:S(2)}, u32[]{:S(2)}) collective-permute-start(bf16[288,384]{1,0:T(8,128)(2,1)S(1)} %get-tuple-element.81.refs_4_.refs_1_.refs_0_), channel_id=1, source_target_pairs={{0,12},{4,0},{8,4},{12,8},{1,13},{5,1},{9,5},{13,9},{2,14},{6,2},{... | collective-permute-start | bytes 663560 | tf_op jit(solution)/shard_map/ppermute | solution.py:348
  69.5 3.8 %collective-permute-start.26 = (bf16[288,384]{1,0:T(8,128)(2,1)S(1)}, bf16[288,384]{1,0:T(8,128)(2,1)S(1)}, u32[]{:S(2)}, u32[]{:S(2)}) collective-permute-start(bf16[288,384]{1,0:T(8,128)(2,1)S(1)} %get-tuple-element.73.refs_5_.refs_1_), channel_id=1, source_target_pairs={{0,12},{4,0},{8,4},{12,8},{1,13},{5,1},{9,5},{13,9},{2,14},{6,2},{... | collective-permute-start | bytes 663560 | tf_op jit(solution)/shard_map/ppermute | solution.py:348
  73.3 1.1 collective-permute-start.1
  74.4 5.9 %collective-permute-done.1.refs_2_ = bf16[64,768]{1,0:T(8,128)(2,1)S(1)} collective-permute-done((bf16[64,768]{1,0:T(8,128)(2,1)S(1)}, bf16[64,768]{1,0:T(8,128)(2,1)S(1)}, u32[]{:S(2)}, u32[]{:S(2)}) %collective-permute-start.1) | collective-permute-done | bytes 98336 | tf_op jit(solution)/shard_map/ppermute | solution.py:344
  80.3 2.7 %copy-done.1 = bf16[1536,5,384]{2,0,1:T(8,128)(2,1)S(1)} copy-done((bf16[1536,5,384]{2,0,1:T(8,128)(2,1)S(1)}, bf16[1536,5,384]{2,0,1:T(8,128)(2,1)}, u32[]{:S(2)}) %copy-start.1) | copy-done | bytes 5898264
  83.0 0.6 stage.3.refs_4_
  83.6 1.5 %collective-permute-done.2.refs_3_ = bf16[64,768]{1,0:T(8,128)(2,1)S(1)} collective-permute-done((bf16[64,768]{1,0:T(8,128)(2,1)S(1)}, bf16[64,768]{1,0:T(8,128)(2,1)S(1)}, u32[]{:S(2)}, u32[]{:S(2)}) %collective-permute-start.2) | collective-permute-done | bytes 98336 | tf_op jit(solution)/shard_map/ppermute | solution.py:344
  85.2 0.1 collective-permute-done.24.refs_6_.refs_2_
  85.3 2.3 %collective-permute-done.26.refs_8_ = bf16[288,384]{1,0:T(8,128)(2,1)S(1)} collective-permute-done((bf16[288,384]{1,0:T(8,128)(2,1)S(1)}, bf16[288,384]{1,0:T(8,128)(2,1)S(1)}, u32[]{:S(2)}, u32[]{:S(2)}) %collective-permute-start.26) | collective-permute-done | bytes 221216 | tf_op jit(solution)/shard_map/ppermute | solution.py:348
  87.5 2.0 %dx_far.1 = (bf16[384,384]{1,0:T(8,128)(2,1)S(1)}, f32[384,384]{1,0:T(8,128)S(1)}) custom-call(bf16[288,384]{1,0:T(8,128)(2,1)S(1)} %get-tuple-element.81.refs_4_.refs_1_.refs_0_, bf16[288,384]{1,0:T(8,128)(2,1)S(1)} %get-tuple-element.73.refs_5_.refs_1_, bf16[288,384]{1,0:T(8,128)(2,1)S(1)} %collective-permute-done.24.refs_6_.refs_2_, ...), custom_call_target="tpu_custom_call" | custom-call | flops 1132462080 | bytes 2949120 | tf_op jit(solution)/shard_map/dx_far/pallas_call | solution.py:29
  89.6 0.1 collective-permute-start.28
  89.7 8.3 %collective-permute-done.16.refs_6_.refs_3_ = bf16[288,384]{1,0:T(8,128)(2,1)S(1)} collective-permute-done((bf16[288,384]{1,0:T(8,128)(2,1)S(1)}, bf16[288,384]{1,0:T(8,128)(2,1)S(1)}, u32[]{:S(2)}, u32[]{:S(2)}) %collective-permute-start.16) | collective-permute-done | bytes 221216 | tf_op jit(solution)/shard_map/ppermute | solution.py:348
  98.0 2.0 %dx_near.1 = (bf16[384,384]{1,0:T(8,128)(2,1)S(1)}, f32[384,384]{1,0:T(8,128)S(1)}) custom-call(bf16[288,384]{1,0:T(8,128)(2,1)S(1)} %get-tuple-element.81.refs_4_.refs_1_.refs_0_, bf16[288,384]{1,0:T(8,128)(2,1)S(1)} %get-tuple-element.73.refs_5_.refs_1_, bf16[288,384]{1,0:T(8,128)(2,1)S(1)} %collective-permute-done.24.refs_6_.refs_2_, ...), custom_call_target="tpu_custom_call" | custom-call | flops 1132462080 | bytes 2949120 | tf_op jit(solution)/shard_map/dx_near/pallas_call | solution.py:29
  100.0 0.1 collective-permute-start.27
  100.1 0.1 add_convert_fusion.1
  100.2 0.9 collective-permute-start.29
  101.1 0.6 collective-permute-done.27
  101.7 8.0 %collective-permute-done.29 = bf16[384,384]{1,0:T(8,128)(2,1)S(1)} collective-permute-done((bf16[384,384]{1,0:T(8,128)(2,1)S(1)}, bf16[384,384]{1,0:T(8,128)(2,1)S(1)}, u32[]{:S(2)}, u32[]{:S(2)}) %collective-permute-start.29) | collective-permute-done | bytes 294944 | tf_op jit(solution)/shard_map/ppermute | solution.py:645
  109.6 0.8 add_convert_fusion
  110.4 1.3 copy-done.3
  111.7 0.5 turn_x.1.refs_0_
  112.2 1.2 projection.1
  113.4 0.8 collective-permute-start.22
  114.2 1.0 collective-permute-start.23
  115.3 5.3 %dw.1 = f32[5,384,384]{2,1,0:T(8,128)} custom-call(bf16[384,1536]{1,0:T(8,128)(2,1)S(1)} %turn_x.1.refs_0_, bf16[288,384]{1,0:T(8,128)(2,1)S(1)} %get-tuple-element.81.refs_4_.refs_1_.refs_0_, bf16[288,384]{1,0:T(8,128)(2,1)S(1)} %collective-permute-done.15.refs_5_.refs_2_, bf16[288,384]{1,0:T(8,128)(2,1)S(1)} %collective-permute-done.16.refs_6_.refs_3_, ...), custom_call_target="tpu_custom_call" | custom-call | flops 2264924160 | bytes 2949120 | tf_op jit(solution)/shard_map/dw/pallas_call | solution.py:29
  120.5 0.7 add_convert_fusion.2
  (39 shorter events, 0.1 us)
Async XLA Ops:
  7.2 103.3 %all-gather.3.cloned.1.call-start = ((), (), s32[]{:S(2)}) async-start(), calls=%async_computation | async-start | bytes 1474560 | tf_op jit(solution)/shard_map/all_gather | solution.py:614
  7.2 0.9 copy-start.4
  8.1 1.0 copy-start.7
  9.1 0.7 copy-start.9
  9.8 0.7 copy-start.10
  11.7 10.7 %collective-permute-start.3 = (bf16[240,384]{1,0:T(8,128)(2,1)S(1)}, bf16[240,384]{1,0:T(8,128)(2,1)S(1)}, u32[]{:S(2)}, u32[]{:S(2)}) collective-permute-start(bf16[240,384]{1,0:T(8,128)(2,1)S(1)} %get-tuple-element.46), channel_id=1, source_target_pairs={{0,4},{4,8},{8,12},{12,0},{1,5},{5,9},{9,13},{13,1},{2,6},{6,10},{... | collective-permute-start | bytes 552968 | tf_op jit(solution)/shard_map/ppermute | solution.py:348
  14.8 14.7 %collective-permute-start.4 = (bf16[240,384]{1,0:T(8,128)(2,1)S(1)}, bf16[240,384]{1,0:T(8,128)(2,1)S(1)}, u32[]{:S(2)}, u32[]{:S(2)}) collective-permute-start(bf16[240,384]{1,0:T(8,128)(2,1)S(1)} %get-tuple-element.47), channel_id=1, source_target_pairs={{0,8},{4,12},{8,0},{12,4},{1,9},{5,13},{9,1},{13,5},{2,10},{6,14},... | collective-permute-start | bytes 552968 | tf_op jit(solution)/shard_map/ppermute | solution.py:348
  17.3 12.1 %collective-permute-start.5 = (bf16[240,384]{1,0:T(8,128)(2,1)S(1)}, bf16[240,384]{1,0:T(8,128)(2,1)S(1)}, u32[]{:S(2)}, u32[]{:S(2)}) collective-permute-start(bf16[240,384]{1,0:T(8,128)(2,1)S(1)} %get-tuple-element.48), channel_id=1, source_target_pairs={{0,12},{4,0},{8,4},{12,8},{1,13},{5,1},{9,5},{13,9},{2,14},{6,2},{... | collective-permute-start | bytes 552968 | tf_op jit(solution)/shard_map/ppermute | solution.py:348
  18.7 2.7 %copy-start = (bf16[1536,5,384]{2,0,1:T(8,128)(2,1)S(1)}, bf16[1536,5,384]{2,0,1:T(8,128)(2,1)}, u32[]{:S(2)}) copy-start(bf16[1536,5,384]{2,0,1:T(8,128)(2,1)} %param.11) | copy-start | bytes 17694724
  21.4 26.1 %copy-start.2 = (bf16[1024,384]{1,0:T(8,128)(2,1)S(1)}, bf16[1024,384]{1,0:T(8,128)(2,1)}, u32[]{:S(2)}) copy-start(bf16[1024,384]{1,0:T(8,128)(2,1)} %refs_8_) | copy-start | bytes 2359300
  21.4 26.1 %copy-start.6 = (f32[384]{0:T(512)S(1)}, f32[384]{0:T(512)}, u32[]{:S(2)}) copy-start(f32[384]{0:T(512)} %refs_7_.1) | copy-start | bytes 4612
  21.4 33.8 %copy-start.8 = (f32[384]{0:T(512)S(1)}, f32[384]{0:T(512)}, u32[]{:S(2)}) copy-start(f32[384]{0:T(512)} %refs_5_.2) | copy-start | bytes 4612
  30.0 9.2 %collective-permute-start.7 = (bf16[400,384]{1,0:T(8,128)(2,1)S(1)}, bf16[400,384]{1,0:T(8,128)(2,1)S(1)}, u32[]{:S(2)}, u32[]{:S(2)}) collective-permute-start(bf16[400,384]{1,0:T(8,128)(2,1)S(1)} %get-tuple-element.53.refs_0_), channel_id=1, source_target_pairs={{0,2},{1,3},{2,0},{3,1},{4,6},{5,7},{6,4},{7,5},{8,10},{9,11},{10,... | collective-permute-start | bytes 921608 | tf_op jit(solution)/shard_map/ppermute | solution.py:353
  31.6 16.4 %collective-permute-start.6 = (bf16[400,384]{1,0:T(8,128)(2,1)S(1)}, bf16[400,384]{1,0:T(8,128)(2,1)S(1)}, u32[]{:S(2)}, u32[]{:S(2)}) collective-permute-start(bf16[400,384]{1,0:T(8,128)(2,1)S(1)} %get-tuple-element.53.refs_0_), channel_id=1, source_target_pairs={{0,1},{1,0},{2,3},{3,2},{4,5},{5,4},{6,7},{7,6},{8,9},{9,8},{10,11... | collective-permute-start | bytes 921608 | tf_op jit(solution)/shard_map/ppermute | solution.py:354
  39.2 8.8 %collective-permute-start.8 = (bf16[400,384]{1,0:T(8,128)(2,1)S(1)}, bf16[400,384]{1,0:T(8,128)(2,1)S(1)}, u32[]{:S(2)}, u32[]{:S(2)}) collective-permute-start(bf16[400,384]{1,0:T(8,128)(2,1)S(1)} %collective-permute-done.7.refs_2_), channel_id=1, source_target_pairs={{0,1},{1,0},{2,3},{3,2},{4,5},{5,4},{6,7},{7,6},{8,9},{9,8},{10,11... | collective-permute-start | bytes 921608 | tf_op jit(solution)/shard_map/ppermute | solution.py:354
  39.2 6.3 %collective-permute-start.10 = (bf16[4,64,192]{2,1,0:T(8,128)(2,1)S(1)}, bf16[4,64,192]{2,1,0:T(8,128)(2,1)S(1)}, u32[]{:S(2)}, u32[]{:S(2)}) collective-permute-start(bf16[4,64,192]{2,1,0:T(8,128)(2,1)S(1)} %get-tuple-element.56.refs_0_), channel_id=1, source_target_pairs={{0,2},{1,3},{2,0},{3,1},{4,6},{5,7},{6,4},{7,5},{8,10},{9,11},{10,... | collective-permute-start | bytes 294920 | tf_op jit(solution)/shard_map/ppermute | solution.py:344
  40.7 6.8 %collective-permute-start.11 = (bf16[4,64,192]{2,1,0:T(8,128)(2,1)S(1)}, bf16[4,64,192]{2,1,0:T(8,128)(2,1)S(1)}, u32[]{:S(2)}, u32[]{:S(2)}) collective-permute-start(bf16[4,64,192]{2,1,0:T(8,128)(2,1)S(1)} %get-tuple-element.56.refs_0_), channel_id=1, source_target_pairs={{0,3},{1,2},{2,1},{3,0},{4,7},{5,6},{6,5},{7,4},{8,11},{9,10},{10,... | collective-permute-start | bytes 294920 | tf_op jit(solution)/shard_map/ppermute | solution.py:344
  41.0 6.5 %collective-permute-start.9 = (bf16[4,64,192]{2,1,0:T(8,128)(2,1)S(1)}, bf16[4,64,192]{2,1,0:T(8,128)(2,1)S(1)}, u32[]{:S(2)}, u32[]{:S(2)}) collective-permute-start(bf16[4,64,192]{2,1,0:T(8,128)(2,1)S(1)} %get-tuple-element.56.refs_0_), channel_id=1, source_target_pairs={{0,1},{1,0},{2,3},{3,2},{4,5},{5,4},{6,7},{7,6},{8,9},{9,8},{10,11... | collective-permute-start | bytes 294920 | tf_op jit(solution)/shard_map/ppermute | solution.py:344
  48.1 17.3 %copy-start.5 = (bf16[64,768]{1,0:T(8,128)(2,1)S(1)}, bf16[64,768]{1,0:T(8,128)(2,1)}, u32[]{:S(2)}) copy-start(bf16[64,768]{1,0:T(8,128)(2,1)} %refs_0_.1) | copy-start | bytes 294916
  48.2 16.4 %collective-permute-start.18 = (bf16[96,384]{1,0:T(8,128)(2,1)S(1)}, bf16[96,384]{1,0:T(8,128)(2,1)S(1)}, u32[]{:S(2)}, u32[]{:S(2)}) collective-permute-start(bf16[96,384]{1,0:T(8,128)(2,1)S(1)} %get-tuple-element.60), channel_id=1, source_target_pairs={{0,4},{4,8},{8,12},{12,0},{1,5},{5,9},{9,13},{13,1},{2,6},{6,10},{... | collective-permute-start | bytes 221192 | tf_op jit(solution)/shard_map/ppermute | solution.py:348
  52.7 11.9 %collective-permute-start.19 = (bf16[96,384]{1,0:T(8,128)(2,1)S(1)}, bf16[96,384]{1,0:T(8,128)(2,1)S(1)}, u32[]{:S(2)}, u32[]{:S(2)}) collective-permute-start(bf16[96,384]{1,0:T(8,128)(2,1)S(1)} %get-tuple-element.61), channel_id=1, source_target_pairs={{0,8},{4,12},{8,0},{12,4},{1,9},{5,13},{9,1},{13,5},{2,10},{6,14},... | collective-permute-start | bytes 221192 | tf_op jit(solution)/shard_map/ppermute | solution.py:348
  53.3 11.3 %collective-permute-start.20 = (bf16[96,384]{1,0:T(8,128)(2,1)S(1)}, bf16[96,384]{1,0:T(8,128)(2,1)S(1)}, u32[]{:S(2)}, u32[]{:S(2)}) collective-permute-start(bf16[96,384]{1,0:T(8,128)(2,1)S(1)} %get-tuple-element.62), channel_id=1, source_target_pairs={{0,12},{4,0},{8,4},{12,8},{1,13},{5,1},{9,5},{13,9},{2,14},{6,2},{... | collective-permute-start | bytes 221192 | tf_op jit(solution)/shard_map/ppermute | solution.py:348
  59.3 1.6 %collective-permute-start.12 = (f32[8,256]{1,0:T(8,128)S(1)}, f32[8,256]{1,0:T(8,128)S(1)}, u32[]{:S(2)}, u32[]{:S(2)}) collective-permute-start(f32[8,256]{1,0:T(8,128)S(1)} %sums.1.refs_0_), channel_id=1, source_target_pairs={{0,1},{1,0},{2,3},{3,2},{4,5},{5,4},{6,7},{7,6},{8,9},{9,8},{10,11... | collective-permute-start | bytes 24584 | tf_op jit(solution)/shard_map/ppermute | solution.py:344
  59.3 3.7 %collective-permute-start.13 = (f32[8,256]{1,0:T(8,128)S(1)}, f32[8,256]{1,0:T(8,128)S(1)}, u32[]{:S(2)}, u32[]{:S(2)}) collective-permute-start(f32[8,256]{1,0:T(8,128)S(1)} %sums.1.refs_0_), channel_id=1, source_target_pairs={{0,2},{1,3},{2,0},{3,1},{4,6},{5,7},{6,4},{7,5},{8,10},{9,11},{10,... | collective-permute-start | bytes 24584 | tf_op jit(solution)/shard_map/ppermute | solution.py:344
  60.9 3.1 %collective-permute-start.14 = (f32[8,256]{1,0:T(8,128)S(1)}, f32[8,256]{1,0:T(8,128)S(1)}, u32[]{:S(2)}, u32[]{:S(2)}) collective-permute-start(f32[8,256]{1,0:T(8,128)S(1)} %sums.1.refs_0_), channel_id=1, source_target_pairs={{0,3},{1,2},{2,1},{3,0},{4,7},{5,6},{6,5},{7,4},{8,11},{9,10},{10,... | collective-permute-start | bytes 24584 | tf_op jit(solution)/shard_map/ppermute | solution.py:344
  65.4 7.9 %collective-permute-start = (bf16[64,768]{1,0:T(8,128)(2,1)S(1)}, bf16[64,768]{1,0:T(8,128)(2,1)S(1)}, u32[]{:S(2)}, u32[]{:S(2)}) collective-permute-start(bf16[64,768]{1,0:T(8,128)(2,1)S(1)} %copy-done.5), channel_id=1, source_target_pairs={{0,1},{1,0},{2,3},{3,2},{4,5},{5,4},{6,7},{7,6},{8,9},{9,8},{10,11... | collective-permute-start | bytes 294920 | tf_op jit(solution)/shard_map/ppermute | solution.py:344
  65.6 19.5 %collective-permute-start.15 = (bf16[288,384]{1,0:T(8,128)(2,1)S(1)}, bf16[288,384]{1,0:T(8,128)(2,1)S(1)}, u32[]{:S(2)}, u32[]{:S(2)}) collective-permute-start(bf16[288,384]{1,0:T(8,128)(2,1)S(1)} %get-tuple-element.81.refs_4_.refs_1_.refs_0_), channel_id=1, source_target_pairs={{0,4},{4,8},{8,12},{12,0},{1,5},{5,9},{9,13},{13,1},{2,6},{6,10},{... | collective-permute-start | bytes 663560 | tf_op jit(solution)/shard_map/ppermute | solution.py:348
  65.8 19.4 %collective-permute-start.17 = (bf16[288,384]{1,0:T(8,128)(2,1)S(1)}, bf16[288,384]{1,0:T(8,128)(2,1)S(1)}, u32[]{:S(2)}, u32[]{:S(2)}) collective-permute-start(bf16[288,384]{1,0:T(8,128)(2,1)S(1)} %get-tuple-element.81.refs_4_.refs_1_.refs_0_), channel_id=1, source_target_pairs={{0,12},{4,0},{8,4},{12,8},{1,13},{5,1},{9,5},{13,9},{2,14},{6,2},{... | collective-permute-start | bytes 663560 | tf_op jit(solution)/shard_map/ppermute | solution.py:348
  69.5 15.8 %collective-permute-start.24 = (bf16[288,384]{1,0:T(8,128)(2,1)S(1)}, bf16[288,384]{1,0:T(8,128)(2,1)S(1)}, u32[]{:S(2)}, u32[]{:S(2)}) collective-permute-start(bf16[288,384]{1,0:T(8,128)(2,1)S(1)} %get-tuple-element.73.refs_5_.refs_1_), channel_id=1, source_target_pairs={{0,4},{4,8},{8,12},{12,0},{1,5},{5,9},{9,13},{13,1},{2,6},{6,10},{... | collective-permute-start | bytes 663560 | tf_op jit(solution)/shard_map/ppermute | solution.py:348
  69.5 18.1 %collective-permute-start.26 = (bf16[288,384]{1,0:T(8,128)(2,1)S(1)}, bf16[288,384]{1,0:T(8,128)(2,1)S(1)}, u32[]{:S(2)}, u32[]{:S(2)}) collective-permute-start(bf16[288,384]{1,0:T(8,128)(2,1)S(1)} %get-tuple-element.73.refs_5_.refs_1_), channel_id=1, source_target_pairs={{0,12},{4,0},{8,4},{12,8},{1,13},{5,1},{9,5},{13,9},{2,14},{6,2},{... | collective-permute-start | bytes 663560 | tf_op jit(solution)/shard_map/ppermute | solution.py:348
  73.3 7.0 %collective-permute-start.1 = (bf16[64,768]{1,0:T(8,128)(2,1)S(1)}, bf16[64,768]{1,0:T(8,128)(2,1)S(1)}, u32[]{:S(2)}, u32[]{:S(2)}) collective-permute-start(bf16[64,768]{1,0:T(8,128)(2,1)S(1)} %copy-done.5), channel_id=1, source_target_pairs={{0,2},{1,3},{2,0},{3,1},{4,6},{5,7},{6,4},{7,5},{8,10},{9,11},{10,... | collective-permute-start | bytes 294920 | tf_op jit(solution)/shard_map/ppermute | solution.py:344
  80.3 4.8 %collective-permute-start.2 = (bf16[64,768]{1,0:T(8,128)(2,1)S(1)}, bf16[64,768]{1,0:T(8,128)(2,1)S(1)}, u32[]{:S(2)}, u32[]{:S(2)}) collective-permute-start(bf16[64,768]{1,0:T(8,128)(2,1)S(1)} %copy-done.5), channel_id=1, source_target_pairs={{0,3},{1,2},{2,1},{3,0},{4,7},{5,6},{6,5},{7,4},{8,11},{9,10},{10,... | collective-permute-start | bytes 294920 | tf_op jit(solution)/shard_map/ppermute | solution.py:344
  80.3 2.7 %copy-start.1 = (bf16[1536,5,384]{2,0,1:T(8,128)(2,1)S(1)}, bf16[1536,5,384]{2,0,1:T(8,128)(2,1)}, u32[]{:S(2)}) copy-start(bf16[1536,5,384]{2,0,1:T(8,128)(2,1)} %param.11) | copy-start | bytes 17694724
  85.2 12.8 %collective-permute-start.16 = (bf16[288,384]{1,0:T(8,128)(2,1)S(1)}, bf16[288,384]{1,0:T(8,128)(2,1)S(1)}, u32[]{:S(2)}, u32[]{:S(2)}) collective-permute-start(bf16[288,384]{1,0:T(8,128)(2,1)S(1)} %get-tuple-element.81.refs_4_.refs_1_.refs_0_), channel_id=1, source_target_pairs={{0,8},{4,12},{8,0},{12,4},{1,9},{5,13},{9,1},{13,5},{2,10},{6,14},... | collective-permute-start | bytes 663560 | tf_op jit(solution)/shard_map/ppermute | solution.py:348
  89.6 10.5 %collective-permute-start.28 = (bf16[384,384]{1,0:T(8,128)(2,1)S(1)}, bf16[384,384]{1,0:T(8,128)(2,1)S(1)}, u32[]{:S(2)}, u32[]{:S(2)}) collective-permute-start(bf16[384,384]{1,0:T(8,128)(2,1)S(1)} %get-tuple-element.85), channel_id=1, source_target_pairs={{0,1},{1,0},{2,3},{3,2},{4,5},{5,4},{6,7},{7,6},{8,9},{9,8},{10,11... | collective-permute-start | bytes 884744 | tf_op jit(solution)/shard_map/ppermute | solution.py:644
  100.0 1.6 %collective-permute-start.27 = (bf16[384,384]{1,0:T(8,128)(2,1)S(1)}, bf16[384,384]{1,0:T(8,128)(2,1)S(1)}, u32[]{:S(2)}, u32[]{:S(2)}) collective-permute-start(bf16[384,384]{1,0:T(8,128)(2,1)S(1)} %get-tuple-element.83), channel_id=1, source_target_pairs={{0,1},{1,0},{2,3},{3,2},{4,5},{5,4},{6,7},{7,6},{8,9},{9,8},{10,11... | collective-permute-start | bytes 884744 | tf_op jit(solution)/shard_map/ppermute | solution.py:647
  100.2 9.5 %collective-permute-start.29 = (bf16[384,384]{1,0:T(8,128)(2,1)S(1)}, bf16[384,384]{1,0:T(8,128)(2,1)S(1)}, u32[]{:S(2)}, u32[]{:S(2)}) collective-permute-start(bf16[384,384]{1,0:T(8,128)(2,1)S(1)} %add_convert_fusion.1), channel_id=1, source_target_pairs={{0,2},{1,3},{2,0},{3,1},{4,6},{5,7},{6,4},{7,5},{8,10},{9,11},{10,... | collective-permute-start | bytes 884744 | tf_op jit(solution)/shard_map/ppermute | solution.py:645
  101.1 14.2 %collective-permute-start.25 = (bf16[288,384]{1,0:T(8,128)(2,1)S(1)}, bf16[288,384]{1,0:T(8,128)(2,1)S(1)}, u32[]{:S(2)}, u32[]{:S(2)}) collective-permute-start(bf16[288,384]{1,0:T(8,128)(2,1)S(1)} %get-tuple-element.73.refs_5_.refs_1_), channel_id=1, source_target_pairs={{0,8},{4,12},{8,0},{12,4},{1,9},{5,13},{9,1},{13,5},{2,10},{6,14},... | collective-permute-start | bytes 663560 | tf_op jit(solution)/shard_map/ppermute | solution.py:348
  110.4 1.3 copy-start.3
  113.4 7.1 %collective-permute-start.21 = (bf16[64,768]{1,0:T(8,128)(2,1)S(1)}, bf16[64,768]{1,0:T(8,128)(2,1)S(1)}, u32[]{:S(2)}, u32[]{:S(2)}) collective-permute-start(bf16[64,768]{1,0:T(8,128)(2,1)S(1)} %get-tuple-element.69), channel_id=1, source_target_pairs={{0,1},{1,0},{2,3},{3,2},{4,5},{5,4},{6,7},{7,6},{8,9},{9,8},{10,11... | collective-permute-start | bytes 294920 | tf_op jit(solution)/shard_map/ppermute | solution.py:666
  113.4 7.1 %collective-permute-start.22 = (bf16[64,768]{1,0:T(8,128)(2,1)S(1)}, bf16[64,768]{1,0:T(8,128)(2,1)S(1)}, u32[]{:S(2)}, u32[]{:S(2)}) collective-permute-start(bf16[64,768]{1,0:T(8,128)(2,1)S(1)} %get-tuple-element.70), channel_id=1, source_target_pairs={{0,2},{1,3},{2,0},{3,1},{4,6},{5,7},{6,4},{7,5},{8,10},{9,11},{10,... | collective-permute-start | bytes 294920 | tf_op jit(solution)/shard_map/ppermute | solution.py:666
  114.2 6.3 %collective-permute-start.23 = (bf16[64,768]{1,0:T(8,128)(2,1)S(1)}, bf16[64,768]{1,0:T(8,128)(2,1)S(1)}, u32[]{:S(2)}, u32[]{:S(2)}) collective-permute-start(bf16[64,768]{1,0:T(8,128)(2,1)S(1)} %get-tuple-element.71), channel_id=1, source_target_pairs={{0,3},{1,2},{2,1},{3,0},{4,7},{5,6},{6,5},{7,4},{8,11},{9,10},{10,... | collective-permute-start | bytes 294920 | tf_op jit(solution)/shard_map/ppermute | solution.py:666
Sparse Core Ops, SparseCore 0:
  65.5 18.7 all-gather.2

commit v4 on v3

--- a/solution.py
+++ b/solution.py
@@ -46,11 +46,11 @@
     return lax.rem(value + count, count)
 
 
-def pack_kernel(slabs, rows, block_len, dest_hbm, kept_hbm, x_hbm, cot_ref, *refs):
-    outs, (dest_ref, kept_ref, x_ref, parts, sems) = refs[:slabs], refs[slabs:]
+def pack_kernel(slabs, rows, block_len, dest_hbm, kept_hbm, x_hbm, cot_hbm, *refs):
+    outs, (dest_ref, kept_ref, x_ref, cot_ref, parts, sems) = refs[:slabs], refs[slabs:]
     copies = [
         pltpu.make_async_copy(a, b, sems.at[n])
-        for n, (a, b) in enumerate(((dest_hbm, dest_ref), (kept_hbm, kept_ref), (x_hbm, x_ref)))
+        for n, (a, b) in enumerate(((dest_hbm, dest_ref), (kept_hbm, kept_ref), (x_hbm, x_ref), (cot_hbm, cot_ref)))
     ]
     for copy in copies:
         copy.start()
@@ -58,9 +58,7 @@
     copies[1].wait()
     me = lax.axis_index("seq")
     payload = CAP * block_len + 16
-    feat, count = parts.shape[1:]
-    for d in range(slabs):
-        parts[d] = cot_ref[:, d * count : (d + 1) * count]
+    feat, span = parts.shape[1:]
     dest = [jnp.where(dest_ref[r] >= slabs, -100, dest_ref[r]) for r in range(rows)]
     rank, total = [], []
     for r in range(rows):
@@ -89,6 +87,9 @@
     line = lax.broadcasted_iota(jnp.int32, (payload, 1), 0)
     base = CAP * block_len
     copies[2].wait()
+    copies[3].wait()
+    for d in range(slabs):
+        parts[d] = cot_ref[:, d * span : (d + 1) * span]
     x = x_ref[...]
     for k, out in enumerate(outs):
         to = wrap(me + k, slabs)
@@ -109,7 +110,7 @@
 
 
 def unpack_kernel(slabs, block_len, *refs):
-    ins, out, cot = refs[:slabs], refs[slabs], refs[slabs + 1]
+    ins, out = refs[:slabs], refs[slabs]
     me = lax.axis_index("seq")
     payload = CAP * block_len + 16
     base = CAP * block_len
@@ -124,8 +125,10 @@
     place = (col - slot * block_len).astype(F32)
     slot = slot.astype(F32)
     colf = col.astype(F32)
-    row = lax.broadcasted_iota(jnp.int32, out.shape[:1] + (payload,), 0).astype(F32)
-    total = jnp.zeros(out.shape, F32)
+    shape = (length + 16, out.shape[1])
+    row = lax.broadcasted_iota(jnp.int32, (shape[0], payload), 0).astype(F32)
+    total = jnp.zeros(shape, F32)
+    cot_rows = (out.shape[0] - shape[0]) // slabs
     for k in range(slabs):
         offsets = []
         for counts in (own, prev, following):
@@ -139,22 +142,22 @@
         left = jnp.where((prev[k] > 0.5) & (offsets[1] + prev[k] > slabs - 0.5), length + colf - base - EDGE, -1.0)
         key = jnp.where(col < base, main, jnp.where(col < base + EDGE, right, jnp.where(col < base + 2 * EDGE, left, -1.0)))
         total = total + dot(jnp.where(row == key, 1.0, 0.0).astype(BF), ins[k][:payload])
-        half, count = cot.shape[1] // 2, cot.shape[2]
-        piece = ins[k][payload:].astype(F32)
-        cot[k, :half] = piece[:, :count].astype(BF)
-        cot[k, half:] = piece[:, count:].astype(BF)
-    out[...] = total.astype(BF)
-
-
-def cot_kernel(slabs, chans, *refs):
+        out[shape[0] + k * cot_rows : shape[0] + (k + 1) * cot_rows] = ins[k][payload:]
+    out[: shape[0]] = total.astype(BF)
+
+
+def cot_kernel(slabs, chans, feat, *refs):
     ins, (w_ref, gain_ref, out, full) = refs[:chans], refs[chans:]
     me, ch = lax.axis_index("seq"), lax.axis_index("chan")
-    feat = ins[0].shape[1]
+    half, count = feat // 2, full.shape[1]
+    first = ins[0].shape[0] - slabs * half
     for j in range(chans):
         owner = lax.bitwise_xor(ch, j)
         for k in range(slabs):
             begin = pl.multiple_of((wrap(me - k, slabs) * chans + owner) * feat, 16)
-            full[pl.ds(begin, feat), :] = ins[j][k]
+            piece = ins[j][first + k * half : first + (k + 1) * half].astype(F32)
+            full[pl.ds(begin, half), :] = piece[:, :count].astype(BF)
+            full[pl.ds(begin + half, half), :] = piece[:, count:].astype(BF)
     out[...] = dot(full[...], w_ref[...], ((0,), (0,))) * gain_ref[...][None, :]
 
 
@@ -182,11 +185,12 @@
     xs, (w_ref, bias_ref, pooled_ref, slope_ref), rest = refs[:chans], refs[chans : chans + 4], refs[chans + 4 :]
     full, conv, shifted_sum, lanes = rest
     ch = lax.axis_index("chan")
-    rows, width = xs[0].shape
+    width = xs[0].shape[1]
     length = shifted_sum.shape[0]
+    rows = length + 16
     for j in range(chans):
         begin = pl.multiple_of(lax.bitwise_xor(ch, j) * width, 128)
-        full[:, pl.ds(begin, width)] = xs[j][...]
+        full[:, pl.ds(begin, width)] = xs[j][:rows]
     x = full[...]
     for t in range(KERNEL_TAPS):
         product = dot(x, w_ref[t])
@@ -233,7 +237,7 @@
 
 
 def grad_kernel(chans, *refs):
-    stats, (pooled_ref, slope_ref, dxhat_ref, gain_ref, low_ref, high_ref, twice) = refs[:chans], refs[chans:]
+    stats, (pooled_ref, slope_ref, dxhat_ref, gain_ref, low_ref, high_ref, head_ref, tail_ref, twice) = refs[:chans], refs[chans:]
     count, width = pooled_ref.shape
     total = stats[0][...]
     for s in stats[1:]:
@@ -256,6 +260,8 @@
     extra = low_ref.shape[0] - count
     low_ref[count:] = dy[:extra]
     high_ref[...] = dy[extra:]
+    head_ref[...] = dy[:16]
+    tail_ref[...] = dy[dy.shape[0] - 16 :]
 
 
 def dx_kernel(picks, *refs):
@@ -267,8 +273,8 @@
     upper = high_ref.shape[0]
     begin = low_ref.shape[0] - (length - upper)
     me = lax.axis_index("seq")
-    left = left_ref[upper - 16 : upper].astype(F32)[16 - EDGE :]
-    right = right_ref[begin : begin + 16].astype(F32)[:EDGE]
+    left = left_ref[...].astype(F32)[16 - EDGE :]
+    right = right_ref[...].astype(F32)[:EDGE]
     wide[0:EDGE] = jnp.where(me == 0, 0.0, left)
     wide[EDGE : EDGE + length - upper] = low_ref[begin:].astype(F32)
     wide[EDGE + length - upper : EDGE + length] = high_ref[...].astype(F32)
@@ -308,7 +314,7 @@
     lows = [r[dys[0].shape[0] - extra :] for r in dys[:half]]
     highs = [r[...] for r in dys[half:]]
     for k in range(slabs):
-        begin = pl.multiple_of(wrap(me - k, slabs) * length + 8, 8)
+        begin = pl.multiple_of(lax.bitwise_xor(me, k) * length + 8, 8)
         full[pl.ds(begin, extra), :] = lows[k].astype(F32)
         full[pl.ds(begin + extra, upper), :] = highs[k].astype(F32)
     xt = xt_ref[...]
@@ -327,7 +333,7 @@
     for j in range(chans):
         wide[pl.ds(pl.multiple_of(lax.bitwise_xor(ch, j) * feat, 8), feat), :] = cots[j][...]
     for k, rows in enumerate([r[:count] for r in normed]):
-        full[pl.ds(pl.multiple_of(wrap(me - k, slabs) * count, 8), count), :] = rows
+        full[pl.ds(pl.multiple_of(lax.bitwise_xor(me, k) * count, 8), count), :] = rows
     every = full[...]
     dw_ref[...] = dot(wide[...], every)
     rows = feat * chans
@@ -348,14 +354,10 @@
     return lax.ppermute(value, "seq", [(i, (i + k) % count) for i in range(count)]) if k else value
 
 
-def relay(value, count):
+def relay(value, count, axis):
     near = [(i, i ^ 1) for i in range(count)]
-    far = lax.ppermute(value, "chan", [(i, i ^ 2) for i in range(count)])
-    return [value, lax.ppermute(value, "chan", near), far, lax.ppermute(far, "chan", near)]
-
-
-def gather_seq(value, count):
-    return [turn(value, k, count) for k in range(count)]
+    far = lax.ppermute(value, axis, [(i, i ^ 2) for i in range(count)])
+    return [value, lax.ppermute(value, axis, near), far, lax.ppermute(far, axis, near)]
 
 
 def trade_seq(values, count):
@@ -534,16 +536,18 @@
         functools.partial(pack_kernel, slabs, rows, block_len),
         [struct((payload + feat // 2, width), BF)] * slabs,
         [dest_slab, kept_len, x_rows.reshape(rows * block_len, width), g_cot],
-        specs=[HBM, HBM, HBM, VMEM],
+        specs=[HBM] * 4,
         scratch=[
             pltpu.SMEM((rows,), jnp.int32),
             pltpu.SMEM((rows,), jnp.int32),
             pltpu.VMEM((rows * block_len, width), BF),
+            pltpu.VMEM((feat, positions), BF),
             pltpu.VMEM((slabs, feat, count), BF),
-            pltpu.SemaphoreType.DMA((3,)),
+            pltpu.SemaphoreType.DMA((4,)),
         ],
         flops=2 * payload * slabs * rows * block_len * width,
         moved=2 * payload * slabs * width,
+        room=60,
         name="pack",
     )
     arrived = trade_seq(packed, slabs)
@@ -560,25 +564,25 @@
         )
 
     taps_early = staged()
-    arrived, taps_early = lax.optimization_barrier((arrived, taps_early))
-
-    routed, cot_mine = launch(
+    cot_wide = swaps(after(g_cot, packed[0]), chans)
+    arrived, taps_early, cot_wide = lax.optimization_barrier((arrived, taps_early, cot_wide))
+
+    routed = launch(
         functools.partial(unpack_kernel, slabs, block_len),
-        [struct((padded_rows, width), BF), struct((slabs, feat, count), BF)],
+        struct((padded_rows + slabs * feat // 2, width), BF),
         arrived,
         flops=2 * payload * slabs * padded_rows * width,
         moved=2 * payload * slabs * width,
         name="unpack",
     )
-    x_all = relay(routed, chans)
+    x_all = relay(routed, chans, "chan")
     dxhat = launch(
-        functools.partial(cot_kernel, slabs, chans),
+        functools.partial(cot_kernel, slabs, chans, feat),
         struct((count, width), F32),
-        [*swaps(cot_mine, chans), w_proj, gain],
+        [*x_all, w_proj, gain],
         scratch=[pltpu.VMEM((feat * chans * slabs, count), BF)],
         name="cotangent",
     )
-    cot_wide = swaps(g_cot, chans)
     pieces = launch(
         functools.partial(quarter_kernel, slabs, chans), [struct((part, own), BF)] * slabs, x_all, name="quarter"
     )
@@ -602,9 +606,9 @@
     stats = launch(
         sums_kernel, struct((8, -(-count // 128) * 128), F32), [pooled, dxhat], name="sums"
     )
-    low, high = launch(
+    low, high, head, tail = launch(
         functools.partial(grad_kernel, chans),
-        [struct((count + extra, width), BF), struct((length - extra, width), BF)],
+        [struct((n, width), BF) for n in (count + extra, length - extra, 16, 16)],
         [*swaps(stats, chans), pooled, slope, dxhat, gain],
         scratch=[pltpu.VMEM((width // 128, length, 128), F32)],
         flops=20 * length * width,
@@ -619,18 +623,19 @@
         scratch=[pltpu.VMEM((length * slabs, own), BF)],
         name="turn_x",
     )
-    low_all = gather_seq(low, slabs)
-    high_all = gather_seq(high, slabs)
+    low_all = relay(low, slabs, "seq")
+    high_all = relay(high, slabs, "seq")
+    from_left, from_right = turn(tail, 1, slabs), turn(head, slabs - 1, slabs)
 
     taps_late = staged(low)
-    low_far = after(low, low_all[1], low_all[3], high_all[1], high_all[3], taps_late, cot_wide)
-    low_near = after(low_far, low_all[2])
+    low_far = after(low, low_all[1], low_all[2], taps_late)
+    low_near = after(low_far, low_all[3], high_all[2])
 
     def dx_part(low, picks, dtypes, name):
         return launch(
             functools.partial(dx_kernel, picks),
             [struct((width, length), d) for d in dtypes],
-            [low, high, high_all[1], low_all[3], taps_late],
+            [low, high, from_left, from_right, taps_late],
             scratch=[pltpu.VMEM((length + 2 * EDGE, width), F32), pltpu.VMEM((KERNEL_TAPS, length, width), BF)],
             flops=2 * len(picks) * length * width * width * KERNEL_TAPS,
             moved=2 * len(picks) * width * width * KERNEL_TAPS,
@@ -645,7 +650,6 @@
     across = lax.ppermute(across, "chan", over)
     beside, mine_dx = dx_part(low_near, (1, 0), (BF, F32), "dx_near")
     beside = lax.ppermute(beside, "chan", near)
-    dx_field = (mine_dx + beside.astype(F32) + across.astype(F32)).astype(BF)
 
     w_late, x_turned = lax.optimization_barrier((w_proj, x_turned))
     proj = launch(
@@ -674,7 +678,8 @@
         moved=4 * own * width * KERNEL_TAPS,
         name="dw",
     )
-    qk_got, dw_taps = lax.optimization_barrier((qk_got, dw_taps))
+    qk_got, beside, across, dw_taps = lax.optimization_barrier((qk_got, beside, across, dw_taps))
+    dx_field = (mine_dx + beside.astype(F32) + across.astype(F32)).astype(BF)
     qk_sum = qk_parts[0]
     for got in qk_got:
         qk_sum = qk_sum + got.astype(F32)

time: 128 us -> 113 us (0.88)
  waiting for transfers between devices: 50.2 us -> 35.4 us
  local copies, waits for them, and re-layouts: 9.84 us -> 6.74 us
  Pallas kernels: 19.4 us -> 21.6 us
  other arithmetic: 2.32 us -> 4.08 us
    ppermute x3 -> x9, waiting for transfers between devices: 7.61 us -> 25.1 us  [the longest x3 18.4 us: relay(): far = lax.ppermute(value, axis, [(i, i ^ 2) for i in range(count)])]
    ppermute x12 -> x8, waiting for transfers between devices: 18.2 us -> 4.78 us  [turn(): lax.ppermute(value, 'seq', [(i, (i + k) % count) for i in range(count)])]
    ppermute x9 -> x6, waiting for transfers between devices: 15.9 us -> 4.23 us  [swaps(): lax.ppermute(value, 'chan', [(i, i ^ j) for i in range(count)])]
    ppermute x1, waiting for transfers between devices: 7.97 us -> 0.01 us  [per_device(): across = lax.ppermute(across, 'chan', over)]
    ppermute x3 -> x9, starting transfers between devices: 1.55 us -> 6.41 us  [the longest x3 3.37 us: relay(): far = lax.ppermute(value, axis, [(i, i ^ 2) for i in range(count)])]
    ppermute x12 -> x8, starting transfers between devices: 21.7 us -> 17.4 us  [turn(): lax.ppermute(value, 'seq', [(i, (i + k) % count) for i in range(count)])]
    unnamed x22 -> x16, local copies, waits for them, and re-layouts: 9.84 us -> 6.74 us
    pallas_call x14, Pallas kernels: 19.4 us -> 21.6 us  [launch(): pl.pallas_call(body, out_shape=outs, in_specs=specs or [VMEM] * len(ins),...]
  transfers between devices with their start and end apart: 31 -> 30, of which waited for: 14 -> 12; matrix products, arithmetic and copies ran while one was open for 1% -> 1% of each run, Pallas kernels for 14% -> 16%
where the time goes in v4:
time: 113 us
  waiting for transfers between devices  35.4 us (31%)
  starting transfers between devices  30.9 us (27%)
  Pallas kernels  21.6 us (19%)
  between operations  14.3 us (13%)
  local copies, waits for them, and re-layouts  6.74 us (6%)
  other arithmetic  4.08 us (4%)
    pallas_call x14, Pallas kernels, launch(): pl.pallas_call(body, out_shape=outs, in_specs=specs or [VMEM] * len(ins),...  21.6 us
    ppermute x3, waiting for transfers between devices, relay(): far = lax.ppermute(value, axis, [(i, i ^ 2) for i in range(count)])  18.4 us
    ppermute x8, starting transfers between devices, turn(): lax.ppermute(value, 'seq', [(i, (i + k) % count) for i in range(count)])  17.4 us
    unnamed x16, local copies, waits for them, and re-layouts  6.74 us
    ppermute x3, waiting for transfers between devices, relay(): lax.ppermute(far, axis, near)  5.3 us
    ppermute x8, waiting for transfers between devices, turn(): lax.ppermute(value, 'seq', [(i, (i + k) % count) for i in range(count)])  4.78 us
    ppermute x6, starting transfers between devices, swaps(): lax.ppermute(value, 'chan', [(i, i ^ j) for i in range(count)])  4.47 us
    ppermute x6, waiting for transfers between devices, swaps(): lax.ppermute(value, 'chan', [(i, i ^ j) for i in range(count)])  4.23 us
  transfers between devices with their start and end apart: 30, of which 12 were waited for; matrix products, arithmetic and copies ran while one was open for 1% of the time, Pallas kernels for 16%

profile of v4, /device:TPU:0, one launch (start us, length us, event | category | flops | bytes accessed | tf_op | source)
XLA Modules:
  0.0 113.0 jit_solution(12816993684279196308)
XLA Ops:
  7.2 0.0 all-gather.3.cloned.1.call-start
  7.2 2.4 %pack.1 = (bf16[240,384]{1,0:T(8,128)(2,1)}, bf16[240,384]{1,0:T(8,128)(2,1)}, bf16[240,384]{1,0:T(8,128)(2,1)}, bf16[240,384]{1,0:T(8,128)(2,1)}) custom-call(s32[5]{0:T(128)} %dest_hbm.1, s32[5]{0:T(128)} %kept_hbm.1, bf16[480,384]{1,0:T(8,128)(2,1)} %bitcast.15, bf16[64,768]{1,0:T(8,128)(2,1)} %refs_0_), custom_call_target="tpu_custom_call" | custom-call | flops 306708480 | bytes 638976 | tf_op jit(solution)/shard_map/pack/pallas_call | solution.py:29
  9.6 0.5 collective-permute-start.3
  10.2 2.6 %collective-permute-start = (bf16[240,384]{1,0:T(8,128)(2,1)}, bf16[240,384]{1,0:T(8,128)(2,1)S(1)}, u32[]{:S(2)}, u32[]{:S(2)}) collective-permute-start(bf16[240,384]{1,0:T(8,128)(2,1)} %get-tuple-element.53), channel_id=1, source_target_pairs={{0,4},{4,8},{8,12},{12,0},{1,5},{5,9},{9,13},{13,1},{2,6},{6,10},{... | collective-permute-start | bytes 552968 | tf_op jit(solution)/shard_map/ppermute | solution.py:354
  12.8 2.6 %collective-permute-start.1 = (bf16[240,384]{1,0:T(8,128)(2,1)}, bf16[240,384]{1,0:T(8,128)(2,1)S(1)}, u32[]{:S(2)}, u32[]{:S(2)}) collective-permute-start(bf16[240,384]{1,0:T(8,128)(2,1)} %get-tuple-element.54), channel_id=1, source_target_pairs={{0,8},{4,12},{8,0},{12,4},{1,9},{5,13},{9,1},{13,5},{2,10},{6,14},... | collective-permute-start | bytes 552968 | tf_op jit(solution)/shard_map/ppermute | solution.py:354
  15.4 1.3 %collective-permute-start.2 = (bf16[240,384]{1,0:T(8,128)(2,1)}, bf16[240,384]{1,0:T(8,128)(2,1)S(1)}, u32[]{:S(2)}, u32[]{:S(2)}) collective-permute-start(bf16[240,384]{1,0:T(8,128)(2,1)} %get-tuple-element.55), channel_id=1, source_target_pairs={{0,12},{4,0},{8,4},{12,8},{1,13},{5,1},{9,5},{13,9},{2,14},{6,2},{... | collective-permute-start | bytes 552968 | tf_op jit(solution)/shard_map/ppermute | solution.py:354
  16.7 1.5 %collective-permute-start.4 = (bf16[64,768]{1,0:T(8,128)(2,1)}, bf16[64,768]{1,0:T(8,128)(2,1)S(1)}, u32[]{:S(2)}, u32[]{:S(2)}) collective-permute-start(bf16[64,768]{1,0:T(8,128)(2,1)} %refs_0_), channel_id=1, source_target_pairs={{0,2},{1,3},{2,0},{3,1},{4,6},{5,7},{6,4},{7,5},{8,10},{9,11},{10,... | collective-permute-start | bytes 294920 | tf_op jit(solution)/shard_map/ppermute | solution.py:350
  18.2 0.0 collective-permute-start.5
  18.2 2.7 %copy-done = bf16[1536,5,384]{2,0,1:T(8,128)(2,1)S(1)} copy-done((bf16[1536,5,384]{2,0,1:T(8,128)(2,1)S(1)}, bf16[1536,5,384]{2,0,1:T(8,128)(2,1)}, u32[]{:S(2)}) %copy-start) | copy-done | bytes 5898264
  20.9 0.6 stage.2.refs_4_
  21.5 0.0 copy-start.2
  21.5 0.0 copy-start.6
  21.5 0.2 collective-permute-done.4.refs_2_
  21.7 1.8 %collective-permute-done.5.refs_3_ = bf16[64,768]{1,0:T(8,128)(2,1)S(1)} collective-permute-done((bf16[64,768]{1,0:T(8,128)(2,1)}, bf16[64,768]{1,0:T(8,128)(2,1)S(1)}, u32[]{:S(2)}, u32[]{:S(2)}) %collective-permute-start.5) | collective-permute-done | bytes 98336 | tf_op jit(solution)/shard_map/ppermute | solution.py:350
  23.5 4.8 %collective-permute-done.1.refs_2_ = bf16[240,384]{1,0:T(8,128)(2,1)S(1)} collective-permute-done((bf16[240,384]{1,0:T(8,128)(2,1)}, bf16[240,384]{1,0:T(8,128)(2,1)S(1)}, u32[]{:S(2)}, u32[]{:S(2)}) %collective-permute-start.1) | collective-permute-done | bytes 184352 | tf_op jit(solution)/shard_map/ppermute | solution.py:354
  28.3 0.6 unpack.1.refs_0_
  28.9 1.6 %collective-permute-start.7 = (bf16[528,384]{1,0:T(8,128)(2,1)S(1)}, bf16[528,384]{1,0:T(8,128)(2,1)S(1)}, u32[]{:S(2)}, u32[]{:S(2)}) collective-permute-start(bf16[528,384]{1,0:T(8,128)(2,1)S(1)} %unpack.1.refs_0_), channel_id=1, source_target_pairs={{0,2},{1,3},{2,0},{3,1},{4,6},{5,7},{6,4},{7,5},{8,10},{9,11},{10,... | collective-permute-start | bytes 1216520 | tf_op jit(solution)/shard_map/ppermute | solution.py:359
  30.5 9.7 %collective-permute-done.7.refs_2_ = bf16[528,384]{1,0:T(8,128)(2,1)S(1)} collective-permute-done((bf16[528,384]{1,0:T(8,128)(2,1)S(1)}, bf16[528,384]{1,0:T(8,128)(2,1)S(1)}, u32[]{:S(2)}, u32[]{:S(2)}) %collective-permute-start.7) | collective-permute-done | bytes 405536 | tf_op jit(solution)/shard_map/ppermute | solution.py:359
  40.2 1.7 %collective-permute-done.8.refs_3_ = bf16[528,384]{1,0:T(8,128)(2,1)S(1)} collective-permute-done((bf16[528,384]{1,0:T(8,128)(2,1)S(1)}, bf16[528,384]{1,0:T(8,128)(2,1)S(1)}, u32[]{:S(2)}, u32[]{:S(2)}) %collective-permute-start.8) | collective-permute-done | bytes 405536 | tf_op jit(solution)/shard_map/ppermute | solution.py:360
  42.0 0.1 quarter.1
  42.0 4.6 %collective-permute-start.15 = (bf16[96,384]{1,0:T(8,128)(2,1)S(1)}, bf16[96,384]{1,0:T(8,128)(2,1)S(1)}, u32[]{:S(2)}, u32[]{:S(2)}) collective-permute-start(bf16[96,384]{1,0:T(8,128)(2,1)S(1)} %get-tuple-element.70), channel_id=1, source_target_pairs={{0,4},{4,8},{8,12},{12,0},{1,5},{5,9},{9,13},{13,1},{2,6},{6,10},{... | collective-permute-start | bytes 221192 | tf_op jit(solution)/shard_map/ppermute | solution.py:354
  46.6 1.2 %collective-permute-start.16 = (bf16[96,384]{1,0:T(8,128)(2,1)S(1)}, bf16[96,384]{1,0:T(8,128)(2,1)S(1)}, u32[]{:S(2)}, u32[]{:S(2)}) collective-permute-start(bf16[96,384]{1,0:T(8,128)(2,1)S(1)} %get-tuple-element.71), channel_id=1, source_target_pairs={{0,8},{4,12},{8,0},{12,4},{1,9},{5,13},{9,1},{13,5},{2,10},{6,14},... | collective-permute-start | bytes 221192 | tf_op jit(solution)/shard_map/ppermute | solution.py:354
  47.8 1.2 %collective-permute-start.17 = (bf16[96,384]{1,0:T(8,128)(2,1)S(1)}, bf16[96,384]{1,0:T(8,128)(2,1)S(1)}, u32[]{:S(2)}, u32[]{:S(2)}) collective-permute-start(bf16[96,384]{1,0:T(8,128)(2,1)S(1)} %get-tuple-element.72), channel_id=1, source_target_pairs={{0,12},{4,0},{8,4},{12,8},{1,13},{5,1},{9,5},{13,9},{2,14},{6,2},{... | collective-permute-start | bytes 221192 | tf_op jit(solution)/shard_map/ppermute | solution.py:354
  49.0 3.9 %conv.1 = (f32[192,384]{1,0:T(8,128)S(1)}, f32[384,384]{1,0:T(8,128)S(1)}) custom-call(bf16[528,384]{1,0:T(8,128)(2,1)S(1)} %unpack.1.refs_0_, bf16[528,384]{1,0:T(8,128)(2,1)S(1)} %collective-permute-done.6.refs_1_, bf16[528,384]{1,0:T(8,128)(2,1)S(1)} %collective-permute-done.7.refs_2_, bf16[528,384]{1,0:T(8,128)(2,1)S(1)} %collective-permute-done.8.refs_3_, ...), custom_call_target="tpu_custom_call" | custom-call | flops 2359296000 | bytes 5898240 | tf_op jit(solution)/shard_map/conv/pallas_call | solution.py:29
  53.0 0.5 cotangent.1.dxhat_ref.refs_6_
  53.5 0.2 sums.1.refs_0_
  53.8 0.0 collective-permute-start.9
  53.8 1.6 %collective-permute-start.10 = (f32[8,256]{1,0:T(8,128)S(1)}, f32[8,256]{1,0:T(8,128)S(1)}, u32[]{:S(2)}, u32[]{:S(2)}) collective-permute-start(f32[8,256]{1,0:T(8,128)S(1)} %sums.1.refs_0_), channel_id=1, source_target_pairs={{0,2},{1,3},{2,0},{3,1},{4,6},{5,7},{6,4},{7,5},{8,10},{9,11},{10,... | collective-permute-start | bytes 24584 | tf_op jit(solution)/shard_map/ppermute | solution.py:350
  55.4 0.9 collective-permute-start.11
  56.2 1.3 %collective-permute-done.10.refs_2_ = f32[8,256]{1,0:T(8,128)S(1)} collective-permute-done((f32[8,256]{1,0:T(8,128)S(1)}, f32[8,256]{1,0:T(8,128)S(1)}, u32[]{:S(2)}, u32[]{:S(2)}) %collective-permute-start.10) | collective-permute-done | bytes 8224 | tf_op jit(solution)/shard_map/ppermute | solution.py:350
  57.5 0.9 collective-permute-done.11.refs_3_
  58.4 0.6 gradient.1
  59.1 0.8 pad_maximum_fusion
  59.8 0.0 all-gather.3.cloned.1.call-update
  59.9 0.8 collective-permute-start.12
  60.7 1.7 %collective-permute-start.13 = (bf16[288,384]{1,0:T(8,128)(2,1)S(1)}, bf16[288,384]{1,0:T(8,128)(2,1)S(1)}, u32[]{:S(2)}, u32[]{:S(2)}) collective-permute-start(bf16[288,384]{1,0:T(8,128)(2,1)S(1)} %get-tuple-element.85.refs_4_.refs_0_.refs_1_), channel_id=1, source_target_pairs={{0,8},{4,12},{8,0},{12,4},{1,9},{5,13},{9,1},{13,5},{2,10},{6,14},... | collective-permute-start | bytes 663560 | tf_op jit(solution)/shard_map/ppermute | solution.py:359
  62.4 0.1 collective-permute-start.22
  62.5 3.7 %collective-permute-start.23 = (bf16[16,384]{1,0:T(8,128)(2,1)S(1)}, bf16[16,384]{1,0:T(8,128)(2,1)S(1)}, u32[]{:S(2)}, u32[]{:S(2)}) collective-permute-start(bf16[16,384]{1,0:T(8,128)(2,1)S(1)} %get-tuple-element.87), channel_id=1, source_target_pairs={{0,12},{4,0},{8,4},{12,8},{1,13},{5,1},{9,5},{13,9},{2,14},{6,2},{... | collective-permute-start | bytes 36872 | tf_op jit(solution)/shard_map/ppermute | solution.py:354
  66.3 2.8 %copy-done.1 = bf16[1536,5,384]{2,0,1:T(8,128)(2,1)S(1)} copy-done((bf16[1536,5,384]{2,0,1:T(8,128)(2,1)S(1)}, bf16[1536,5,384]{2,0,1:T(8,128)(2,1)}, u32[]{:S(2)}) %copy-start.1) | copy-done | bytes 5898264
  69.0 0.6 stage.3.refs_4_
  69.6 0.1 collective-permute-start.21
  69.7 1.5 %collective-permute-done.12.refs_5_.refs_2_ = bf16[288,384]{1,0:T(8,128)(2,1)S(1)} collective-permute-done((bf16[288,384]{1,0:T(8,128)(2,1)S(1)}, bf16[288,384]{1,0:T(8,128)(2,1)S(1)}, u32[]{:S(2)}, u32[]{:S(2)}) %collective-permute-start.12) | collective-permute-done | bytes 221216 | tf_op jit(solution)/shard_map/ppermute | solution.py:360
  71.2 8.6 %collective-permute-done.13.refs_6_.refs_3_ = bf16[288,384]{1,0:T(8,128)(2,1)S(1)} collective-permute-done((bf16[288,384]{1,0:T(8,128)(2,1)S(1)}, bf16[288,384]{1,0:T(8,128)(2,1)S(1)}, u32[]{:S(2)}, u32[]{:S(2)}) %collective-permute-start.13) | collective-permute-done | bytes 221216 | tf_op jit(solution)/shard_map/ppermute | solution.py:359
  79.8 2.1 %dx_far.1 = (bf16[384,384]{1,0:T(8,128)(2,1)S(1)}, f32[384,384]{1,0:T(8,128)S(1)}) custom-call(bf16[288,384]{1,0:T(8,128)(2,1)S(1)} %get-tuple-element.85.refs_4_.refs_0_.refs_1_, bf16[288,384]{1,0:T(8,128)(2,1)S(1)} %get-tuple-element.84.refs_1_.refs_5_, bf16[16,384]{1,0:T(8,128)(2,1)S(1)} %collective-permute-done.22.refs_2_, ...), custom_call_target="tpu_custom_call" | custom-call | flops 1132462080 | bytes 2949120 | tf_op jit(solution)/shard_map/dx_far/pallas_call | solution.py:29
  81.9 0.0 copy-start.5
  81.9 0.1 collective-permute-start.25
  82.0 2.1 %collective-permute-start.27 = (bf16[288,384]{1,0:T(8,128)(2,1)S(1)}, bf16[288,384]{1,0:T(8,128)(2,1)}, u32[]{:S(2)}, u32[]{:S(2)}) collective-permute-start(bf16[288,384]{1,0:T(8,128)(2,1)S(1)} %get-tuple-element.84.refs_1_.refs_5_), channel_id=1, source_target_pairs={{0,4},{4,0},{8,12},{12,8},{1,5},{5,1},{9,13},{13,9},{2,6},{6,2},{1... | collective-permute-start | bytes 663560 | tf_op jit(solution)/shard_map/ppermute | solution.py:360
  84.1 0.1 collective-permute-start.28
  84.2 3.0 %collective-permute-done.14.refs_7_.refs_4_ = bf16[288,384]{1,0:T(8,128)(2,1)S(1)} collective-permute-done((bf16[288,384]{1,0:T(8,128)(2,1)S(1)}, bf16[288,384]{1,0:T(8,128)(2,1)S(1)}, u32[]{:S(2)}, u32[]{:S(2)}) %collective-permute-start.14) | collective-permute-done | bytes 221216 | tf_op jit(solution)/shard_map/ppermute | solution.py:360
  87.2 2.1 %dx_near.1 = (bf16[384,384]{1,0:T(8,128)(2,1)S(1)}, f32[384,384]{1,0:T(8,128)S(1)}) custom-call(bf16[288,384]{1,0:T(8,128)(2,1)S(1)} %get-tuple-element.85.refs_4_.refs_0_.refs_1_, bf16[288,384]{1,0:T(8,128)(2,1)S(1)} %get-tuple-element.84.refs_1_.refs_5_, bf16[16,384]{1,0:T(8,128)(2,1)S(1)} %collective-permute-done.22.refs_2_, ...), custom_call_target="tpu_custom_call" | custom-call | flops 1132462080 | bytes 2949120 | tf_op jit(solution)/shard_map/dx_near/pallas_call | solution.py:29
  89.3 0.1 collective-permute-start.24
  89.4 0.8 add_convert_fusion.1
  90.2 1.1 collective-permute-start.26
  91.3 1.3 %copy-done.3 = bf16[16,96,384]{2,1,0:T(8,128)(2,1)S(1)} copy-done((bf16[16,96,384]{2,1,0:T(8,128)(2,1)S(1)}, bf16[16,96,384]{2,1,0:T(8,128)(2,1)}, u32[]{:S(2)}) %copy-start.3) | copy-done | bytes 1179672
  92.6 0.5 turn_x.1.refs_0_
  93.0 1.2 %projection.1 = (f32[256,384]{1,0:T(8,128)}, f32[64,768]{1,0:T(8,128)S(1)}, bf16[64,768]{1,0:T(8,128)(2,1)S(1)}, bf16[64,768]{1,0:T(8,128)(2,1)S(1)}, bf16[64,768]{1,0:T(8,128)(2,1)S(1)}) custom-call(bf16[64,768]{1,0:T(8,128)(2,1)S(1)} %copy-done.5, bf16[64,768]{1,0:T(8,128)(2,1)S(1)} %collective-permute-done.3.refs_1_, ...), custom_call_target="tpu_custom_call" | custom-call | flops 301989888 | bytes 393216 | tf_op jit(solution)/shard_map/projection/pallas_call | solution.py:29
  94.2 0.2 collective-permute-start.18
  94.5 0.9 collective-permute-start.19
  95.4 0.5 collective-permute-done.28.refs_8_
  95.9 0.2 collective-permute-start.20
  96.1 6.2 %dw.1 = f32[5,384,384]{2,1,0:T(8,128)} custom-call(bf16[384,1536]{1,0:T(8,128)(2,1)S(1)} %turn_x.1.refs_0_, bf16[288,384]{1,0:T(8,128)(2,1)S(1)} %get-tuple-element.85.refs_4_.refs_0_.refs_1_, bf16[288,384]{1,0:T(8,128)(2,1)S(1)} %collective-permute-done.12.refs_5_.refs_2_, bf16[288,384]{1,0:T(8,128)(2,1)S(1)} %collective-permute-done.13.refs_6_.refs_3_, ...), custom_call_target="tpu_custom_call" | custom-call | flops 2264924160 | bytes 2949120 | tf_op jit(solution)/shard_map/dw/pallas_call | solution.py:29
  102.3 1.3 %collective-permute-done.20 = bf16[64,768]{1,0:T(8,128)(2,1)S(1)} collective-permute-done((bf16[64,768]{1,0:T(8,128)(2,1)S(1)}, bf16[64,768]{1,0:T(8,128)(2,1)S(1)}, u32[]{:S(2)}, u32[]{:S(2)}) %collective-permute-start.20) | collective-permute-done | bytes 98336 | tf_op jit(solution)/shard_map/ppermute | solution.py:670
  103.6 1.9 %add_convert_fusion = bf16[384,384]{1,0:T(8,128)(2,1)} fusion(bf16[384,384]{1,0:T(8,128)(2,1)} %collective-permute-done.26, f32[384,384]{1,0:T(8,128)S(1)} %get-tuple-element.97, bf16[384,384]{1,0:T(8,128)(2,1)} %collective-permute-done.24), kind=kLoop, calls=%fused_computation | loop fusion | flops 737280 | bytes 1474560 | tf_op jit(solution)/shard_map/convert_element_type | solution.py:682
  105.5 0.7 add_convert_fusion.2
  (31 shorter events, 0.1 us)
Async XLA Ops:
  7.2 84.1 %all-gather.3.cloned.1.call-start = ((), (), s32[]{:S(2)}) async-start(), calls=%async_computation | async-start | bytes 1474560 | tf_op jit(solution)/shard_map/all_gather | solution.py:618
  9.6 8.6 %collective-permute-start.3 = (bf16[64,768]{1,0:T(8,128)(2,1)}, bf16[64,768]{1,0:T(8,128)(2,1)S(1)}, u32[]{:S(2)}, u32[]{:S(2)}) collective-permute-start(bf16[64,768]{1,0:T(8,128)(2,1)} %refs_0_), channel_id=1, source_target_pairs={{0,1},{1,0},{2,3},{3,2},{4,5},{5,4},{6,7},{7,6},{8,9},{9,8},{10,11... | collective-permute-start | bytes 294920 | tf_op jit(solution)/shard_map/ppermute | solution.py:350
  10.2 13.4 %collective-permute-start = (bf16[240,384]{1,0:T(8,128)(2,1)}, bf16[240,384]{1,0:T(8,128)(2,1)S(1)}, u32[]{:S(2)}, u32[]{:S(2)}) collective-permute-start(bf16[240,384]{1,0:T(8,128)(2,1)} %get-tuple-element.53), channel_id=1, source_target_pairs={{0,4},{4,8},{8,12},{12,0},{1,5},{5,9},{9,13},{13,1},{2,6},{6,10},{... | collective-permute-start | bytes 552968 | tf_op jit(solution)/shard_map/ppermute | solution.py:354
  12.8 15.5 %collective-permute-start.1 = (bf16[240,384]{1,0:T(8,128)(2,1)}, bf16[240,384]{1,0:T(8,128)(2,1)S(1)}, u32[]{:S(2)}, u32[]{:S(2)}) collective-permute-start(bf16[240,384]{1,0:T(8,128)(2,1)} %get-tuple-element.54), channel_id=1, source_target_pairs={{0,8},{4,12},{8,0},{12,4},{1,9},{5,13},{9,1},{13,5},{2,10},{6,14},... | collective-permute-start | bytes 552968 | tf_op jit(solution)/shard_map/ppermute | solution.py:354
  15.4 12.9 %collective-permute-start.2 = (bf16[240,384]{1,0:T(8,128)(2,1)}, bf16[240,384]{1,0:T(8,128)(2,1)S(1)}, u32[]{:S(2)}, u32[]{:S(2)}) collective-permute-start(bf16[240,384]{1,0:T(8,128)(2,1)} %get-tuple-element.55), channel_id=1, source_target_pairs={{0,12},{4,0},{8,4},{12,8},{1,13},{5,1},{9,5},{13,9},{2,14},{6,2},{... | collective-permute-start | bytes 552968 | tf_op jit(solution)/shard_map/ppermute | solution.py:354
  16.7 5.0 %collective-permute-start.4 = (bf16[64,768]{1,0:T(8,128)(2,1)}, bf16[64,768]{1,0:T(8,128)(2,1)S(1)}, u32[]{:S(2)}, u32[]{:S(2)}) collective-permute-start(bf16[64,768]{1,0:T(8,128)(2,1)} %refs_0_), channel_id=1, source_target_pairs={{0,2},{1,3},{2,0},{3,1},{4,6},{5,7},{6,4},{7,5},{8,10},{9,11},{10,... | collective-permute-start | bytes 294920 | tf_op jit(solution)/shard_map/ppermute | solution.py:350
  18.2 5.3 %collective-permute-start.5 = (bf16[64,768]{1,0:T(8,128)(2,1)}, bf16[64,768]{1,0:T(8,128)(2,1)S(1)}, u32[]{:S(2)}, u32[]{:S(2)}) collective-permute-start(bf16[64,768]{1,0:T(8,128)(2,1)} %refs_0_), channel_id=1, source_target_pairs={{0,3},{1,2},{2,1},{3,0},{4,7},{5,6},{6,5},{7,4},{8,11},{9,10},{10,... | collective-permute-start | bytes 294920 | tf_op jit(solution)/shard_map/ppermute | solution.py:350
  18.2 2.7 %copy-start = (bf16[1536,5,384]{2,0,1:T(8,128)(2,1)S(1)}, bf16[1536,5,384]{2,0,1:T(8,128)(2,1)}, u32[]{:S(2)}) copy-start(bf16[1536,5,384]{2,0,1:T(8,128)(2,1)} %param.11) | copy-start | bytes 17694724
  20.9 7.4 %copy-start.4 = (bf16[240,384]{1,0:T(8,128)(2,1)S(1)}, bf16[240,384]{1,0:T(8,128)(2,1)}, u32[]{:S(2)}) copy-start(bf16[240,384]{1,0:T(8,128)(2,1)} %get-tuple-element.61.refs_0_) | copy-start | bytes 552964
  20.9 28.1 %copy-start.7 = (f32[384]{0:T(512)S(1)}, f32[384]{0:T(512)}, u32[]{:S(2)}) copy-start(f32[384]{0:T(512)} %refs_5_.2) | copy-start | bytes 4612
  21.5 31.5 %copy-start.2 = (bf16[1024,384]{1,0:T(8,128)(2,1)S(1)}, bf16[1024,384]{1,0:T(8,128)(2,1)}, u32[]{:S(2)}) copy-start(bf16[1024,384]{1,0:T(8,128)(2,1)} %refs_8_) | copy-start | bytes 2359300
  21.5 31.5 %copy-start.6 = (f32[384]{0:T(512)S(1)}, f32[384]{0:T(512)}, u32[]{:S(2)}) copy-start(f32[384]{0:T(512)} %refs_7_.1) | copy-start | bytes 4612
  28.9 11.3 %collective-permute-start.7 = (bf16[528,384]{1,0:T(8,128)(2,1)S(1)}, bf16[528,384]{1,0:T(8,128)(2,1)S(1)}, u32[]{:S(2)}, u32[]{:S(2)}) collective-permute-start(bf16[528,384]{1,0:T(8,128)(2,1)S(1)} %unpack.1.refs_0_), channel_id=1, source_target_pairs={{0,2},{1,3},{2,0},{3,1},{4,6},{5,7},{6,4},{7,5},{8,10},{9,11},{10,... | collective-permute-start | bytes 1216520 | tf_op jit(solution)/shard_map/ppermute | solution.py:359
  30.5 9.8 %collective-permute-start.6 = (bf16[528,384]{1,0:T(8,128)(2,1)S(1)}, bf16[528,384]{1,0:T(8,128)(2,1)S(1)}, u32[]{:S(2)}, u32[]{:S(2)}) collective-permute-start(bf16[528,384]{1,0:T(8,128)(2,1)S(1)} %unpack.1.refs_0_), channel_id=1, source_target_pairs={{0,1},{1,0},{2,3},{3,2},{4,5},{5,4},{6,7},{7,6},{8,9},{9,8},{10,11... | collective-permute-start | bytes 1216520 | tf_op jit(solution)/shard_map/ppermute | solution.py:360
  40.2 1.7 %collective-permute-start.8 = (bf16[528,384]{1,0:T(8,128)(2,1)S(1)}, bf16[528,384]{1,0:T(8,128)(2,1)S(1)}, u32[]{:S(2)}, u32[]{:S(2)}) collective-permute-start(bf16[528,384]{1,0:T(8,128)(2,1)S(1)} %collective-permute-done.7.refs_2_), channel_id=1, source_target_pairs={{0,1},{1,0},{2,3},{3,2},{4,5},{5,4},{6,7},{7,6},{8,9},{9,8},{10,11... | collective-permute-start | bytes 1216520 | tf_op jit(solution)/shard_map/ppermute | solution.py:360
  42.0 17.0 %collective-permute-start.15 = (bf16[96,384]{1,0:T(8,128)(2,1)S(1)}, bf16[96,384]{1,0:T(8,128)(2,1)S(1)}, u32[]{:S(2)}, u32[]{:S(2)}) collective-permute-start(bf16[96,384]{1,0:T(8,128)(2,1)S(1)} %get-tuple-element.70), channel_id=1, source_target_pairs={{0,4},{4,8},{8,12},{12,0},{1,5},{5,9},{9,13},{13,1},{2,6},{6,10},{... | collective-permute-start | bytes 221192 | tf_op jit(solution)/shard_map/ppermute | solution.py:354
  46.6 12.5 %collective-permute-start.16 = (bf16[96,384]{1,0:T(8,128)(2,1)S(1)}, bf16[96,384]{1,0:T(8,128)(2,1)S(1)}, u32[]{:S(2)}, u32[]{:S(2)}) collective-permute-start(bf16[96,384]{1,0:T(8,128)(2,1)S(1)} %get-tuple-element.71), channel_id=1, source_target_pairs={{0,8},{4,12},{8,0},{12,4},{1,9},{5,13},{9,1},{13,5},{2,10},{6,14},... | collective-permute-start | bytes 221192 | tf_op jit(solution)/shard_map/ppermute | solution.py:354
  47.8 11.3 %collective-permute-start.17 = (bf16[96,384]{1,0:T(8,128)(2,1)S(1)}, bf16[96,384]{1,0:T(8,128)(2,1)S(1)}, u32[]{:S(2)}, u32[]{:S(2)}) collective-permute-start(bf16[96,384]{1,0:T(8,128)(2,1)S(1)} %get-tuple-element.72), channel_id=1, source_target_pairs={{0,12},{4,0},{8,4},{12,8},{1,13},{5,1},{9,5},{13,9},{2,14},{6,2},{... | collective-permute-start | bytes 221192 | tf_op jit(solution)/shard_map/ppermute | solution.py:354
  53.8 1.6 %collective-permute-start.9 = (f32[8,256]{1,0:T(8,128)S(1)}, f32[8,256]{1,0:T(8,128)S(1)}, u32[]{:S(2)}, u32[]{:S(2)}) collective-permute-start(f32[8,256]{1,0:T(8,128)S(1)} %sums.1.refs_0_), channel_id=1, source_target_pairs={{0,1},{1,0},{2,3},{3,2},{4,5},{5,4},{6,7},{7,6},{8,9},{9,8},{10,11... | collective-permute-start | bytes 24584 | tf_op jit(solution)/shard_map/ppermute | solution.py:350
  53.8 3.7 %collective-permute-start.10 = (f32[8,256]{1,0:T(8,128)S(1)}, f32[8,256]{1,0:T(8,128)S(1)}, u32[]{:S(2)}, u32[]{:S(2)}) collective-permute-start(f32[8,256]{1,0:T(8,128)S(1)} %sums.1.refs_0_), channel_id=1, source_target_pairs={{0,2},{1,3},{2,0},{3,1},{4,6},{5,7},{6,4},{7,5},{8,10},{9,11},{10,... | collective-permute-start | bytes 24584 | tf_op jit(solution)/shard_map/ppermute | solution.py:350
  55.4 3.1 %collective-permute-start.11 = (f32[8,256]{1,0:T(8,128)S(1)}, f32[8,256]{1,0:T(8,128)S(1)}, u32[]{:S(2)}, u32[]{:S(2)}) collective-permute-start(f32[8,256]{1,0:T(8,128)S(1)} %sums.1.refs_0_), channel_id=1, source_target_pairs={{0,3},{1,2},{2,1},{3,0},{4,7},{5,6},{6,5},{7,4},{8,11},{9,10},{10,... | collective-permute-start | bytes 24584 | tf_op jit(solution)/shard_map/ppermute | solution.py:350
  59.9 11.3 %collective-permute-start.12 = (bf16[288,384]{1,0:T(8,128)(2,1)S(1)}, bf16[288,384]{1,0:T(8,128)(2,1)S(1)}, u32[]{:S(2)}, u32[]{:S(2)}) collective-permute-start(bf16[288,384]{1,0:T(8,128)(2,1)S(1)} %get-tuple-element.85.refs_4_.refs_0_.refs_1_), channel_id=1, source_target_pairs={{0,4},{4,0},{8,12},{12,8},{1,5},{5,1},{9,13},{13,9},{2,6},{6,2},{1... | collective-permute-start | bytes 663560 | tf_op jit(solution)/shard_map/ppermute | solution.py:360
  60.7 19.1 %collective-permute-start.13 = (bf16[288,384]{1,0:T(8,128)(2,1)S(1)}, bf16[288,384]{1,0:T(8,128)(2,1)S(1)}, u32[]{:S(2)}, u32[]{:S(2)}) collective-permute-start(bf16[288,384]{1,0:T(8,128)(2,1)S(1)} %get-tuple-element.85.refs_4_.refs_0_.refs_1_), channel_id=1, source_target_pairs={{0,8},{4,12},{8,0},{12,4},{1,9},{5,13},{9,1},{13,5},{2,10},{6,14},... | collective-permute-start | bytes 663560 | tf_op jit(solution)/shard_map/ppermute | solution.py:359
  62.4 17.3 %collective-permute-start.22 = (bf16[16,384]{1,0:T(8,128)(2,1)S(1)}, bf16[16,384]{1,0:T(8,128)(2,1)S(1)}, u32[]{:S(2)}, u32[]{:S(2)}) collective-permute-start(bf16[16,384]{1,0:T(8,128)(2,1)S(1)} %get-tuple-element.86), channel_id=1, source_target_pairs={{0,4},{4,8},{8,12},{12,0},{1,5},{5,9},{9,13},{13,1},{2,6},{6,10},{... | collective-permute-start | bytes 36872 | tf_op jit(solution)/shard_map/ppermute | solution.py:354
  62.5 17.3 %collective-permute-start.23 = (bf16[16,384]{1,0:T(8,128)(2,1)S(1)}, bf16[16,384]{1,0:T(8,128)(2,1)S(1)}, u32[]{:S(2)}, u32[]{:S(2)}) collective-permute-start(bf16[16,384]{1,0:T(8,128)(2,1)S(1)} %get-tuple-element.87), channel_id=1, source_target_pairs={{0,12},{4,0},{8,4},{12,8},{1,13},{5,1},{9,5},{13,9},{2,14},{6,2},{... | collective-permute-start | bytes 36872 | tf_op jit(solution)/shard_map/ppermute | solution.py:354
  66.3 2.8 %copy-start.1 = (bf16[1536,5,384]{2,0,1:T(8,128)(2,1)S(1)}, bf16[1536,5,384]{2,0,1:T(8,128)(2,1)}, u32[]{:S(2)}) copy-start(bf16[1536,5,384]{2,0,1:T(8,128)(2,1)} %param.11) | copy-start | bytes 17694724
  69.6 14.5 %collective-permute-start.21 = (bf16[288,384]{1,0:T(8,128)(2,1)S(1)}, bf16[288,384]{1,0:T(8,128)(2,1)S(1)}, u32[]{:S(2)}, u32[]{:S(2)}) collective-permute-start(bf16[288,384]{1,0:T(8,128)(2,1)S(1)} %get-tuple-element.84.refs_1_.refs_5_), channel_id=1, source_target_pairs={{0,8},{4,12},{8,0},{12,4},{1,9},{5,13},{9,1},{13,5},{2,10},{6,14},... | collective-permute-start | bytes 663560 | tf_op jit(solution)/shard_map/ppermute | solution.py:359
  79.8 7.5 %collective-permute-start.14 = (bf16[288,384]{1,0:T(8,128)(2,1)S(1)}, bf16[288,384]{1,0:T(8,128)(2,1)S(1)}, u32[]{:S(2)}, u32[]{:S(2)}) collective-permute-start(bf16[288,384]{1,0:T(8,128)(2,1)S(1)} %collective-permute-done.13.refs_6_.refs_3_), channel_id=1, source_target_pairs={{0,4},{4,0},{8,12},{12,8},{1,5},{5,1},{9,13},{13,9},{2,6},{6,2},{1... | collective-permute-start | bytes 663560 | tf_op jit(solution)/shard_map/ppermute | solution.py:360
  81.9 11.1 %copy-start.5 = (bf16[64,768]{1,0:T(8,128)(2,1)S(1)}, bf16[64,768]{1,0:T(8,128)(2,1)}, u32[]{:S(2)}) copy-start(bf16[64,768]{1,0:T(8,128)(2,1)} %refs_0_) | copy-start | bytes 294916
  81.9 7.5 %collective-permute-start.25 = (bf16[384,384]{1,0:T(8,128)(2,1)S(1)}, bf16[384,384]{1,0:T(8,128)(2,1)S(1)}, u32[]{:S(2)}, u32[]{:S(2)}) collective-permute-start(bf16[384,384]{1,0:T(8,128)(2,1)S(1)} %get-tuple-element.90), channel_id=1, source_target_pairs={{0,1},{1,0},{2,3},{3,2},{4,5},{5,4},{6,7},{7,6},{8,9},{9,8},{10,11... | collective-permute-start | bytes 884744 | tf_op jit(solution)/shard_map/ppermute | solution.py:649
  82.0 12.5 %collective-permute-start.27 = (bf16[288,384]{1,0:T(8,128)(2,1)S(1)}, bf16[288,384]{1,0:T(8,128)(2,1)}, u32[]{:S(2)}, u32[]{:S(2)}) collective-permute-start(bf16[288,384]{1,0:T(8,128)(2,1)S(1)} %get-tuple-element.84.refs_1_.refs_5_), channel_id=1, source_target_pairs={{0,4},{4,0},{8,12},{12,8},{1,5},{5,1},{9,13},{13,9},{2,6},{6,2},{1... | collective-permute-start | bytes 663560 | tf_op jit(solution)/shard_map/ppermute | solution.py:360
  84.1 11.8 %collective-permute-start.28 = (bf16[288,384]{1,0:T(8,128)(2,1)S(1)}, bf16[288,384]{1,0:T(8,128)(2,1)}, u32[]{:S(2)}, u32[]{:S(2)}) collective-permute-start(bf16[288,384]{1,0:T(8,128)(2,1)S(1)} %collective-permute-done.21.refs_7_), channel_id=1, source_target_pairs={{0,4},{4,0},{8,12},{12,8},{1,5},{5,1},{9,13},{13,9},{2,6},{6,2},{1... | collective-permute-start | bytes 663560 | tf_op jit(solution)/shard_map/ppermute | solution.py:360
  89.3 13.0 %collective-permute-start.24 = (bf16[384,384]{1,0:T(8,128)(2,1)S(1)}, bf16[384,384]{1,0:T(8,128)(2,1)}, u32[]{:S(2)}, u32[]{:S(2)}) collective-permute-start(bf16[384,384]{1,0:T(8,128)(2,1)S(1)} %get-tuple-element.88), channel_id=1, source_target_pairs={{0,1},{1,0},{2,3},{3,2},{4,5},{5,4},{6,7},{7,6},{8,9},{9,8},{10,11... | collective-permute-start | bytes 884744 | tf_op jit(solution)/shard_map/ppermute | solution.py:652
  90.2 12.1 %collective-permute-start.26 = (bf16[384,384]{1,0:T(8,128)(2,1)}, bf16[384,384]{1,0:T(8,128)(2,1)}, u32[]{:S(2)}, u32[]{:S(2)}) collective-permute-start(bf16[384,384]{1,0:T(8,128)(2,1)} %add_convert_fusion.1), channel_id=1, source_target_pairs={{0,2},{1,3},{2,0},{3,1},{4,6},{5,7},{6,4},{7,5},{8,10},{9,11},{10,... | collective-permute-start | bytes 884744 | tf_op jit(solution)/shard_map/ppermute | solution.py:650
  91.3 1.3 %copy-start.3 = (bf16[16,96,384]{2,1,0:T(8,128)(2,1)S(1)}, bf16[16,96,384]{2,1,0:T(8,128)(2,1)}, u32[]{:S(2)}) copy-start(bf16[16,96,384]{2,1,0:T(8,128)(2,1)} %all-gather.3.cloned.1.call-done) | copy-start | bytes 3538948
  94.2 8.1 %collective-permute-start.18 = (bf16[64,768]{1,0:T(8,128)(2,1)S(1)}, bf16[64,768]{1,0:T(8,128)(2,1)S(1)}, u32[]{:S(2)}, u32[]{:S(2)}) collective-permute-start(bf16[64,768]{1,0:T(8,128)(2,1)S(1)} %get-tuple-element.79), channel_id=1, source_target_pairs={{0,1},{1,0},{2,3},{3,2},{4,5},{5,4},{6,7},{7,6},{8,9},{9,8},{10,11... | collective-permute-start | bytes 294920 | tf_op jit(solution)/shard_map/ppermute | solution.py:670
  94.5 7.9 %collective-permute-start.19 = (bf16[64,768]{1,0:T(8,128)(2,1)S(1)}, bf16[64,768]{1,0:T(8,128)(2,1)S(1)}, u32[]{:S(2)}, u32[]{:S(2)}) collective-permute-start(bf16[64,768]{1,0:T(8,128)(2,1)S(1)} %get-tuple-element.80), channel_id=1, source_target_pairs={{0,2},{1,3},{2,0},{3,1},{4,6},{5,7},{6,4},{7,5},{8,10},{9,11},{10,... | collective-permute-start | bytes 294920 | tf_op jit(solution)/shard_map/ppermute | solution.py:670
  95.9 7.7 %collective-permute-start.20 = (bf16[64,768]{1,0:T(8,128)(2,1)S(1)}, bf16[64,768]{1,0:T(8,128)(2,1)S(1)}, u32[]{:S(2)}, u32[]{:S(2)}) collective-permute-start(bf16[64,768]{1,0:T(8,128)(2,1)S(1)} %get-tuple-element.81), channel_id=1, source_target_pairs={{0,3},{1,2},{2,1},{3,0},{4,7},{5,6},{6,5},{7,4},{8,11},{9,10},{10,... | collective-permute-start | bytes 294920 | tf_op jit(solution)/shard_map/ppermute | solution.py:670
Sparse Core Ops, SparseCore 0:
  60.0 16.6 all-gather.2

commit v5 on v4

--- a/solution.py
+++ b/solution.py
@@ -324,6 +324,15 @@
         out[t] = dot(xt, moved[...])
 
 
+def finish_kernel(*refs):
+    ins, (dx_ref, qk_ref) = refs[:-2], refs[-2:]
+    dx_ref[...] = (ins[0][...] + ins[1][...].astype(F32) + ins[2][...].astype(F32)).astype(BF)
+    total = ins[3][...]
+    for part in ins[4:]:
+        total = total + part[...].astype(F32)
+    qk_ref[...] = total.astype(BF)
+
+
 def proj_kernel(slabs, chans, *refs):
     cots, normed, rest = refs[:chans], refs[chans : -(chans + 5)], refs[-(chans + 5) :]
     (w_ref, dw_ref), outs, (wide, full, part) = rest[:2], rest[2 : 2 + chans], rest[2 + chans :]
@@ -624,7 +633,7 @@
         name="turn_x",
     )
     low_all = relay(low, slabs, "seq")
-    high_all = relay(high, slabs, "seq")
+    high_all = relay(after(high, low_all[2]), slabs, "seq")
     from_left, from_right = turn(tail, 1, slabs), turn(head, slabs - 1, slabs)
 
     taps_late = staged(low)
@@ -679,11 +688,12 @@
         name="dw",
     )
     qk_got, beside, across, dw_taps = lax.optimization_barrier((qk_got, beside, across, dw_taps))
-    dx_field = (mine_dx + beside.astype(F32) + across.astype(F32)).astype(BF)
-    qk_sum = qk_parts[0]
-    for got in qk_got:
-        qk_sum = qk_sum + got.astype(F32)
-    qk_out = qk_sum.astype(BF)
+    dx_field, qk_out = launch(
+        finish_kernel,
+        [struct((width, length), BF), struct((feat, positions), BF)],
+        [mine_dx, beside, across, qk_parts[0], *qk_got],
+        name="finish",
+    )
     return (qk_out, jnp.transpose(dw_taps, (1, 0, 2)), dw_proj, dx_field)
 
 

time: 113 us -> 111 us (0.982)
  waiting for transfers between devices: 35.4 us -> 32.6 us
  other arithmetic: 4.08 us -> 1.55 us
  starting transfers between devices: 30.9 us -> 33 us
    ppermute x3, waiting for transfers between devices: 18.4 us -> 12.7 us  [relay(): far = lax.ppermute(value, axis, [(i, i ^ 2) for i in range(count)])]
    ppermute x3, starting transfers between devices: 0.11 us -> 4.01 us  [relay(): lax.ppermute(far, axis, near)]
    ppermute x3, waiting for transfers between devices: 5.3 us -> 9.05 us  [relay(): lax.ppermute(far, axis, near)]
    convert_element_type x2 -> x0, other arithmetic: 2.55 us -> none  [the longest x1 1.86 us: per_device(): dx_field = (mine_dx + beside.astype(F32) + across.astype(F32)).astype(BF)]
    ppermute x3, starting transfers between devices: 2.93 us -> 0.99 us  [relay(): lax.ppermute(value, axis, near)]
    pallas_call x14 -> x15, Pallas kernels: 21.6 us -> 22.5 us  [launch(): pl.pallas_call(body, out_shape=outs, in_specs=specs or [VMEM] * len(ins),...]
  transfers between devices with their start and end apart: 30 -> 30, of which waited for: 12 -> 12; matrix products, arithmetic and copies ran while one was open for 1% -> 1% of each run, Pallas kernels for 16% -> 17%
where the time goes in v5:
time: 111 us
  starting transfers between devices  33 us (30%)
  waiting for transfers between devices  32.6 us (29%)
  Pallas kernels  22.5 us (20%)
  between operations  14.2 us (13%)
  local copies, waits for them, and re-layouts  6.72 us (6%)
  other arithmetic  1.55 us (1%)
    pallas_call x15, Pallas kernels, launch(): pl.pallas_call(body, out_shape=outs, in_specs=specs or [VMEM] * len(ins),...  22.5 us
    ppermute x8, starting transfers between devices, turn(): lax.ppermute(value, 'seq', [(i, (i + k) % count) for i in range(count)])  17.4 us
    ppermute x3, waiting for transfers between devices, relay(): far = lax.ppermute(value, axis, [(i, i ^ 2) for i in range(count)])  12.7 us
    ppermute x3, waiting for transfers between devices, relay(): lax.ppermute(far, axis, near)  9.05 us
    unnamed x16, local copies, waits for them, and re-layouts  6.72 us
    ppermute x8, waiting for transfers between devices, turn(): lax.ppermute(value, 'seq', [(i, (i + k) % count) for i in range(count)])  4.78 us
    ppermute x6, starting transfers between devices, swaps(): lax.ppermute(value, 'chan', [(i, i ^ j) for i in range(count)])  4.48 us
    ppermute x6, waiting for transfers between devices, swaps(): lax.ppermute(value, 'chan', [(i, i ^ j) for i in range(count)])  4.23 us
  transfers between devices with their start and end apart: 30, of which 12 were waited for; matrix products, arithmetic and copies ran while one was open for 1% of the time, Pallas kernels for 17%

profile of v5, /device:TPU:0, one launch (start us, length us, event | category | flops | bytes accessed | tf_op | source)
XLA Modules:
  0.0 110.7 jit_solution(13114430582607155532)
XLA Ops:
  7.2 0.0 all-gather.3.cloned.1.call-start
  7.2 2.4 %pack.1 = (bf16[240,384]{1,0:T(8,128)(2,1)}, bf16[240,384]{1,0:T(8,128)(2,1)}, bf16[240,384]{1,0:T(8,128)(2,1)}, bf16[240,384]{1,0:T(8,128)(2,1)}) custom-call(s32[5]{0:T(128)} %dest_hbm.1, s32[5]{0:T(128)} %kept_hbm.1, bf16[480,384]{1,0:T(8,128)(2,1)} %bitcast.15, bf16[64,768]{1,0:T(8,128)(2,1)} %refs_0_), custom_call_target="tpu_custom_call" | custom-call | flops 306708480 | bytes 638976 | tf_op jit(solution)/shard_map/pack/pallas_call | solution.py:29
  9.6 0.5 collective-permute-start.3
  10.2 2.6 %collective-permute-start = (bf16[240,384]{1,0:T(8,128)(2,1)}, bf16[240,384]{1,0:T(8,128)(2,1)S(1)}, u32[]{:S(2)}, u32[]{:S(2)}) collective-permute-start(bf16[240,384]{1,0:T(8,128)(2,1)} %get-tuple-element.56), channel_id=1, source_target_pairs={{0,4},{4,8},{8,12},{12,0},{1,5},{5,9},{9,13},{13,1},{2,6},{6,10},{... | collective-permute-start | bytes 552968 | tf_op jit(solution)/shard_map/ppermute | solution.py:363
  12.8 2.6 %collective-permute-start.1 = (bf16[240,384]{1,0:T(8,128)(2,1)}, bf16[240,384]{1,0:T(8,128)(2,1)S(1)}, u32[]{:S(2)}, u32[]{:S(2)}) collective-permute-start(bf16[240,384]{1,0:T(8,128)(2,1)} %get-tuple-element.57), channel_id=1, source_target_pairs={{0,8},{4,12},{8,0},{12,4},{1,9},{5,13},{9,1},{13,5},{2,10},{6,14},... | collective-permute-start | bytes 552968 | tf_op jit(solution)/shard_map/ppermute | solution.py:363
  15.4 1.3 %collective-permute-start.2 = (bf16[240,384]{1,0:T(8,128)(2,1)}, bf16[240,384]{1,0:T(8,128)(2,1)S(1)}, u32[]{:S(2)}, u32[]{:S(2)}) collective-permute-start(bf16[240,384]{1,0:T(8,128)(2,1)} %get-tuple-element.58), channel_id=1, source_target_pairs={{0,12},{4,0},{8,4},{12,8},{1,13},{5,1},{9,5},{13,9},{2,14},{6,2},{... | collective-permute-start | bytes 552968 | tf_op jit(solution)/shard_map/ppermute | solution.py:363
  16.7 1.5 %collective-permute-start.4 = (bf16[64,768]{1,0:T(8,128)(2,1)}, bf16[64,768]{1,0:T(8,128)(2,1)S(1)}, u32[]{:S(2)}, u32[]{:S(2)}) collective-permute-start(bf16[64,768]{1,0:T(8,128)(2,1)} %refs_0_), channel_id=1, source_target_pairs={{0,2},{1,3},{2,0},{3,1},{4,6},{5,7},{6,4},{7,5},{8,10},{9,11},{10,... | collective-permute-start | bytes 294920 | tf_op jit(solution)/shard_map/ppermute | solution.py:359
  18.2 2.7 %copy-done = bf16[1536,5,384]{2,0,1:T(8,128)(2,1)S(1)} copy-done((bf16[1536,5,384]{2,0,1:T(8,128)(2,1)S(1)}, bf16[1536,5,384]{2,0,1:T(8,128)(2,1)}, u32[]{:S(2)}) %copy-start) | copy-done | bytes 5898264
  20.9 0.6 stage.2.refs_4_
  21.5 0.0 copy-start.2
  21.5 0.0 copy-start.6
  21.5 0.2 collective-permute-done.4.refs_2_
  21.7 1.8 %collective-permute-done.5.refs_3_ = bf16[64,768]{1,0:T(8,128)(2,1)S(1)} collective-permute-done((bf16[64,768]{1,0:T(8,128)(2,1)}, bf16[64,768]{1,0:T(8,128)(2,1)S(1)}, u32[]{:S(2)}, u32[]{:S(2)}) %collective-permute-start.5) | collective-permute-done | bytes 98336 | tf_op jit(solution)/shard_map/ppermute | solution.py:359
  23.5 4.8 %collective-permute-done.1.refs_2_ = bf16[240,384]{1,0:T(8,128)(2,1)S(1)} collective-permute-done((bf16[240,384]{1,0:T(8,128)(2,1)}, bf16[240,384]{1,0:T(8,128)(2,1)S(1)}, u32[]{:S(2)}, u32[]{:S(2)}) %collective-permute-start.1) | collective-permute-done | bytes 184352 | tf_op jit(solution)/shard_map/ppermute | solution.py:363
  28.3 0.0 collective-permute-done.2.refs_3_
  28.3 0.6 unpack.1.refs_0_
  28.9 1.5 %collective-permute-start.7 = (bf16[528,384]{1,0:T(8,128)(2,1)S(1)}, bf16[528,384]{1,0:T(8,128)(2,1)S(1)}, u32[]{:S(2)}, u32[]{:S(2)}) collective-permute-start(bf16[528,384]{1,0:T(8,128)(2,1)S(1)} %unpack.1.refs_0_), channel_id=1, source_target_pairs={{0,2},{1,3},{2,0},{3,1},{4,6},{5,7},{6,4},{7,5},{8,10},{9,11},{10,... | collective-permute-start | bytes 1216520 | tf_op jit(solution)/shard_map/ppermute | solution.py:368
  30.5 9.8 %collective-permute-done.7.refs_2_ = bf16[528,384]{1,0:T(8,128)(2,1)S(1)} collective-permute-done((bf16[528,384]{1,0:T(8,128)(2,1)S(1)}, bf16[528,384]{1,0:T(8,128)(2,1)S(1)}, u32[]{:S(2)}, u32[]{:S(2)}) %collective-permute-start.7) | collective-permute-done | bytes 405536 | tf_op jit(solution)/shard_map/ppermute | solution.py:368
  40.2 1.7 %collective-permute-done.8.refs_3_ = bf16[528,384]{1,0:T(8,128)(2,1)S(1)} collective-permute-done((bf16[528,384]{1,0:T(8,128)(2,1)S(1)}, bf16[528,384]{1,0:T(8,128)(2,1)S(1)}, u32[]{:S(2)}, u32[]{:S(2)}) %collective-permute-start.8) | collective-permute-done | bytes 405536 | tf_op jit(solution)/shard_map/ppermute | solution.py:369
  42.0 0.1 quarter.1
  42.0 4.6 %collective-permute-start.18 = (bf16[96,384]{1,0:T(8,128)(2,1)S(1)}, bf16[96,384]{1,0:T(8,128)(2,1)S(1)}, u32[]{:S(2)}, u32[]{:S(2)}) collective-permute-start(bf16[96,384]{1,0:T(8,128)(2,1)S(1)} %get-tuple-element.81), channel_id=1, source_target_pairs={{0,4},{4,8},{8,12},{12,0},{1,5},{5,9},{9,13},{13,1},{2,6},{6,10},{... | collective-permute-start | bytes 221192 | tf_op jit(solution)/shard_map/ppermute | solution.py:363
  46.6 1.2 %collective-permute-start.19 = (bf16[96,384]{1,0:T(8,128)(2,1)S(1)}, bf16[96,384]{1,0:T(8,128)(2,1)S(1)}, u32[]{:S(2)}, u32[]{:S(2)}) collective-permute-start(bf16[96,384]{1,0:T(8,128)(2,1)S(1)} %get-tuple-element.82), channel_id=1, source_target_pairs={{0,8},{4,12},{8,0},{12,4},{1,9},{5,13},{9,1},{13,5},{2,10},{6,14},... | collective-permute-start | bytes 221192 | tf_op jit(solution)/shard_map/ppermute | solution.py:363
  47.8 1.2 %collective-permute-start.20 = (bf16[96,384]{1,0:T(8,128)(2,1)S(1)}, bf16[96,384]{1,0:T(8,128)(2,1)S(1)}, u32[]{:S(2)}, u32[]{:S(2)}) collective-permute-start(bf16[96,384]{1,0:T(8,128)(2,1)S(1)} %get-tuple-element.83), channel_id=1, source_target_pairs={{0,12},{4,0},{8,4},{12,8},{1,13},{5,1},{9,5},{13,9},{2,14},{6,2},{... | collective-permute-start | bytes 221192 | tf_op jit(solution)/shard_map/ppermute | solution.py:363
  49.0 3.9 %conv.1 = (f32[192,384]{1,0:T(8,128)S(1)}, f32[384,384]{1,0:T(8,128)S(1)}) custom-call(bf16[528,384]{1,0:T(8,128)(2,1)S(1)} %unpack.1.refs_0_, bf16[528,384]{1,0:T(8,128)(2,1)S(1)} %collective-permute-done.6.refs_1_, bf16[528,384]{1,0:T(8,128)(2,1)S(1)} %collective-permute-done.7.refs_2_, bf16[528,384]{1,0:T(8,128)(2,1)S(1)} %collective-permute-done.8.refs_3_, ...), custom_call_target="tpu_custom_call" | custom-call | flops 2359296000 | bytes 5898240 | tf_op jit(solution)/shard_map/conv/pallas_call | solution.py:29
  53.0 0.5 cotangent.1.dxhat_ref.refs_6_
  53.5 0.2 sums.1.refs_0_
  53.8 0.0 collective-permute-start.9
  53.8 1.6 %collective-permute-start.10 = (f32[8,256]{1,0:T(8,128)S(1)}, f32[8,256]{1,0:T(8,128)S(1)}, u32[]{:S(2)}, u32[]{:S(2)}) collective-permute-start(f32[8,256]{1,0:T(8,128)S(1)} %sums.1.refs_0_), channel_id=1, source_target_pairs={{0,2},{1,3},{2,0},{3,1},{4,6},{5,7},{6,4},{7,5},{8,10},{9,11},{10,... | collective-permute-start | bytes 24584 | tf_op jit(solution)/shard_map/ppermute | solution.py:359
  55.4 0.9 collective-permute-start.11
  56.2 1.3 %collective-permute-done.10.refs_2_ = f32[8,256]{1,0:T(8,128)S(1)} collective-permute-done((f32[8,256]{1,0:T(8,128)S(1)}, f32[8,256]{1,0:T(8,128)S(1)}, u32[]{:S(2)}, u32[]{:S(2)}) %collective-permute-start.10) | collective-permute-done | bytes 8224 | tf_op jit(solution)/shard_map/ppermute | solution.py:359
  57.5 0.9 collective-permute-done.11.refs_3_
  58.5 0.6 gradient.1
  59.1 0.8 pad_maximum_fusion
  59.8 0.0 all-gather.3.cloned.1.call-update
  59.9 0.8 collective-permute-start.12
  60.7 1.7 %collective-permute-start.13 = (bf16[288,384]{1,0:T(8,128)(2,1)S(1)}, bf16[288,384]{1,0:T(8,128)(2,1)S(1)}, u32[]{:S(2)}, u32[]{:S(2)}) collective-permute-start(bf16[288,384]{1,0:T(8,128)(2,1)S(1)} %get-tuple-element.72.refs_0_.refs_4_.refs_1_), channel_id=1, source_target_pairs={{0,8},{4,12},{8,0},{12,4},{1,9},{5,13},{9,1},{13,5},{2,10},{6,14},... | collective-permute-start | bytes 663560 | tf_op jit(solution)/shard_map/ppermute | solution.py:368
  62.5 0.1 collective-permute-start.16
  62.5 3.7 %collective-permute-start.17 = (bf16[16,384]{1,0:T(8,128)(2,1)S(1)}, bf16[16,384]{1,0:T(8,128)(2,1)S(1)}, u32[]{:S(2)}, u32[]{:S(2)}) collective-permute-start(bf16[16,384]{1,0:T(8,128)(2,1)S(1)} %get-tuple-element.74), channel_id=1, source_target_pairs={{0,12},{4,0},{8,4},{12,8},{1,13},{5,1},{9,5},{13,9},{2,14},{6,2},{... | collective-permute-start | bytes 36872 | tf_op jit(solution)/shard_map/ppermute | solution.py:363
  66.3 2.8 %copy-done.1 = bf16[1536,5,384]{2,0,1:T(8,128)(2,1)S(1)} copy-done((bf16[1536,5,384]{2,0,1:T(8,128)(2,1)S(1)}, bf16[1536,5,384]{2,0,1:T(8,128)(2,1)}, u32[]{:S(2)}) %copy-start.1) | copy-done | bytes 5898264
  69.0 0.6 stage.3.refs_4_
  69.6 1.6 %collective-permute-done.12.refs_5_.refs_2_ = bf16[288,384]{1,0:T(8,128)(2,1)S(1)} collective-permute-done((bf16[288,384]{1,0:T(8,128)(2,1)S(1)}, bf16[288,384]{1,0:T(8,128)(2,1)S(1)}, u32[]{:S(2)}, u32[]{:S(2)}) %collective-permute-start.12) | collective-permute-done | bytes 221216 | tf_op jit(solution)/shard_map/ppermute | solution.py:369
  71.2 2.9 %collective-permute-done.13.refs_6_.refs_3_ = bf16[288,384]{1,0:T(8,128)(2,1)S(1)} collective-permute-done((bf16[288,384]{1,0:T(8,128)(2,1)S(1)}, bf16[288,384]{1,0:T(8,128)(2,1)S(1)}, u32[]{:S(2)}, u32[]{:S(2)}) %collective-permute-start.13) | collective-permute-done | bytes 221216 | tf_op jit(solution)/shard_map/ppermute | solution.py:368
  74.0 0.1 collective-permute-start.15
  74.2 1.9 %collective-permute-start.14 = (bf16[288,384]{1,0:T(8,128)(2,1)S(1)}, bf16[288,384]{1,0:T(8,128)(2,1)S(1)}, u32[]{:S(2)}, u32[]{:S(2)}) collective-permute-start(bf16[288,384]{1,0:T(8,128)(2,1)S(1)} %collective-permute-done.13.refs_6_.refs_3_), channel_id=1, source_target_pairs={{0,4},{4,0},{8,12},{12,8},{1,5},{5,1},{9,13},{13,9},{2,6},{6,2},{1... | collective-permute-start | bytes 663560 | tf_op jit(solution)/shard_map/ppermute | solution.py:369
  76.1 2.1 %dx_far.1 = (bf16[384,384]{1,0:T(8,128)(2,1)S(1)}, f32[384,384]{1,0:T(8,128)S(1)}) custom-call(bf16[288,384]{1,0:T(8,128)(2,1)S(1)} %get-tuple-element.72.refs_0_.refs_4_.refs_1_, bf16[288,384]{1,0:T(8,128)(2,1)S(1)} %get-tuple-element.71.refs_1_.refs_5_, bf16[16,384]{1,0:T(8,128)(2,1)S(1)} %collective-permute-done.16.refs_2_, ...), custom_call_target="tpu_custom_call" | custom-call | flops 1132462080 | bytes 2949120 | tf_op jit(solution)/shard_map/dx_far/pallas_call | solution.py:29
  78.2 0.0 copy-start.5
  78.2 0.1 collective-permute-start.25
  78.3 0.1 collective-permute-start.27
  78.5 6.8 %collective-permute-done.14.refs_7_.refs_4_ = bf16[288,384]{1,0:T(8,128)(2,1)S(1)} collective-permute-done((bf16[288,384]{1,0:T(8,128)(2,1)S(1)}, bf16[288,384]{1,0:T(8,128)(2,1)S(1)}, u32[]{:S(2)}, u32[]{:S(2)}) %collective-permute-start.14) | collective-permute-done | bytes 221216 | tf_op jit(solution)/shard_map/ppermute | solution.py:369
  85.2 0.1 collective-permute-done.15.refs_7_
  85.3 2.1 %dx_near.1 = (bf16[384,384]{1,0:T(8,128)(2,1)}, f32[384,384]{1,0:T(8,128)S(1)}) custom-call(bf16[288,384]{1,0:T(8,128)(2,1)S(1)} %get-tuple-element.72.refs_0_.refs_4_.refs_1_, bf16[288,384]{1,0:T(8,128)(2,1)S(1)} %get-tuple-element.71.refs_1_.refs_5_, bf16[16,384]{1,0:T(8,128)(2,1)S(1)} %collective-permute-done.16.refs_2_, ...), custom_call_target="tpu_custom_call" | custom-call | flops 1132462080 | bytes 2949120 | tf_op jit(solution)/shard_map/dx_near/pallas_call | solution.py:29
  87.4 0.1 collective-permute-start.24
  87.5 2.1 %collective-permute-start.28 = (bf16[288,384]{1,0:T(8,128)(2,1)}, bf16[288,384]{1,0:T(8,128)(2,1)}, u32[]{:S(2)}, u32[]{:S(2)}) collective-permute-start(bf16[288,384]{1,0:T(8,128)(2,1)} %collective-permute-done.15.refs_7_), channel_id=1, source_target_pairs={{0,4},{4,0},{8,12},{12,8},{1,5},{5,1},{9,13},{13,9},{2,6},{6,2},{1... | collective-permute-start | bytes 663560 | tf_op jit(solution)/shard_map/ppermute | solution.py:369
  89.5 0.8 add_convert_fusion
  90.3 1.1 collective-permute-start.26
  91.4 1.3 %copy-done.3 = bf16[16,96,384]{2,1,0:T(8,128)(2,1)S(1)} copy-done((bf16[16,96,384]{2,1,0:T(8,128)(2,1)S(1)}, bf16[16,96,384]{2,1,0:T(8,128)(2,1)}, u32[]{:S(2)}) %copy-start.3) | copy-done | bytes 1179672
  92.7 0.5 turn_x.1.refs_0_
  93.2 1.2 %projection.1 = (f32[256,384]{1,0:T(8,128)}, f32[64,768]{1,0:T(8,128)S(1)}, bf16[64,768]{1,0:T(8,128)(2,1)S(1)}, bf16[64,768]{1,0:T(8,128)(2,1)S(1)}, bf16[64,768]{1,0:T(8,128)(2,1)S(1)}) custom-call(bf16[64,768]{1,0:T(8,128)(2,1)S(1)} %copy-done.5, bf16[64,768]{1,0:T(8,128)(2,1)S(1)} %collective-permute-done.3.refs_1_, ...), custom_call_target="tpu_custom_call" | custom-call | flops 301989888 | bytes 393216 | tf_op jit(solution)/shard_map/projection/pallas_call | solution.py:29
  94.4 0.9 collective-permute-start.22
  95.3 0.6 collective-permute-done.28.refs_8_
  95.9 0.5 collective-permute-start.23
  96.4 6.3 %dw.1 = f32[5,384,384]{2,1,0:T(8,128)} custom-call(bf16[384,1536]{1,0:T(8,128)(2,1)S(1)} %turn_x.1.refs_0_, bf16[288,384]{1,0:T(8,128)(2,1)S(1)} %get-tuple-element.72.refs_0_.refs_4_.refs_1_, bf16[288,384]{1,0:T(8,128)(2,1)S(1)} %collective-permute-done.12.refs_5_.refs_2_, bf16[288,384]{1,0:T(8,128)(2,1)S(1)} %collective-permute-done.13.refs_6_.refs_3_, ...), custom_call_target="tpu_custom_call" | custom-call | flops 2264924160 | bytes 2949120 | tf_op jit(solution)/shard_map/dw/pallas_call | solution.py:29
  102.7 0.3 collective-permute-done.23.refs_6_
  103.1 0.8 finish.1
  (30 shorter events, 0.1 us)
Async XLA Ops:
  7.2 84.3 %all-gather.3.cloned.1.call-start = ((), (), s32[]{:S(2)}) async-start(), calls=%async_computation | async-start | bytes 1474560 | tf_op jit(solution)/shard_map/all_gather | solution.py:627
  9.6 8.6 %collective-permute-start.3 = (bf16[64,768]{1,0:T(8,128)(2,1)}, bf16[64,768]{1,0:T(8,128)(2,1)S(1)}, u32[]{:S(2)}, u32[]{:S(2)}) collective-permute-start(bf16[64,768]{1,0:T(8,128)(2,1)} %refs_0_), channel_id=1, source_target_pairs={{0,1},{1,0},{2,3},{3,2},{4,5},{5,4},{6,7},{7,6},{8,9},{9,8},{10,11... | collective-permute-start | bytes 294920 | tf_op jit(solution)/shard_map/ppermute | solution.py:359
  10.2 13.4 %collective-permute-start = (bf16[240,384]{1,0:T(8,128)(2,1)}, bf16[240,384]{1,0:T(8,128)(2,1)S(1)}, u32[]{:S(2)}, u32[]{:S(2)}) collective-permute-start(bf16[240,384]{1,0:T(8,128)(2,1)} %get-tuple-element.56), channel_id=1, source_target_pairs={{0,4},{4,8},{8,12},{12,0},{1,5},{5,9},{9,13},{13,1},{2,6},{6,10},{... | collective-permute-start | bytes 552968 | tf_op jit(solution)/shard_map/ppermute | solution.py:363
  12.8 15.5 %collective-permute-start.1 = (bf16[240,384]{1,0:T(8,128)(2,1)}, bf16[240,384]{1,0:T(8,128)(2,1)S(1)}, u32[]{:S(2)}, u32[]{:S(2)}) collective-permute-start(bf16[240,384]{1,0:T(8,128)(2,1)} %get-tuple-element.57), channel_id=1, source_target_pairs={{0,8},{4,12},{8,0},{12,4},{1,9},{5,13},{9,1},{13,5},{2,10},{6,14},... | collective-permute-start | bytes 552968 | tf_op jit(solution)/shard_map/ppermute | solution.py:363
  15.4 12.9 %collective-permute-start.2 = (bf16[240,384]{1,0:T(8,128)(2,1)}, bf16[240,384]{1,0:T(8,128)(2,1)S(1)}, u32[]{:S(2)}, u32[]{:S(2)}) collective-permute-start(bf16[240,384]{1,0:T(8,128)(2,1)} %get-tuple-element.58), channel_id=1, source_target_pairs={{0,12},{4,0},{8,4},{12,8},{1,13},{5,1},{9,5},{13,9},{2,14},{6,2},{... | collective-permute-start | bytes 552968 | tf_op jit(solution)/shard_map/ppermute | solution.py:363
  16.7 5.0 %collective-permute-start.4 = (bf16[64,768]{1,0:T(8,128)(2,1)}, bf16[64,768]{1,0:T(8,128)(2,1)S(1)}, u32[]{:S(2)}, u32[]{:S(2)}) collective-permute-start(bf16[64,768]{1,0:T(8,128)(2,1)} %refs_0_), channel_id=1, source_target_pairs={{0,2},{1,3},{2,0},{3,1},{4,6},{5,7},{6,4},{7,5},{8,10},{9,11},{10,... | collective-permute-start | bytes 294920 | tf_op jit(solution)/shard_map/ppermute | solution.py:359
  18.2 5.3 %collective-permute-start.5 = (bf16[64,768]{1,0:T(8,128)(2,1)}, bf16[64,768]{1,0:T(8,128)(2,1)S(1)}, u32[]{:S(2)}, u32[]{:S(2)}) collective-permute-start(bf16[64,768]{1,0:T(8,128)(2,1)} %refs_0_), channel_id=1, source_target_pairs={{0,3},{1,2},{2,1},{3,0},{4,7},{5,6},{6,5},{7,4},{8,11},{9,10},{10,... | collective-permute-start | bytes 294920 | tf_op jit(solution)/shard_map/ppermute | solution.py:359
  18.2 2.7 %copy-start = (bf16[1536,5,384]{2,0,1:T(8,128)(2,1)S(1)}, bf16[1536,5,384]{2,0,1:T(8,128)(2,1)}, u32[]{:S(2)}) copy-start(bf16[1536,5,384]{2,0,1:T(8,128)(2,1)} %param.11) | copy-start | bytes 17694724
  20.9 7.4 %copy-start.4 = (bf16[240,384]{1,0:T(8,128)(2,1)S(1)}, bf16[240,384]{1,0:T(8,128)(2,1)}, u32[]{:S(2)}) copy-start(bf16[240,384]{1,0:T(8,128)(2,1)} %get-tuple-element.60.refs_0_) | copy-start | bytes 552964
  20.9 28.1 %copy-start.7 = (f32[384]{0:T(512)S(1)}, f32[384]{0:T(512)}, u32[]{:S(2)}) copy-start(f32[384]{0:T(512)} %refs_5_.2) | copy-start | bytes 4612
  21.5 31.5 %copy-start.2 = (bf16[1024,384]{1,0:T(8,128)(2,1)S(1)}, bf16[1024,384]{1,0:T(8,128)(2,1)}, u32[]{:S(2)}) copy-start(bf16[1024,384]{1,0:T(8,128)(2,1)} %refs_8_) | copy-start | bytes 2359300
  21.5 31.5 %copy-start.6 = (f32[384]{0:T(512)S(1)}, f32[384]{0:T(512)}, u32[]{:S(2)}) copy-start(f32[384]{0:T(512)} %refs_7_.1) | copy-start | bytes 4612
  28.9 11.3 %collective-permute-start.7 = (bf16[528,384]{1,0:T(8,128)(2,1)S(1)}, bf16[528,384]{1,0:T(8,128)(2,1)S(1)}, u32[]{:S(2)}, u32[]{:S(2)}) collective-permute-start(bf16[528,384]{1,0:T(8,128)(2,1)S(1)} %unpack.1.refs_0_), channel_id=1, source_target_pairs={{0,2},{1,3},{2,0},{3,1},{4,6},{5,7},{6,4},{7,5},{8,10},{9,11},{10,... | collective-permute-start | bytes 1216520 | tf_op jit(solution)/shard_map/ppermute | solution.py:368
  30.5 9.8 %collective-permute-start.6 = (bf16[528,384]{1,0:T(8,128)(2,1)S(1)}, bf16[528,384]{1,0:T(8,128)(2,1)S(1)}, u32[]{:S(2)}, u32[]{:S(2)}) collective-permute-start(bf16[528,384]{1,0:T(8,128)(2,1)S(1)} %unpack.1.refs_0_), channel_id=1, source_target_pairs={{0,1},{1,0},{2,3},{3,2},{4,5},{5,4},{6,7},{7,6},{8,9},{9,8},{10,11... | collective-permute-start | bytes 1216520 | tf_op jit(solution)/shard_map/ppermute | solution.py:369
  40.2 1.7 %collective-permute-start.8 = (bf16[528,384]{1,0:T(8,128)(2,1)S(1)}, bf16[528,384]{1,0:T(8,128)(2,1)S(1)}, u32[]{:S(2)}, u32[]{:S(2)}) collective-permute-start(bf16[528,384]{1,0:T(8,128)(2,1)S(1)} %collective-permute-done.7.refs_2_), channel_id=1, source_target_pairs={{0,1},{1,0},{2,3},{3,2},{4,5},{5,4},{6,7},{7,6},{8,9},{9,8},{10,11... | collective-permute-start | bytes 1216520 | tf_op jit(solution)/shard_map/ppermute | solution.py:369
  42.0 17.0 %collective-permute-start.18 = (bf16[96,384]{1,0:T(8,128)(2,1)S(1)}, bf16[96,384]{1,0:T(8,128)(2,1)S(1)}, u32[]{:S(2)}, u32[]{:S(2)}) collective-permute-start(bf16[96,384]{1,0:T(8,128)(2,1)S(1)} %get-tuple-element.81), channel_id=1, source_target_pairs={{0,4},{4,8},{8,12},{12,0},{1,5},{5,9},{9,13},{13,1},{2,6},{6,10},{... | collective-permute-start | bytes 221192 | tf_op jit(solution)/shard_map/ppermute | solution.py:363
  46.6 12.5 %collective-permute-start.19 = (bf16[96,384]{1,0:T(8,128)(2,1)S(1)}, bf16[96,384]{1,0:T(8,128)(2,1)S(1)}, u32[]{:S(2)}, u32[]{:S(2)}) collective-permute-start(bf16[96,384]{1,0:T(8,128)(2,1)S(1)} %get-tuple-element.82), channel_id=1, source_target_pairs={{0,8},{4,12},{8,0},{12,4},{1,9},{5,13},{9,1},{13,5},{2,10},{6,14},... | collective-permute-start | bytes 221192 | tf_op jit(solution)/shard_map/ppermute | solution.py:363
  47.8 11.3 %collective-permute-start.20 = (bf16[96,384]{1,0:T(8,128)(2,1)S(1)}, bf16[96,384]{1,0:T(8,128)(2,1)S(1)}, u32[]{:S(2)}, u32[]{:S(2)}) collective-permute-start(bf16[96,384]{1,0:T(8,128)(2,1)S(1)} %get-tuple-element.83), channel_id=1, source_target_pairs={{0,12},{4,0},{8,4},{12,8},{1,13},{5,1},{9,5},{13,9},{2,14},{6,2},{... | collective-permute-start | bytes 221192 | tf_op jit(solution)/shard_map/ppermute | solution.py:363
  53.8 1.6 %collective-permute-start.9 = (f32[8,256]{1,0:T(8,128)S(1)}, f32[8,256]{1,0:T(8,128)S(1)}, u32[]{:S(2)}, u32[]{:S(2)}) collective-permute-start(f32[8,256]{1,0:T(8,128)S(1)} %sums.1.refs_0_), channel_id=1, source_target_pairs={{0,1},{1,0},{2,3},{3,2},{4,5},{5,4},{6,7},{7,6},{8,9},{9,8},{10,11... | collective-permute-start | bytes 24584 | tf_op jit(solution)/shard_map/ppermute | solution.py:359
  53.8 3.7 %collective-permute-start.10 = (f32[8,256]{1,0:T(8,128)S(1)}, f32[8,256]{1,0:T(8,128)S(1)}, u32[]{:S(2)}, u32[]{:S(2)}) collective-permute-start(f32[8,256]{1,0:T(8,128)S(1)} %sums.1.refs_0_), channel_id=1, source_target_pairs={{0,2},{1,3},{2,0},{3,1},{4,6},{5,7},{6,4},{7,5},{8,10},{9,11},{10,... | collective-permute-start | bytes 24584 | tf_op jit(solution)/shard_map/ppermute | solution.py:359
  55.4 3.1 %collective-permute-start.11 = (f32[8,256]{1,0:T(8,128)S(1)}, f32[8,256]{1,0:T(8,128)S(1)}, u32[]{:S(2)}, u32[]{:S(2)}) collective-permute-start(f32[8,256]{1,0:T(8,128)S(1)} %sums.1.refs_0_), channel_id=1, source_target_pairs={{0,3},{1,2},{2,1},{3,0},{4,7},{5,6},{6,5},{7,4},{8,11},{9,10},{10,... | collective-permute-start | bytes 24584 | tf_op jit(solution)/shard_map/ppermute | solution.py:359
  59.9 11.3 %collective-permute-start.12 = (bf16[288,384]{1,0:T(8,128)(2,1)S(1)}, bf16[288,384]{1,0:T(8,128)(2,1)S(1)}, u32[]{:S(2)}, u32[]{:S(2)}) collective-permute-start(bf16[288,384]{1,0:T(8,128)(2,1)S(1)} %get-tuple-element.72.refs_0_.refs_4_.refs_1_), channel_id=1, source_target_pairs={{0,4},{4,0},{8,12},{12,8},{1,5},{5,1},{9,13},{13,9},{2,6},{6,2},{1... | collective-permute-start | bytes 663560 | tf_op jit(solution)/shard_map/ppermute | solution.py:369
  60.7 13.3 %collective-permute-start.13 = (bf16[288,384]{1,0:T(8,128)(2,1)S(1)}, bf16[288,384]{1,0:T(8,128)(2,1)S(1)}, u32[]{:S(2)}, u32[]{:S(2)}) collective-permute-start(bf16[288,384]{1,0:T(8,128)(2,1)S(1)} %get-tuple-element.72.refs_0_.refs_4_.refs_1_), channel_id=1, source_target_pairs={{0,8},{4,12},{8,0},{12,4},{1,9},{5,13},{9,1},{13,5},{2,10},{6,14},... | collective-permute-start | bytes 663560 | tf_op jit(solution)/shard_map/ppermute | solution.py:368
  62.5 13.7 %collective-permute-start.16 = (bf16[16,384]{1,0:T(8,128)(2,1)S(1)}, bf16[16,384]{1,0:T(8,128)(2,1)S(1)}, u32[]{:S(2)}, u32[]{:S(2)}) collective-permute-start(bf16[16,384]{1,0:T(8,128)(2,1)S(1)} %get-tuple-element.73), channel_id=1, source_target_pairs={{0,4},{4,8},{8,12},{12,0},{1,5},{5,9},{9,13},{13,1},{2,6},{6,10},{... | collective-permute-start | bytes 36872 | tf_op jit(solution)/shard_map/ppermute | solution.py:363
  62.5 13.6 %collective-permute-start.17 = (bf16[16,384]{1,0:T(8,128)(2,1)S(1)}, bf16[16,384]{1,0:T(8,128)(2,1)S(1)}, u32[]{:S(2)}, u32[]{:S(2)}) collective-permute-start(bf16[16,384]{1,0:T(8,128)(2,1)S(1)} %get-tuple-element.74), channel_id=1, source_target_pairs={{0,12},{4,0},{8,4},{12,8},{1,13},{5,1},{9,5},{13,9},{2,14},{6,2},{... | collective-permute-start | bytes 36872 | tf_op jit(solution)/shard_map/ppermute | solution.py:363
  66.3 2.8 %copy-start.1 = (bf16[1536,5,384]{2,0,1:T(8,128)(2,1)S(1)}, bf16[1536,5,384]{2,0,1:T(8,128)(2,1)}, u32[]{:S(2)}) copy-start(bf16[1536,5,384]{2,0,1:T(8,128)(2,1)} %param.11) | copy-start | bytes 17694724
  74.0 11.3 %collective-permute-start.15 = (bf16[288,384]{1,0:T(8,128)(2,1)S(1)}, bf16[288,384]{1,0:T(8,128)(2,1)}, u32[]{:S(2)}, u32[]{:S(2)}) collective-permute-start(bf16[288,384]{1,0:T(8,128)(2,1)S(1)} %get-tuple-element.71.refs_1_.refs_5_), channel_id=1, source_target_pairs={{0,8},{4,12},{8,0},{12,4},{1,9},{5,13},{9,1},{13,5},{2,10},{6,14},... | collective-permute-start | bytes 663560 | tf_op jit(solution)/shard_map/ppermute | solution.py:368
  74.2 11.1 %collective-permute-start.14 = (bf16[288,384]{1,0:T(8,128)(2,1)S(1)}, bf16[288,384]{1,0:T(8,128)(2,1)S(1)}, u32[]{:S(2)}, u32[]{:S(2)}) collective-permute-start(bf16[288,384]{1,0:T(8,128)(2,1)S(1)} %collective-permute-done.13.refs_6_.refs_3_), channel_id=1, source_target_pairs={{0,4},{4,0},{8,12},{12,8},{1,5},{5,1},{9,13},{13,9},{2,6},{6,2},{1... | collective-permute-start | bytes 663560 | tf_op jit(solution)/shard_map/ppermute | solution.py:369
  78.2 14.9 %copy-start.5 = (bf16[64,768]{1,0:T(8,128)(2,1)S(1)}, bf16[64,768]{1,0:T(8,128)(2,1)}, u32[]{:S(2)}) copy-start(bf16[64,768]{1,0:T(8,128)(2,1)} %refs_0_) | copy-start | bytes 294916
  78.2 11.3 %collective-permute-start.25 = (bf16[384,384]{1,0:T(8,128)(2,1)S(1)}, bf16[384,384]{1,0:T(8,128)(2,1)S(1)}, u32[]{:S(2)}, u32[]{:S(2)}) collective-permute-start(bf16[384,384]{1,0:T(8,128)(2,1)S(1)} %get-tuple-element.94), channel_id=1, source_target_pairs={{0,1},{1,0},{2,3},{3,2},{4,5},{5,4},{6,7},{7,6},{8,9},{9,8},{10,11... | collective-permute-start | bytes 884744 | tf_op jit(solution)/shard_map/ppermute | solution.py:658
  78.3 16.1 %collective-permute-start.27 = (bf16[288,384]{1,0:T(8,128)(2,1)S(1)}, bf16[288,384]{1,0:T(8,128)(2,1)}, u32[]{:S(2)}, u32[]{:S(2)}) collective-permute-start(bf16[288,384]{1,0:T(8,128)(2,1)S(1)} %get-tuple-element.71.refs_1_.refs_5_), channel_id=1, source_target_pairs={{0,4},{4,0},{8,12},{12,8},{1,5},{5,1},{9,13},{13,9},{2,6},{6,2},{1... | collective-permute-start | bytes 663560 | tf_op jit(solution)/shard_map/ppermute | solution.py:369
  87.4 15.3 %collective-permute-start.24 = (bf16[384,384]{1,0:T(8,128)(2,1)}, bf16[384,384]{1,0:T(8,128)(2,1)S(1)}, u32[]{:S(2)}, u32[]{:S(2)}) collective-permute-start(bf16[384,384]{1,0:T(8,128)(2,1)} %get-tuple-element.92), channel_id=1, source_target_pairs={{0,1},{1,0},{2,3},{3,2},{4,5},{5,4},{6,7},{7,6},{8,9},{9,8},{10,11... | collective-permute-start | bytes 884744 | tf_op jit(solution)/shard_map/ppermute | solution.py:661
  87.5 8.4 %collective-permute-start.28 = (bf16[288,384]{1,0:T(8,128)(2,1)}, bf16[288,384]{1,0:T(8,128)(2,1)}, u32[]{:S(2)}, u32[]{:S(2)}) collective-permute-start(bf16[288,384]{1,0:T(8,128)(2,1)} %collective-permute-done.15.refs_7_), channel_id=1, source_target_pairs={{0,4},{4,0},{8,12},{12,8},{1,5},{5,1},{9,13},{13,9},{2,6},{6,2},{1... | collective-permute-start | bytes 663560 | tf_op jit(solution)/shard_map/ppermute | solution.py:369
  90.3 12.4 %collective-permute-start.26 = (bf16[384,384]{1,0:T(8,128)(2,1)}, bf16[384,384]{1,0:T(8,128)(2,1)S(1)}, u32[]{:S(2)}, u32[]{:S(2)}) collective-permute-start(bf16[384,384]{1,0:T(8,128)(2,1)} %add_convert_fusion), channel_id=1, source_target_pairs={{0,2},{1,3},{2,0},{3,1},{4,6},{5,7},{6,4},{7,5},{8,10},{9,11},{10,... | collective-permute-start | bytes 884744 | tf_op jit(solution)/shard_map/ppermute | solution.py:659
  91.4 1.3 %copy-start.3 = (bf16[16,96,384]{2,1,0:T(8,128)(2,1)S(1)}, bf16[16,96,384]{2,1,0:T(8,128)(2,1)}, u32[]{:S(2)}) copy-start(bf16[16,96,384]{2,1,0:T(8,128)(2,1)} %all-gather.3.cloned.1.call-done) | copy-start | bytes 3538948
  94.4 8.3 %collective-permute-start.21 = (bf16[64,768]{1,0:T(8,128)(2,1)S(1)}, bf16[64,768]{1,0:T(8,128)(2,1)S(1)}, u32[]{:S(2)}, u32[]{:S(2)}) collective-permute-start(bf16[64,768]{1,0:T(8,128)(2,1)S(1)} %get-tuple-element.89), channel_id=1, source_target_pairs={{0,1},{1,0},{2,3},{3,2},{4,5},{5,4},{6,7},{7,6},{8,9},{9,8},{10,11... | collective-permute-start | bytes 294920 | tf_op jit(solution)/shard_map/ppermute | solution.py:679
  94.4 8.3 %collective-permute-start.22 = (bf16[64,768]{1,0:T(8,128)(2,1)S(1)}, bf16[64,768]{1,0:T(8,128)(2,1)S(1)}, u32[]{:S(2)}, u32[]{:S(2)}) collective-permute-start(bf16[64,768]{1,0:T(8,128)(2,1)S(1)} %get-tuple-element.90), channel_id=1, source_target_pairs={{0,2},{1,3},{2,0},{3,1},{4,6},{5,7},{6,4},{7,5},{8,10},{9,11},{10,... | collective-permute-start | bytes 294920 | tf_op jit(solution)/shard_map/ppermute | solution.py:679
  95.9 7.2 %collective-permute-start.23 = (bf16[64,768]{1,0:T(8,128)(2,1)S(1)}, bf16[64,768]{1,0:T(8,128)(2,1)S(1)}, u32[]{:S(2)}, u32[]{:S(2)}) collective-permute-start(bf16[64,768]{1,0:T(8,128)(2,1)S(1)} %get-tuple-element.91), channel_id=1, source_target_pairs={{0,3},{1,2},{2,1},{3,0},{4,7},{5,6},{6,5},{7,4},{8,11},{9,10},{10,... | collective-permute-start | bytes 294920 | tf_op jit(solution)/shard_map/ppermute | solution.py:679
Sparse Core Ops, SparseCore 0:
  60.0 16.6 all-gather.2
